TPU v7x, 128 devices: a whole 4x4x4 slice. The times are simulated.
128 devices in a mesh: ctx: 16 (over x_lo, y, core), kvh: 8 (over x_hi, z).
Axes of the slice: x: 4 (x_hi: 2, x_lo: 2; x = x_hi * 2 + x_lo), y: 4, z: 4, core: 2. Of those that a mesh axis runs over, the one named last changes fastest.
Arguments:
- x_kv: bfloat16 [4096, 3072], P('ctx'), may hold values from -17 to 17, as said below
- w_kv: bfloat16 [3072, 2048], P(None, 'kvh'), may hold values from -0.0546875 to 0.0546875
- queries: bfloat16 [3, 6144, 3072], P(None, 'ctx', 'kvh'), may hold values from -6 to 6
- d_out: bfloat16 [3, 6144, 3072], P(None, 'ctx', 'kvh'), may hold values from -12 to 12
- lse: float32 [3, 6144, 24], P(None, 'ctx', 'kvh'), may hold values from 7 to 10
- delta: float32 [3, 6144, 24], P(None, 'ctx', 'kvh'), may hold values from -24 to 24
- offsets: int32 [16], P('ctx'), may hold values from 1 to 4095
- block_mask: int32 [48, 32], P('ctx'), may hold values 0 or 1
Outputs:
- d_queries: bfloat16 [3, 6144, 3072], P(None, 'ctx', 'kvh')
- d_x: bfloat16 [4096, 3072], P('ctx', 'kvh')
- d_w: float32 [3072, 2048], P('ctx', 'kvh')
Inputs may be any that keep to these rules, and one draw needn't show every extreme that they name: `x_kv`: feature scales differ from column to column.
All inputs are finite; a program needn't handle non-finite values.
Results may differ from a plain program's by a relative error of at most 0.012.
Values may be sent and summed in bfloat16 or wider, within the bound.
No kernel may reach another device: no remote copies, remote signals or barrier semaphores. Data moves between devices by JAX's collectives and lax.ppermute only.
A program may use at most 64 MiB of HBM per device.

v0:
```python
import functools

import jax
import jax.numpy as jnp
from jax import lax
from jax.experimental import pallas as pl
from jax.experimental.pallas import tpu as pltpu
from jax.sharding import Mesh, PartitionSpec as P

D = 3072
KVH = 8
HD = 128
NL = 3
NLH = 9
KB = 16
QB = 6
LOG2E = 1.4426950408889634
C1 = LOG2E * HD ** (-0.5)
NEG = -1e30
NT = (((1,), (1,)), ((), ()))
NN = (((1,), (0,)), ((), ()))
C8 = ("xl", "y")
K8 = ("xh", "z")
ALL = ("xl", "y", "co", "xh", "z")


def attn_kernel(groups, ints_o, ints_p, co_ref, small_o, small_p, kv_ref, qo, qp, oo, op, dkv_ref, dqo_ref, dqp_ref,
                q_s, o_s, kT_s, acc_s, dq_s, p_s, ds_s, bias_s, lst, cnt, sem):
    f32=jnp.float32; bf=jnp.bfloat16
    copies=[pltpu.make_async_copy(a, d, sem.at[i]) for i,(a,d) in enumerate(
        [(qo,q_s.at[0]),(oo,o_s.at[0]),(qp,q_s.at[1]),(op,o_s.at[1])])]
    for c in copies: c.start()
    co=co_ref[0]
    acc_s[...]=jnp.zeros(acc_s.shape,f32)
    for kb in range(KB):
        kT_s[kb]=kv_ref[kb,:,:HD].T
    for s,ints in ((0,ints_o),(1,ints_p)):
        off=ints[96]
        for b in range(3):
            n=jnp.int32(0)
            for kb in range(KB):
                j,c=divmod(kb,2)
                i=(j//4)*8+(j%4)*2+co
                st=i*256+c*128
                vis=(ints[b*32+2*i+c]==1)&(st<off+(b*128+127))
                lst[s*3+b,n]=jnp.int32(kb)
                n=n+vis.astype(jnp.int32)
            cnt[s*3+b]=n
            lst[s*3+b,n]=jnp.int32(KB)
    for c in copies: c.wait()

    rowi=lax.broadcasted_iota(jnp.int32,(HD,HD),0)
    coli=lax.broadcasted_iota(jnp.int32,(HD,HD),1)
    dif=coli-rowi

    def qb_body(qb,_):
        s=qb//3; b=qb-3*s
        rows=pl.ds(pl.multiple_of(b*128,128),128)
        n=cnt[qb]
        off=jnp.where(s==0,ints_o[96],ints_p[96])+b*128
        dq_s[...]=jnp.zeros(dq_s.shape,f32)
        def qg(ref,lhs):
            return jnp.concatenate([ref[s,lh//3,rows,(lh%3)*HD:(lh%3+1)*HD] for lh in lhs],axis=0)
        def pair(t,_):
            kb0=lst[qb,2*t]
            kb1r=lst[qb,2*t+1]
            one=2*t+1>=n
            kb1=jnp.where(one,kb0,kb1r)
            def start(kb):
                j=kb//2
                return ((j//4)*8+(j%4)*2+co)*256+(kb-2*j)*128
            st0=start(kb0)
            st1=jnp.where(one,jnp.int32(1<<20),start(kb1))
            bias_s[0:HD]=jnp.where(dif>st0-off,f32(0),f32(NEG))
            bias_s[HD:]=jnp.where(dif>st1-off,f32(0),f32(NEG))
            K2=jnp.concatenate([kv_ref[kb0,:,:HD],kv_ref[kb1,:,:HD]],axis=0)
            V2=jnp.concatenate([kv_ref[kb0,:,HD:],kv_ref[kb1,:,HD:]],axis=0)
            K2T=jnp.concatenate([kT_s[kb0],kT_s[kb1]],axis=1)
            bias=bias_s[...]
            for g in groups:
                Q=qg(q_s,g); O=qg(o_s,g)
                ST=lax.dot_general(K2,Q,NT,preferred_element_type=f32)
                DP=lax.dot_general(V2,O,NT,preferred_element_type=f32)
                for u,lh in enumerate(g):
                    cs=slice(u*HD,(u+1)*HD)
                    lse=jnp.where(s==0,small_o[b,lh],small_p[b,lh])[None,:]*f32(LOG2E)
                    dl=jnp.where(s==0,small_o[b,9+lh],small_p[b,9+lh])[None,:]
                    p=jnp.exp2(ST[:,cs]*f32(C1)-lse+bias)
                    p_s[:,lh*HD:(lh+1)*HD]=p.astype(bf)
                    ds_s[:,lh*HD:(lh+1)*HD]=(p*(DP[:,cs]-dl)).astype(bf)
            allq=tuple(range(NLH))
            dv=lax.dot_general(p_s[...],qg(o_s,allq),NN,preferred_element_type=f32)
            dk=lax.dot_general(ds_s[...],qg(q_s,allq),NN,preferred_element_type=f32)
            acc_s[kb0,:,:HD]+=dk[:HD]
            acc_s[kb0,:,HD:]+=dv[:HD]
            acc_s[kb1,:,:HD]+=dk[HD:]
            acc_s[kb1,:,HD:]+=dv[HD:]
            dq_s[...]+=lax.dot_general(K2T,ds_s[...],NN,preferred_element_type=f32)
            return 0
        lax.fori_loop(0,(n+1)//2,pair,0)
        sc=f32(HD**(-0.5))
        @pl.when(s==0)
        def _(): dqo_ref[b]=dq_s[...]*sc
        @pl.when(s==1)
        def _(): dqp_ref[b]=(dq_s[...]*sc).astype(bf)
        return 0
    lax.fori_loop(0,QB,qb_body,0)
    sc=f32(HD**(-0.5))
    dkv_ref[:,:,:HD]=(acc_s[:,:,:HD]*sc).astype(bf)
    dkv_ref[:,:,HD:]=acc_s[:,:,HD:].astype(bf)


def attn(ints_o,ints_p,co,small_o,small_p,kv,qo,qp,oo,op,groups=((0,1),(2,3),(4,5),(6,7),(8,))):
    f32=jnp.float32; bf=jnp.bfloat16
    S=pl.BlockSpec(memory_space=pltpu.SMEM); V=pl.BlockSpec(memory_space=pltpu.VMEM); A=pl.BlockSpec(memory_space=pl.ANY)
    return pl.pallas_call(
        functools.partial(attn_kernel,groups),
        out_shape=(jax.ShapeDtypeStruct((KB,HD,2*HD),bf),jax.ShapeDtypeStruct((3,HD,NLH*HD),f32),jax.ShapeDtypeStruct((3,HD,NLH*HD),bf)),
        in_specs=[S,S,S,V,V,V,A,A,A,A], out_specs=(V,V,V),
        scratch_shapes=[pltpu.VMEM((2,NL,384,384),bf),pltpu.VMEM((2,NL,384,384),bf),pltpu.VMEM((KB,HD,HD),bf),
            pltpu.VMEM((KB,HD,2*HD),f32),pltpu.VMEM((HD,NLH*HD),f32),pltpu.VMEM((2*HD,NLH*HD),bf),pltpu.VMEM((2*HD,NLH*HD),bf),
            pltpu.VMEM((2*HD,HD),f32),pltpu.SMEM((QB,KB+1),jnp.int32),pltpu.SMEM((QB,),jnp.int32),pltpu.SemaphoreType.DMA((4,))],
        name="attn",
    )(ints_o,ints_p,co,small_o,small_p,kv,qo,qp,oo,op)


VM = pl.BlockSpec(memory_space=pltpu.VMEM)
SM = pl.BlockSpec(memory_space=pltpu.SMEM)


def sum_kernel(r_ref, out_ref):
    acc = r_ref[0].astype(jnp.float32)
    for k in range(1, 8):
        acc += r_ref[k].astype(jnp.float32)
    out_ref[...] = acc.astype(jnp.bfloat16)


def dw_kernel(xa_ref, xb_ref, ga_ref, gb_ref, out_ref):
    for k in range(8):
        acc = lax.dot_general(xa_ref[k], ga_ref[...], NN, preferred_element_type=jnp.float32)
        acc += lax.dot_general(xb_ref[k], gb_ref[...], NN, preferred_element_type=jnp.float32)
        out_ref[k] = acc.astype(jnp.bfloat16)


def grad_kernel(r_ref, grad_ref, sq_ref):
    acc = r_ref[0].astype(jnp.float32)
    for k in range(1, 8):
        acc += r_ref[k].astype(jnp.float32)
    grad_ref[...] = acc
    sq = jnp.sum(jnp.sum(acc * acc, axis=0, keepdims=True), axis=1, keepdims=True)
    sq_ref[...] = jnp.broadcast_to(sq, sq_ref.shape)


def scale_kernel(grad_ref, parts_ref, out_ref):
    total = jnp.sum(parts_ref[...], axis=0, keepdims=True)[:, :1]
    out_ref[...] = grad_ref[...] / jnp.sqrt(total / (D * KVH * 2 * HD) + 1e-06)


def dx_kernel(co_ref, *refs):
    g, wa, wb, out_ref = refs[:8], refs[8:16], refs[16:24], refs[24]
    ca = pl.ds(pl.multiple_of(co_ref[0] * HD, HD), HD)
    cb = pl.ds(pl.multiple_of((1 - co_ref[0]) * HD, HD), HD)
    acc = jnp.zeros((256, 384), jnp.float32)
    for k in range(8):
        acc += lax.dot_general(g[k][:, ca], wa[k][...], NT, preferred_element_type=jnp.float32)
        acc += lax.dot_general(g[k][:, cb], wb[k][...], NT, preferred_element_type=jnp.float32)
    out_ref[...] = acc.astype(jnp.bfloat16)


def dq_kernel(a_ref, b_ref, out_ref):
    for b in range(3):
        for lh in range(NLH):
            cs = slice(lh * HD, (lh + 1) * HD)
            t = a_ref[b, :, cs] + b_ref[b, :, cs].astype(jnp.float32)
            h = lh % 3
            out_ref[lh // 3, b * HD : (b + 1) * HD, h * HD : (h + 1) * HD] = t.T.astype(jnp.bfloat16)


def call(kernel, specs, *shapes):
    out = tuple(jax.ShapeDtypeStruct(s, d) for s, d in shapes)
    return pl.pallas_call(kernel, out_shape=out, in_specs=specs, out_specs=tuple(VM for _ in out))


def swap(a):
    return lax.ppermute(a, "co", [(0, 1), (1, 0)])


DELTAS = [(i, j) for i in range(2) for j in range(4) if (i, j) != (0, 0)]


def shift(a, delta):
    perm = []
    for i in range(2):
        for j in range(4):
            perm.append((4 * i + j, 4 * ((i + delta[0]) % 2) + (j + delta[1]) % 4))
    return lax.ppermute(a, K8, perm)


def exchange(a, axes):
    return lax.all_to_all(a, axes, 0, 0)


def step(x_kv, w_kv, queries, d_out, lse, delta, offsets, block_mask):
    f32 = jnp.float32
    bf = jnp.bfloat16
    co = lax.axis_index("co")
    co1 = co.reshape(1).astype(jnp.int32)
    kv_local = jnp.dot(x_kv, w_kv, preferred_element_type=f32).astype(bf)
    kv_all = exchange(jnp.broadcast_to(kv_local[None], (8, 256, 256)), C8)
    w_half = lax.dynamic_slice_in_dim(w_kv, co * HD, HD, 1).reshape(8, 384, HD)
    xh, z = lax.axis_index("xh"), lax.axis_index("z")
    wa = [lax.dynamic_index_in_dim(w_half, 4 * xh + z, 0, False)]
    for i, j in DELTAS:
        piece = lax.dynamic_index_in_dim(w_half, 4 * ((xh + i) % 2) + (z + j) % 4, 0, False)
        wa.append(shift(piece, (i, j)))
    ints = jnp.concatenate([block_mask.reshape(96), offsets, jnp.zeros((31,), jnp.int32)])
    rows = jnp.concatenate([lse, delta], axis=2).reshape(NL, 3, HD, 2, 3)
    small = jnp.transpose(rows, (1, 3, 0, 4, 2)).reshape(3, 2 * NLH, HD)
    x_t = x_kv.T.reshape(8, 2, 192, 256)
    xa = lax.dynamic_index_in_dim(x_t, co, 1, False)
    xb = swap(lax.dynamic_index_in_dim(x_t, 1 - co, 1, False))
    dkv, dqo, dqp = attn(
        ints, swap(ints), co1, small, swap(small),
        kv_all.reshape(KB, HD, 2 * HD), queries, swap(queries), d_out, swap(d_out),
    )
    dkv_r = exchange(dkv.reshape(8, 256, 256), C8)
    (g,) = call(sum_kernel, [VM], ((256, 256), bf))(dkv_r)
    (dw_part,) = call(dw_kernel, [VM] * 4, ((8, 192, 256), bf))(xa, xb, g, swap(g))
    dw_r = exchange(dw_part, C8)
    grad, sq = call(grad_kernel, [VM], ((192, 256), f32), ((128, HD), f32))(dw_r)
    parts = exchange(sq.reshape(128, 1, HD), ALL)
    gs = [g] + [shift(g, d) for d in DELTAS]
    wb = swap(jnp.stack(wa))
    (d_x,) = call(dx_kernel, [SM] + [VM] * 24, ((256, 384), bf))(
        co1, *gs, *wa, *[wb[k] for k in range(8)]
    )
    (d_queries,) = call(dq_kernel, [VM] * 2, ((NL, 384, 384), bf))(dqo, swap(dqp))
    (d_w,) = call(scale_kernel, [VM] * 2, ((192, 256), f32))(grad, parts.reshape(128, HD))
    return (d_queries, d_x, d_w)


def solution(mesh):
    mesh5 = Mesh(mesh.devices.reshape(2, 4, 2, 2, 4), ALL)
    ctx = ("xl", "y", "co")
    kvh = ("xh", "z")
    in_specs = (
        P(ctx, None),
        P(None, kvh),
        P(None, ctx, kvh),
        P(None, ctx, kvh),
        P(None, ctx, kvh),
        P(None, ctx, kvh),
        P(ctx),
        P(ctx, None),
    )
    out_specs = (P(None, ctx, kvh), P(ctx, kvh), P(ctx, kvh))
    return jax.shard_map(step, mesh=mesh5, in_specs=in_specs, out_specs=out_specs, check_vma=False)
```

profile of v0, /device:TPU:0, one launch (start us, length us, event | category | flops | bytes accessed | tf_op | source)
XLA Modules:
  0.0 146.6 jit_solution(8311766839457877052)
XLA Ops:
  2.3 2.0 %convolution_convert_fusion = bf16[256,256]{1,0:T(8,128)(2,1)S(1)} fusion(bf16[256,3072]{1,0:T(8,128)(2,1)} %param.8, bf16[3072,256]{1,0:T(8,128)(2,1)S(1)} %copy-done), kind=kOutput, calls=%fused_computation | convolution fusion | flops 402718720 | bytes 3276800 | tf_op jit(solution)/shard_map/dot_general | solution.py:208
  4.3 1.1 broadcast_in_dim.2
  5.4 5.5 %all-to-all-start = ((bf16[8,256,256]{2,1,0:T(8,128)(2,1)}), bf16[8,256,256]{2,1,0:T(8,128)(2,1)}, u32[]{:S(2)}, u32[]{:S(2)}) async-start(bf16[8,256,256]{2,1,0:T(8,128)(2,1)} %broadcast_in_dim.2), calls=%async_computation | async-start | bytes 2097152 | tf_op jit(solution)/shard_map/all_to_all | solution.py:200
  12.8 1.9 %collective-permute-start.12 = (bf16[384,128]{1,0:T(8,128)(2,1)}, bf16[384,128]{1,0:T(8,128)(2,1)S(1)}, u32[]{:S(2)}, u32[]{:S(2)}) collective-permute-start(bf16[384,128]{1,0:T(8,128)(2,1)} %get-tuple-element.30), channel_id=1, source_target_pairs={{0,1},{1,2},{2,3},{3,0},{4,5},{5,6},{6,7},{7,4},{8,9},{9,10},{10,1... | collective-permute-start | bytes 294920 | tf_op jit(solution)/shard_map/ppermute | solution.py:196
  14.7 1.7 %copy.21 = bf16[256,3072]{0,1:T(8,128)(2,1)S(1)} copy(bf16[256,3072]{1,0:T(8,128)(2,1)} %param.8) | data formatting | bytes 3145728 | tf_op args[0]
  16.4 1.3 dynamic-slice_bitcast_fusion
  17.7 2.6 %collective-permute-done.12.refs_9_ = bf16[384,128]{1,0:T(8,128)(2,1)S(1)} collective-permute-done((bf16[384,128]{1,0:T(8,128)(2,1)}, bf16[384,128]{1,0:T(8,128)(2,1)S(1)}, u32[]{:S(2)}, u32[]{:S(2)}) %collective-permute-start.12) | collective-permute-done | bytes 98336 | tf_op jit(solution)/shard_map/ppermute | solution.py:196
  20.3 1.6 %collective-permute-start.13 = (bf16[384,128]{1,0:T(8,128)(2,1)}, bf16[384,128]{1,0:T(8,128)(2,1)S(1)}, u32[]{:S(2)}, u32[]{:S(2)}) collective-permute-start(bf16[384,128]{1,0:T(8,128)(2,1)} %get-tuple-element.29), channel_id=1, source_target_pairs={{0,2},{1,3},{2,0},{3,1},{4,6},{5,7},{6,4},{7,5},{8,10},{9,11},{10,... | collective-permute-start | bytes 294920 | tf_op jit(solution)/shard_map/ppermute | solution.py:196
  23.3 2.7 %collective-permute-start.15 = (bf16[384,128]{1,0:T(8,128)(2,1)}, bf16[384,128]{1,0:T(8,128)(2,1)S(1)}, u32[]{:S(2)}, u32[]{:S(2)}) collective-permute-start(bf16[384,128]{1,0:T(8,128)(2,1)} %get-tuple-element.27), channel_id=1, source_target_pairs={{0,4},{1,5},{2,6},{3,7},{4,0},{5,1},{6,2},{7,3},{8,12},{9,13},{10,... | collective-permute-start | bytes 294920 | tf_op jit(solution)/shard_map/ppermute | solution.py:196
  26.0 1.6 %collective-permute-start.16 = (bf16[384,128]{1,0:T(8,128)(2,1)S(1)}, bf16[384,128]{1,0:T(8,128)(2,1)S(1)}, u32[]{:S(2)}, u32[]{:S(2)}) collective-permute-start(bf16[384,128]{1,0:T(8,128)(2,1)S(1)} %get-tuple-element.26), channel_id=1, source_target_pairs={{0,5},{1,6},{2,7},{3,4},{4,1},{5,2},{6,3},{7,0},{8,13},{9,14},{10,... | collective-permute-start | bytes 294920 | tf_op jit(solution)/shard_map/ppermute | solution.py:196
  27.5 4.1 %collective-permute-start.17 = (bf16[384,128]{1,0:T(8,128)(2,1)S(1)}, bf16[384,128]{1,0:T(8,128)(2,1)S(1)}, u32[]{:S(2)}, u32[]{:S(2)}) collective-permute-start(bf16[384,128]{1,0:T(8,128)(2,1)S(1)} %get-tuple-element.25), channel_id=1, source_target_pairs={{0,6},{1,7},{2,4},{3,5},{4,2},{5,3},{6,0},{7,1},{8,14},{9,15},{10,... | collective-permute-start | bytes 294920 | tf_op jit(solution)/shard_map/ppermute | solution.py:196
  31.7 33.7 %attn.1 = (bf16[16,128,256]{2,1,0:T(8,128)(2,1)}, f32[3,128,1152]{2,1,0:T(8,128)}, bf16[3,128,1152]{2,1,0:T(8,128)(2,1)}) custom-call(s32[128]{0:T(128)} %copy-done.22, s32[128]{0:T(128)} %copy-done.23, s32[1]{0:T(128)} %bitcast.co_ref, f32[3,18,128]{2,1,0:T(8,128)} %copy-done.12, f32[3,18,128]{2,1,0:T(8,128)} %copy-done.19, ...), custom_call_target="tpu_custom_call" | custom-call | tf_op jit(solution)/shard_map/attn/pallas_call | solution.py:116
  65.4 10.2 %all-to-all-start.1 = ((bf16[8,256,256]{2,1,0:T(8,128)(2,1)}), bf16[8,256,256]{2,1,0:T(8,128)(2,1)S(1)}, u32[]{:S(2)}, u32[]{:S(2)}) async-start(bf16[8,256,256]{2,1,0:T(8,128)(2,1)} %bitcast.69), calls=%async_computation.1 | async-start | bytes 2097152 | tf_op jit(solution)/shard_map/all_to_all | solution.py:200
  75.6 2.0 %collective-permute-start.18 = (bf16[384,128]{1,0:T(8,128)(2,1)}, bf16[384,128]{1,0:T(8,128)(2,1)}, u32[]{:S(2)}, u32[]{:S(2)}) collective-permute-start(bf16[384,128]{1,0:T(8,128)(2,1)} %get-tuple-element.24), channel_id=1, source_target_pairs={{0,7},{1,4},{2,5},{3,6},{4,3},{5,0},{6,1},{7,2},{8,15},{9,12},{10,... | collective-permute-start | bytes 294920 | tf_op jit(solution)/shard_map/ppermute | solution.py:196
  81.6 7.0 %all-to-all-done.1.r_ref = bf16[8,256,256]{2,1,0:T(8,128)(2,1)S(1)} async-done(((bf16[8,256,256]{2,1,0:T(8,128)(2,1)}), bf16[8,256,256]{2,1,0:T(8,128)(2,1)S(1)}, u32[]{:S(2)}, u32[]{:S(2)}) %all-to-all-start.1) | async-done | bytes 1048608 | tf_op jit(solution)/shard_map/all_to_all | solution.py:200
  89.6 2.0 %shard_map.104.refs_0_.ga_ref = bf16[256,256]{1,0:T(8,128)(2,1)} custom-call(bf16[8,256,256]{2,1,0:T(8,128)(2,1)} %copy-done.1), custom_call_target="tpu_custom_call" | custom-call | tf_op jit(solution)/shard_map/pallas_call | solution.py:227
  91.6 1.5 %bitcast_dynamic-update-slice_fusion = bf16[8,384,128]{2,1,0:T(8,128)(2,1)} fusion(bf16[8,384,128]{2,1,0:T(8,128)(2,1)} %bitcast_dynamic-update-slice_fusion.1, bf16[384,128]{1,0:T(8,128)(2,1)} %collective-permute-done.18.refs_15_), kind=kLoop, calls=%fused_computation.11 | loop fusion | bytes 196608 | tf_op jit(solution)/shard_map/stack | solution.py:233
  94.3 2.9 %shard_map.106 = bf16[8,192,256]{2,1,0:T(8,128)(2,1)} custom-call(bf16[8,192,256]{2,1,0:T(8,128)(2,1)} %get-tuple-element.14.xa_ref, bf16[8,192,256]{2,1,0:T(8,128)(2,1)} %collective-permute-done.20.xb_ref, bf16[256,256]{1,0:T(8,128)(2,1)} %shard_map.104.refs_0_.ga_ref, bf16[256,256]{1,0:T(8,128)(2,1)} %copy-done.18), custom_call_target="tpu_custom_call" | custom-call | tf_op jit(solution)/shard_map/pallas_call | solution.py:228
  97.3 3.6 %all-to-all-start.2 = ((bf16[8,192,256]{2,1,0:T(8,128)(2,1)}), bf16[8,192,256]{2,1,0:T(8,128)(2,1)S(1)}, u32[]{:S(2)}, u32[]{:S(2)}) async-start(bf16[8,192,256]{2,1,0:T(8,128)(2,1)} %shard_map.106), calls=%async_computation.2 | async-start | bytes 1572864 | tf_op jit(solution)/shard_map/all_to_all | solution.py:200
  101.7 2.4 %collective-permute-start.6 = (bf16[256,256]{1,0:T(8,128)(2,1)S(1)}, bf16[256,256]{1,0:T(8,128)(2,1)}, u32[]{:S(2)}, u32[]{:S(2)}) collective-permute-start(bf16[256,256]{1,0:T(8,128)(2,1)S(1)} %copy-done.3), channel_id=1, source_target_pairs={{0,2},{1,3},{2,0},{3,1},{4,6},{5,7},{6,4},{7,5},{8,10},{9,11},{10,... | collective-permute-start | bytes 393224 | tf_op jit(solution)/shard_map/ppermute | solution.py:196
  104.1 1.0 collective-permute-start.7
  105.1 8.1 %all-to-all-done.2.r_ref = bf16[8,192,256]{2,1,0:T(8,128)(2,1)S(1)} async-done(((bf16[8,192,256]{2,1,0:T(8,128)(2,1)}), bf16[8,192,256]{2,1,0:T(8,128)(2,1)S(1)}, u32[]{:S(2)}, u32[]{:S(2)}) %all-to-all-start.2) | async-done | bytes 786464 | tf_op jit(solution)/shard_map/all_to_all | solution.py:200
  114.1 2.0 %shard_map.107 = (f32[192,256]{1,0:T(8,128)}, f32[128,128]{1,0:T(8,128)}) custom-call(bf16[8,192,256]{2,1,0:T(8,128)(2,1)} %copy-done.2), custom_call_target="tpu_custom_call" | custom-call | tf_op jit(solution)/shard_map/pallas_call | solution.py:230
  116.1 6.9 %all-to-all-start.3 = ((f32[128,1,128]{2,1,0:T(1,128)}), f32[128,1,128]{2,1,0:T(1,128)S(1)}, u32[]{:S(2)}, u32[]{:S(2)}) async-start(f32[128,1,128]{2,1,0:T(1,128)} %bitcast.73), calls=%async_computation.3 | async-start | bytes 131072 | tf_op jit(solution)/shard_map/all_to_all | solution.py:200
  123.0 2.5 %collective-permute-start.8 = (bf16[256,256]{1,0:T(8,128)(2,1)S(1)}, bf16[256,256]{1,0:T(8,128)(2,1)S(1)}, u32[]{:S(2)}, u32[]{:S(2)}) collective-permute-start(bf16[256,256]{1,0:T(8,128)(2,1)S(1)} %copy-done.3), channel_id=1, source_target_pairs={{0,4},{1,5},{2,6},{3,7},{4,0},{5,1},{6,2},{7,3},{8,12},{9,13},{10,... | collective-permute-start | bytes 393224 | tf_op jit(solution)/shard_map/ppermute | solution.py:196
  125.5 1.6 %collective-permute-start.9 = (bf16[256,256]{1,0:T(8,128)(2,1)S(1)}, bf16[256,256]{1,0:T(8,128)(2,1)S(1)}, u32[]{:S(2)}, u32[]{:S(2)}) collective-permute-start(bf16[256,256]{1,0:T(8,128)(2,1)S(1)} %copy-done.3), channel_id=1, source_target_pairs={{0,5},{1,6},{2,7},{3,4},{4,1},{5,2},{6,3},{7,0},{8,13},{9,14},{10,... | collective-permute-start | bytes 393224 | tf_op jit(solution)/shard_map/ppermute | solution.py:196
  127.1 5.7 %collective-permute-start.10 = (bf16[256,256]{1,0:T(8,128)(2,1)S(1)}, bf16[256,256]{1,0:T(8,128)(2,1)S(1)}, u32[]{:S(2)}, u32[]{:S(2)}) collective-permute-start(bf16[256,256]{1,0:T(8,128)(2,1)S(1)} %copy-done.3), channel_id=1, source_target_pairs={{0,6},{1,7},{2,4},{3,5},{4,2},{5,3},{6,0},{7,1},{8,14},{9,15},{10,... | collective-permute-start | bytes 393224 | tf_op jit(solution)/shard_map/ppermute | solution.py:196
  132.8 1.2 collective-permute-start.11
  133.9 2.1 %slice_bitcast_fusion = (bf16[384,128]{1,0:T(8,128)(2,1)}, bf16[384,128]{1,0:T(8,128)(2,1)}, bf16[384,128]{1,0:T(8,128)(2,1)}, bf16[384,128]{1,0:T(8,128)(2,1)},...) fusion(bf16[8,384,128]{2,1,0:T(8,128)(2,1)} %collective-permute-done.19), kind=kLoop, calls=%fused_computation.3 | loop fusion | bytes 1572864 | tf_op jit(solution)/shard_map/squeeze | solution.py:235
  136.1 2.9 %shard_map.103 = bf16[3,384,384]{2,1,0:T(8,128)(2,1)} custom-call(f32[3,128,1152]{2,1,0:T(8,128)} %get-tuple-element.8.a_ref, bf16[3,128,1152]{2,1,0:T(8,128)(2,1)} %copy-done.4), custom_call_target="tpu_custom_call" | custom-call | tf_op jit(solution)/shard_map/pallas_call | solution.py:237
  140.8 3.4 %shard_map.105 = bf16[256,384]{1,0:T(8,128)(2,1)} custom-call(s32[1]{0:T(128)} %bitcast.co_ref, bf16[256,256]{1,0:T(8,128)(2,1)} %shard_map.104.refs_0_.ga_ref, bf16[256,256]{1,0:T(8,128)(2,1)} %copy-done.13, bf16[256,256]{1,0:T(8,128)(2,1)} %collective-permute-done.6.refs_2_, bf16[256,256]{1,0:T(8,128)(2,1)} %collective-permute-done.7.refs_3_, ...), custom_call_target="tpu_custom_call" | custom-call | tf_op jit(solution)/shard_map/pallas_call | solution.py:234
  144.9 1.7 %shard_map.108 = f32[192,256]{1,0:T(8,128)} custom-call(f32[192,256]{1,0:T(8,128)} %get-tuple-element.11.grad_ref, f32[128,128]{1,0:T(8,128)} %bitcast.70), custom_call_target="tpu_custom_call" | custom-call | tf_op jit(solution)/shard_map/pallas_call | solution.py:238
  (96 shorter events, 14.4 us)
Async XLA Ops:
  2.3 20.3 %collective-permute-start = (s32[128]{0:T(128)S(1)}, s32[128]{0:T(128)S(1)}, u32[]{:S(2)}, u32[]{:S(2)}) collective-permute-start(s32[128]{0:T(128)S(1)} %pad_add_fusion.ints_o), channel_id=1, source_target_pairs={{0,8},{8,0},{1,9},{9,1},{2,10},{10,2},{3,11},{11,3},{4,12},{12,4},... | collective-permute-start | bytes 1544 | tf_op jit(solution)/shard_map/ppermute | solution.py:185
  4.3 7.1 %copy-start.20 = (f32[3,384,3]{1,2,0:T(4,128)S(1)}, f32[3,384,3]{1,2,0:T(4,128)}, u32[]{:S(2)}) copy-start(f32[3,384,3]{1,2,0:T(4,128)} %param.13) | copy-start | bytes 41476
  5.4 26.2 %all-to-all-start = ((bf16[8,256,256]{2,1,0:T(8,128)(2,1)}), bf16[8,256,256]{2,1,0:T(8,128)(2,1)}, u32[]{:S(2)}, u32[]{:S(2)}) async-start(bf16[8,256,256]{2,1,0:T(8,128)(2,1)} %broadcast_in_dim.2), calls=%async_computation | async-start | bytes 2097152 | tf_op jit(solution)/shard_map/all_to_all | solution.py:200
  10.9 15.1 %collective-permute-start.2 = (bf16[3,384,384]{2,1,0:T(8,128)(2,1)}, bf16[3,384,384]{2,1,0:T(8,128)(2,1)}, u32[]{:S(2)}, u32[]{:S(2)}) collective-permute-start(bf16[3,384,384]{2,1,0:T(8,128)(2,1)} %qo.1), channel_id=1, source_target_pairs={{0,8},{8,0},{1,9},{9,1},{2,10},{10,2},{3,11},{11,3},{4,12},{12,4},... | collective-permute-start | bytes 2654216 | tf_op jit(solution)/shard_map/ppermute | solution.py:185
  11.1 16.4 %collective-permute-start.3 = (bf16[3,384,384]{2,1,0:T(8,128)(2,1)}, bf16[3,384,384]{2,1,0:T(8,128)(2,1)}, u32[]{:S(2)}, u32[]{:S(2)}) collective-permute-start(bf16[3,384,384]{2,1,0:T(8,128)(2,1)} %oo.1), channel_id=1, source_target_pairs={{0,8},{8,0},{1,9},{9,1},{2,10},{10,2},{3,11},{11,3},{4,12},{12,4},... | collective-permute-start | bytes 2654216 | tf_op jit(solution)/shard_map/ppermute | solution.py:185
  11.5 11.7 %collective-permute-start.1 = (f32[3,18,128]{2,1,0:T(8,128)S(1)}, f32[3,18,128]{2,1,0:T(8,128)S(1)}, u32[]{:S(2)}, u32[]{:S(2)}) collective-permute-start(f32[3,18,128]{2,1,0:T(8,128)S(1)} %copy.20.small_o), channel_id=1, source_target_pairs={{0,8},{8,0},{1,9},{9,1},{2,10},{10,2},{3,11},{11,3},{4,12},{12,4},... | collective-permute-start | bytes 82952 | tf_op jit(solution)/shard_map/ppermute | solution.py:185
  12.8 7.5 %collective-permute-start.12 = (bf16[384,128]{1,0:T(8,128)(2,1)}, bf16[384,128]{1,0:T(8,128)(2,1)S(1)}, u32[]{:S(2)}, u32[]{:S(2)}) collective-permute-start(bf16[384,128]{1,0:T(8,128)(2,1)} %get-tuple-element.30), channel_id=1, source_target_pairs={{0,1},{1,2},{2,3},{3,0},{4,5},{5,6},{6,7},{7,4},{8,9},{9,10},{10,1... | collective-permute-start | bytes 294920 | tf_op jit(solution)/shard_map/ppermute | solution.py:196
  20.3 45.1 %copy-start.5 = (bf16[384,128]{1,0:T(8,128)(2,1)}, bf16[384,128]{1,0:T(8,128)(2,1)S(1)}, u32[]{:S(2)}) copy-start(bf16[384,128]{1,0:T(8,128)(2,1)S(1)} %collective-permute-done.12.refs_9_) | copy-start | bytes 294916
  20.3 55.3 %collective-permute-start.13 = (bf16[384,128]{1,0:T(8,128)(2,1)}, bf16[384,128]{1,0:T(8,128)(2,1)S(1)}, u32[]{:S(2)}, u32[]{:S(2)}) collective-permute-start(bf16[384,128]{1,0:T(8,128)(2,1)} %get-tuple-element.29), channel_id=1, source_target_pairs={{0,2},{1,3},{2,0},{3,1},{4,6},{5,7},{6,4},{7,5},{8,10},{9,11},{10,... | collective-permute-start | bytes 294920 | tf_op jit(solution)/shard_map/ppermute | solution.py:196
  22.5 9.1 %copy-start.23 = (s32[128]{0:T(128)}, s32[128]{0:T(128)S(1)}, u32[]{:S(2)}) copy-start(s32[128]{0:T(128)S(1)} %collective-permute-done.ints_p) | copy-start | bytes 1540
  22.5 55.7 %collective-permute-start.14 = (bf16[384,128]{1,0:T(8,128)(2,1)}, bf16[384,128]{1,0:T(8,128)(2,1)S(1)}, u32[]{:S(2)}, u32[]{:S(2)}) collective-permute-start(bf16[384,128]{1,0:T(8,128)(2,1)} %get-tuple-element.28), channel_id=1, source_target_pairs={{0,3},{1,0},{2,1},{3,2},{4,7},{5,4},{6,5},{7,6},{8,11},{9,8},{10,9... | collective-permute-start | bytes 294920 | tf_op jit(solution)/shard_map/ppermute | solution.py:196
  23.3 8.4 %copy-start.19 = (f32[3,18,128]{2,1,0:T(8,128)}, f32[3,18,128]{2,1,0:T(8,128)S(1)}, u32[]{:S(2)}) copy-start(f32[3,18,128]{2,1,0:T(8,128)S(1)} %collective-permute-done.1.small_p) | copy-start | bytes 82948
  23.3 55.7 %collective-permute-start.15 = (bf16[384,128]{1,0:T(8,128)(2,1)}, bf16[384,128]{1,0:T(8,128)(2,1)S(1)}, u32[]{:S(2)}, u32[]{:S(2)}) collective-permute-start(bf16[384,128]{1,0:T(8,128)(2,1)} %get-tuple-element.27), channel_id=1, source_target_pairs={{0,4},{1,5},{2,6},{3,7},{4,0},{5,1},{6,2},{7,3},{8,12},{9,13},{10,... | collective-permute-start | bytes 294920 | tf_op jit(solution)/shard_map/ppermute | solution.py:196
  26.0 53.7 %collective-permute-start.16 = (bf16[384,128]{1,0:T(8,128)(2,1)S(1)}, bf16[384,128]{1,0:T(8,128)(2,1)S(1)}, u32[]{:S(2)}, u32[]{:S(2)}) collective-permute-start(bf16[384,128]{1,0:T(8,128)(2,1)S(1)} %get-tuple-element.26), channel_id=1, source_target_pairs={{0,5},{1,6},{2,7},{3,4},{4,1},{5,2},{6,3},{7,0},{8,13},{9,14},{10,... | collective-permute-start | bytes 294920 | tf_op jit(solution)/shard_map/ppermute | solution.py:196
  27.5 52.8 %collective-permute-start.17 = (bf16[384,128]{1,0:T(8,128)(2,1)S(1)}, bf16[384,128]{1,0:T(8,128)(2,1)S(1)}, u32[]{:S(2)}, u32[]{:S(2)}) collective-permute-start(bf16[384,128]{1,0:T(8,128)(2,1)S(1)} %get-tuple-element.25), channel_id=1, source_target_pairs={{0,6},{1,7},{2,4},{3,5},{4,2},{5,3},{6,0},{7,1},{8,14},{9,15},{10,... | collective-permute-start | bytes 294920 | tf_op jit(solution)/shard_map/ppermute | solution.py:196
  65.4 23.2 %all-to-all-start.1 = ((bf16[8,256,256]{2,1,0:T(8,128)(2,1)}), bf16[8,256,256]{2,1,0:T(8,128)(2,1)S(1)}, u32[]{:S(2)}, u32[]{:S(2)}) async-start(bf16[8,256,256]{2,1,0:T(8,128)(2,1)} %bitcast.69), calls=%async_computation.1 | async-start | bytes 2097152 | tf_op jit(solution)/shard_map/all_to_all | solution.py:200
  75.6 16.1 %collective-permute-start.18 = (bf16[384,128]{1,0:T(8,128)(2,1)}, bf16[384,128]{1,0:T(8,128)(2,1)}, u32[]{:S(2)}, u32[]{:S(2)}) collective-permute-start(bf16[384,128]{1,0:T(8,128)(2,1)} %get-tuple-element.24), channel_id=1, source_target_pairs={{0,7},{1,4},{2,5},{3,6},{4,3},{5,0},{6,1},{7,2},{8,15},{9,12},{10,... | collective-permute-start | bytes 294920 | tf_op jit(solution)/shard_map/ppermute | solution.py:196
  78.3 15.4 %collective-permute-start.20 = (bf16[8,192,256]{2,1,0:T(8,128)(2,1)}, bf16[8,192,256]{2,1,0:T(8,128)(2,1)}, u32[]{:S(2)}, u32[]{:S(2)}) collective-permute-start(bf16[8,192,256]{2,1,0:T(8,128)(2,1)} %get-tuple-element.13), channel_id=1, source_target_pairs={{0,8},{8,0},{1,9},{9,1},{2,10},{10,2},{3,11},{11,3},{4,12},{12,4},... | collective-permute-start | bytes 2359304 | tf_op jit(solution)/shard_map/ppermute | solution.py:185
  81.1 44.5 %collective-permute-start.4 = (bf16[3,128,1152]{2,1,0:T(8,128)(2,1)}, bf16[3,128,1152]{2,1,0:T(8,128)(2,1)S(1)}, u32[]{:S(2)}, u32[]{:S(2)}) collective-permute-start(bf16[3,128,1152]{2,1,0:T(8,128)(2,1)} %get-tuple-element.9), channel_id=1, source_target_pairs={{0,8},{8,0},{1,9},{9,1},{2,10},{10,2},{3,11},{11,3},{4,12},{12,4},... | collective-permute-start | bytes 2654216 | tf_op jit(solution)/shard_map/ppermute | solution.py:185
  91.6 2.1 %collective-permute-start.21 = (bf16[256,256]{1,0:T(8,128)(2,1)}, bf16[256,256]{1,0:T(8,128)(2,1)S(1)}, u32[]{:S(2)}, u32[]{:S(2)}) collective-permute-start(bf16[256,256]{1,0:T(8,128)(2,1)} %shard_map.104.refs_0_.ga_ref), channel_id=1, source_target_pairs={{0,8},{8,0},{1,9},{9,1},{2,10},{10,2},{3,11},{11,3},{4,12},{12,4},... | collective-permute-start | bytes 393224 | tf_op jit(solution)/shard_map/ppermute | solution.py:185
  93.2 29.8 %collective-permute-start.19 = (bf16[8,384,128]{2,1,0:T(8,128)(2,1)}, bf16[8,384,128]{2,1,0:T(8,128)(2,1)}, u32[]{:S(2)}, u32[]{:S(2)}) collective-permute-start(bf16[8,384,128]{2,1,0:T(8,128)(2,1)} %bitcast_dynamic-update-slice_fusion), channel_id=1, source_target_pairs={{0,8},{8,0},{1,9},{9,1},{2,10},{10,2},{3,11},{11,3},{4,12},{12,4},... | collective-permute-start | bytes 2359304 | tf_op jit(solution)/shard_map/ppermute | solution.py:185
  97.3 15.9 %all-to-all-start.2 = ((bf16[8,192,256]{2,1,0:T(8,128)(2,1)}), bf16[8,192,256]{2,1,0:T(8,128)(2,1)S(1)}, u32[]{:S(2)}, u32[]{:S(2)}) async-start(bf16[8,192,256]{2,1,0:T(8,128)(2,1)} %shard_map.106), calls=%async_computation.2 | async-start | bytes 1572864 | tf_op jit(solution)/shard_map/all_to_all | solution.py:200
  100.9 26.3 %collective-permute-start.5 = (bf16[256,256]{1,0:T(8,128)(2,1)S(1)}, bf16[256,256]{1,0:T(8,128)(2,1)S(1)}, u32[]{:S(2)}, u32[]{:S(2)}) collective-permute-start(bf16[256,256]{1,0:T(8,128)(2,1)S(1)} %copy-done.3), channel_id=1, source_target_pairs={{0,1},{1,2},{2,3},{3,0},{4,5},{5,6},{6,7},{7,4},{8,9},{9,10},{10,1... | collective-permute-start | bytes 393224 | tf_op jit(solution)/shard_map/ppermute | solution.py:196
  101.7 31.1 %collective-permute-start.6 = (bf16[256,256]{1,0:T(8,128)(2,1)S(1)}, bf16[256,256]{1,0:T(8,128)(2,1)}, u32[]{:S(2)}, u32[]{:S(2)}) collective-permute-start(bf16[256,256]{1,0:T(8,128)(2,1)S(1)} %copy-done.3), channel_id=1, source_target_pairs={{0,2},{1,3},{2,0},{3,1},{4,6},{5,7},{6,4},{7,5},{8,10},{9,11},{10,... | collective-permute-start | bytes 393224 | tf_op jit(solution)/shard_map/ppermute | solution.py:196
  104.1 34.9 %collective-permute-start.7 = (bf16[256,256]{1,0:T(8,128)(2,1)S(1)}, bf16[256,256]{1,0:T(8,128)(2,1)}, u32[]{:S(2)}, u32[]{:S(2)}) collective-permute-start(bf16[256,256]{1,0:T(8,128)(2,1)S(1)} %copy-done.3), channel_id=1, source_target_pairs={{0,3},{1,0},{2,1},{3,2},{4,7},{5,4},{6,5},{7,6},{8,11},{9,8},{10,9... | collective-permute-start | bytes 393224 | tf_op jit(solution)/shard_map/ppermute | solution.py:196
  116.1 28.2 %all-to-all-start.3 = ((f32[128,1,128]{2,1,0:T(1,128)}), f32[128,1,128]{2,1,0:T(1,128)S(1)}, u32[]{:S(2)}, u32[]{:S(2)}) async-start(f32[128,1,128]{2,1,0:T(1,128)} %bitcast.73), calls=%async_computation.3 | async-start | bytes 131072 | tf_op jit(solution)/shard_map/all_to_all | solution.py:200
  123.0 16.0 %collective-permute-start.8 = (bf16[256,256]{1,0:T(8,128)(2,1)S(1)}, bf16[256,256]{1,0:T(8,128)(2,1)S(1)}, u32[]{:S(2)}, u32[]{:S(2)}) collective-permute-start(bf16[256,256]{1,0:T(8,128)(2,1)S(1)} %copy-done.3), channel_id=1, source_target_pairs={{0,4},{1,5},{2,6},{3,7},{4,0},{5,1},{6,2},{7,3},{8,12},{9,13},{10,... | collective-permute-start | bytes 393224 | tf_op jit(solution)/shard_map/ppermute | solution.py:196
  125.5 10.5 %copy-start.4 = (bf16[3,128,1152]{2,1,0:T(8,128)(2,1)}, bf16[3,128,1152]{2,1,0:T(8,128)(2,1)S(1)}, u32[]{:S(2)}) copy-start(bf16[3,128,1152]{2,1,0:T(8,128)(2,1)S(1)} %collective-permute-done.4.b_ref) | copy-start | bytes 2654212
  125.5 13.5 %collective-permute-start.9 = (bf16[256,256]{1,0:T(8,128)(2,1)S(1)}, bf16[256,256]{1,0:T(8,128)(2,1)S(1)}, u32[]{:S(2)}, u32[]{:S(2)}) collective-permute-start(bf16[256,256]{1,0:T(8,128)(2,1)S(1)} %copy-done.3), channel_id=1, source_target_pairs={{0,5},{1,6},{2,7},{3,4},{4,1},{5,2},{6,3},{7,0},{8,13},{9,14},{10,... | collective-permute-start | bytes 393224 | tf_op jit(solution)/shard_map/ppermute | solution.py:196
  127.1 11.9 %copy-start.13 = (bf16[256,256]{1,0:T(8,128)(2,1)}, bf16[256,256]{1,0:T(8,128)(2,1)S(1)}, u32[]{:S(2)}) copy-start(bf16[256,256]{1,0:T(8,128)(2,1)S(1)} %collective-permute-done.5.refs_1_) | copy-start | bytes 393220
  127.1 12.8 %collective-permute-start.10 = (bf16[256,256]{1,0:T(8,128)(2,1)S(1)}, bf16[256,256]{1,0:T(8,128)(2,1)S(1)}, u32[]{:S(2)}, u32[]{:S(2)}) collective-permute-start(bf16[256,256]{1,0:T(8,128)(2,1)S(1)} %copy-done.3), channel_id=1, source_target_pairs={{0,6},{1,7},{2,4},{3,5},{4,2},{5,3},{6,0},{7,1},{8,14},{9,15},{10,... | collective-permute-start | bytes 393224 | tf_op jit(solution)/shard_map/ppermute | solution.py:196
  132.8 7.4 %collective-permute-start.11 = (bf16[256,256]{1,0:T(8,128)(2,1)S(1)}, bf16[256,256]{1,0:T(8,128)(2,1)S(1)}, u32[]{:S(2)}, u32[]{:S(2)}) collective-permute-start(bf16[256,256]{1,0:T(8,128)(2,1)S(1)} %copy-done.3), channel_id=1, source_target_pairs={{0,7},{1,4},{2,5},{3,6},{4,3},{5,0},{6,1},{7,2},{8,15},{9,12},{10,... | collective-permute-start | bytes 393224 | tf_op jit(solution)/shard_map/ppermute | solution.py:196
  (18 other events, 37.9 us)
where the time goes:
time: 147 us
  starting transfers between devices  57.8 us (39%)
  Pallas kernels  48.7 us (33%)
  waiting for transfers between devices  18.8 us (13%)
  local copies, waits for them, and re-layouts  17.5 us (12%)
  matrix products  1.98 us (1%)
  between operations  1.65 us (1%)
    pallas_call x1, Pallas kernels, attn(): pl.pallas_call(functools.partial(attn_kernel, groups), out_shape=(jax.Sha...  33.7 us
    ppermute x14, starting transfers between devices, shift(): return lax.ppermute(a, K8, perm)  29.8 us
    all_to_all x4, starting transfers between devices, exchange(): return lax.all_to_all(a, axes, 0, 0)  26.1 us
    all_to_all x4, waiting for transfers between devices, exchange(): return lax.all_to_all(a, axes, 0, 0)  15.1 us
    unnamed x56, local copies, waits for them, and re-layouts  10.6 us
    ppermute x14, waiting for transfers between devices, shift(): return lax.ppermute(a, K8, perm)  3.73 us
    pallas_call x1, Pallas kernels, step(): call(dx_kernel, [SM] + [VM] * 24, ((256, 384), bf))  3.43 us
  transfers between devices with their start and end apart: 26, of which 5 were waited for; matrix products, arithmetic and copies ran while one was open for 10% of the time, Pallas kernels for 32%

commit v1 on v0

--- a/solution.py
+++ b/solution.py
@@ -128,6 +128,41 @@
 SM = pl.BlockSpec(memory_space=pltpu.SMEM)
 
 
+def kv_kernel(x_ref, w_ref, out_ref, acc_ref):
+    step = pl.program_id(0)
+    part = jnp.dot(x_ref[...], w_ref[...], preferred_element_type=jnp.float32)
+
+    @pl.when(step == 0)
+    def _():
+        acc_ref[...] = part
+
+    @pl.when(step > 0)
+    def _():
+        acc_ref[...] += part
+
+    @pl.when(step == pl.num_programs(0) - 1)
+    def _():
+        kv = acc_ref[...].astype(jnp.bfloat16)
+        for k in range(8):
+            out_ref[k] = kv
+
+
+def project(x, w, steps=4):
+    depth = D // steps
+    return pl.pallas_call(
+        kv_kernel,
+        grid=(steps,),
+        out_shape=jax.ShapeDtypeStruct((8, 256, 256), jnp.bfloat16),
+        in_specs=[
+            pl.BlockSpec((256, depth), lambda i: (0, i)),
+            pl.BlockSpec((depth, 256), lambda i: (i, 0)),
+        ],
+        out_specs=pl.BlockSpec((8, 256, 256), lambda i: (0, 0, 0)),
+        scratch_shapes=[pltpu.VMEM((256, 256), jnp.float32)],
+        name="kv",
+    )(x, w)
+
+
 def sum_kernel(r_ref, out_ref):
     acc = r_ref[0].astype(jnp.float32)
     for k in range(1, 8):
@@ -157,14 +192,22 @@
 
 
 def dx_kernel(co_ref, *refs):
-    g, wa, wb, out_ref = refs[:8], refs[8:16], refs[16:24], refs[24]
-    ca = pl.ds(pl.multiple_of(co_ref[0] * HD, HD), HD)
-    cb = pl.ds(pl.multiple_of((1 - co_ref[0]) * HD, HD), HD)
-    acc = jnp.zeros((256, 384), jnp.float32)
-    for k in range(8):
-        acc += lax.dot_general(g[k][:, ca], wa[k][...], NT, preferred_element_type=jnp.float32)
-        acc += lax.dot_general(g[k][:, cb], wb[k][...], NT, preferred_element_type=jnp.float32)
-    out_ref[...] = acc.astype(jnp.bfloat16)
+    g, wa, wb, out_ref = refs[:8], refs[8:12], refs[12:16], refs[16]
+
+    def total(near, far):
+        acc = jnp.zeros((256, 384), jnp.float32)
+        for k in range(4):
+            acc += lax.dot_general(g[k][...], near[k][...], NT, preferred_element_type=jnp.float32)
+            acc += lax.dot_general(g[4 + k][...], far[k][...], NT, preferred_element_type=jnp.float32)
+        out_ref[...] = acc.astype(jnp.bfloat16)
+
+    @pl.when(co_ref[0] == 0)
+    def _():
+        total(wa, wb)
+
+    @pl.when(co_ref[0] == 1)
+    def _():
+        total(wb, wa)
 
 
 def dq_kernel(a_ref, b_ref, out_ref):
@@ -176,8 +219,13 @@
             out_ref[lh // 3, b * HD : (b + 1) * HD, h * HD : (h + 1) * HD] = t.T.astype(jnp.bfloat16)
 
 
-def call(kernel, specs, *shapes):
-    out = tuple(jax.ShapeDtypeStruct(s, d) for s, d in shapes)
+def vm(a):
+    return pltpu.with_memory_space_constraint(a, pltpu.VMEM)
+
+
+def call(kernel, specs, *shapes, near=True):
+    kind = pltpu.VMEM if near else jax.ShapeDtypeStruct
+    out = tuple(kind(s, d) for s, d in shapes)
     return pl.pallas_call(kernel, out_shape=out, in_specs=specs, out_specs=tuple(VM for _ in out))
 
 
@@ -196,6 +244,16 @@
     return lax.ppermute(a, K8, perm)
 
 
+def split_shift(a, j):
+    perm = []
+    for i in range(2):
+        for k in range(4):
+            if j > 0:
+                perm.append((4 * i + k, 4 * i + (k + j) % 4))
+            perm.append((8 + 4 * i + k, 8 + 4 * (1 - i) + (k + j) % 4))
+    return lax.ppermute(a, ("co", "xh", "z"), perm)
+
+
 def exchange(a, axes):
     return lax.all_to_all(a, axes, 0, 0)
 
@@ -205,14 +263,14 @@
     bf = jnp.bfloat16
     co = lax.axis_index("co")
     co1 = co.reshape(1).astype(jnp.int32)
-    kv_local = jnp.dot(x_kv, w_kv, preferred_element_type=f32).astype(bf)
-    kv_all = exchange(jnp.broadcast_to(kv_local[None], (8, 256, 256)), C8)
-    w_half = lax.dynamic_slice_in_dim(w_kv, co * HD, HD, 1).reshape(8, 384, HD)
+    kv_all = exchange(project(x_kv, w_kv), C8)
     xh, z = lax.axis_index("xh"), lax.axis_index("z")
-    wa = [lax.dynamic_index_in_dim(w_half, 4 * xh + z, 0, False)]
-    for i, j in DELTAS:
-        piece = lax.dynamic_index_in_dim(w_half, 4 * ((xh + i) % 2) + (z + j) % 4, 0, False)
-        wa.append(shift(piece, (i, j)))
+    w_rows = w_kv.reshape(8, 384, 256)
+    wa = []
+    for j in range(4):
+        piece = lax.dynamic_index_in_dim(w_rows, 4 * ((xh + co) % 2) + (z + j) % 4, 0, False)
+        got = split_shift(piece, j)
+        wa.append(jnp.where(co == 0, piece, got) if j == 0 else got)
     ints = jnp.concatenate([block_mask.reshape(96), offsets, jnp.zeros((31,), jnp.int32)])
     rows = jnp.concatenate([lse, delta], axis=2).reshape(NL, 3, HD, 2, 3)
     small = jnp.transpose(rows, (1, 3, 0, 4, 2)).reshape(3, 2 * NLH, HD)
@@ -220,22 +278,26 @@
     xa = lax.dynamic_index_in_dim(x_t, co, 1, False)
     xb = swap(lax.dynamic_index_in_dim(x_t, 1 - co, 1, False))
     dkv, dqo, dqp = attn(
-        ints, swap(ints), co1, small, swap(small),
-        kv_all.reshape(KB, HD, 2 * HD), queries, swap(queries), d_out, swap(d_out),
+        ints, swap(ints), co1, vm(small), vm(swap(small)),
+        vm(kv_all.reshape(KB, HD, 2 * HD)), queries, swap(queries), d_out, swap(d_out),
     )
     dkv_r = exchange(dkv.reshape(8, 256, 256), C8)
-    (g,) = call(sum_kernel, [VM], ((256, 256), bf))(dkv_r)
-    (dw_part,) = call(dw_kernel, [VM] * 4, ((8, 192, 256), bf))(xa, xb, g, swap(g))
+    (g,) = call(sum_kernel, [VM], ((256, 256), bf))(vm(dkv_r))
+    (dw_part,) = call(dw_kernel, [VM] * 4, ((8, 192, 256), bf))(vm(xa), vm(xb), g, vm(swap(g)))
     dw_r = exchange(dw_part, C8)
-    grad, sq = call(grad_kernel, [VM], ((192, 256), f32), ((128, HD), f32))(dw_r)
+    grad, sq = call(grad_kernel, [VM], ((192, 256), f32), ((128, HD), f32))(vm(dw_r))
     parts = exchange(sq.reshape(128, 1, HD), ALL)
-    gs = [g] + [shift(g, d) for d in DELTAS]
-    wb = swap(jnp.stack(wa))
-    (d_x,) = call(dx_kernel, [SM] + [VM] * 24, ((256, 384), bf))(
-        co1, *gs, *wa, *[wb[k] for k in range(8)]
+    gs = [g]
+    for d in DELTAS:
+        gs.append(shift(g, d))
+    wb = [swap(w) for w in wa]
+    (d_x,) = call(dx_kernel, [SM] + [VM] * 16, ((256, 384), bf), near=False)(
+        co1, *map(vm, gs + wa + wb)
     )
-    (d_queries,) = call(dq_kernel, [VM] * 2, ((NL, 384, 384), bf))(dqo, swap(dqp))
-    (d_w,) = call(scale_kernel, [VM] * 2, ((192, 256), f32))(grad, parts.reshape(128, HD))
+    (d_queries,) = call(dq_kernel, [VM] * 2, ((NL, 384, 384), bf), near=False)(
+        dqo, swap(dqp)
+    )
+    (d_w,) = call(scale_kernel, [VM] * 2, ((192, 256), f32), near=False)(grad, vm(parts.reshape(128, HD)))
     return (d_queries, d_x, d_w)
 
 

time: 147 us -> 146 us (level)
  local copies, waits for them, and re-layouts: 17.5 us -> 6.14 us
  starting transfers between devices: 57.8 us -> 64.7 us
  waiting for transfers between devices: 18.8 us -> 25 us
  matrix products: 1.98 us -> 0 us
    ppermute x14 -> x7, starting transfers between devices: 29.8 us -> 14.2 us  [shift(): return lax.ppermute(a, K8, perm)]
    ppermute x8 -> x11, starting transfers between devices: 1.88 us -> 16.1 us  [swap(): return lax.ppermute(a, 'co', [(0, 1), (1, 0)])]
    ppermute x0 -> x4, starting transfers between devices: none -> 7.84 us  [split_shift(): return lax.ppermute(a, ('co', 'xh', 'z'), perm)]
    unnamed x56 -> x29, local copies, waits for them, and re-layouts: 10.6 us -> 3.74 us
    all_to_all x4, waiting for transfers between devices: 15.1 us -> 21.8 us  [exchange(): return lax.all_to_all(a, axes, 0, 0)]
    ppermute x14 -> x7, waiting for transfers between devices: 3.73 us -> 0.02 us  [shift(): return lax.ppermute(a, K8, perm)]
    ppermute x8 -> x11, waiting for transfers between devices: 0.02 us -> 3.14 us  [swap(): return lax.ppermute(a, 'co', [(0, 1), (1, 0)])]
    dot_general x1 -> x0, matrix products: 1.98 us -> none  [step(): kv_local = jnp.dot(x_kv, w_kv, preferred_element_type=f32).astype(bf)]
  transfers between devices with their start and end apart: 26 -> 26, of which waited for: 5 -> 5; matrix products, arithmetic and copies ran while one was open for 10% -> 3% of each run, Pallas kernels for 32% -> 6%
where the time goes in v1:
time: 146 us; the launch traced here: 145 us
  starting transfers between devices  64.7 us (44%)
  Pallas kernels  47.5 us (33%)
  waiting for transfers between devices  25 us (17%)
  local copies, waits for them, and re-layouts  6.14 us (4%)
  between operations  1.51 us (1%)
    pallas_call x1, Pallas kernels, attn(): pl.pallas_call(functools.partial(attn_kernel, groups), out_shape=(jax.Sha...  32.8 us
    all_to_all x4, starting transfers between devices, exchange(): return lax.all_to_all(a, axes, 0, 0)  26.5 us
    all_to_all x4, waiting for transfers between devices, exchange(): return lax.all_to_all(a, axes, 0, 0)  21.8 us
    ppermute x11, starting transfers between devices, swap(): return lax.ppermute(a, 'co', [(0, 1), (1, 0)])  16.1 us
    ppermute x7, starting transfers between devices, shift(): return lax.ppermute(a, K8, perm)  14.2 us
    ppermute x4, starting transfers between devices, split_shift(): return lax.ppermute(a, ('co', 'xh', 'z'), perm)  7.84 us
    pallas_call x1, Pallas kernels, project(): pl.pallas_call(kv_kernel, grid=(steps,), out_shape=jax.ShapeDtypeStruct((...  4.29 us
    unnamed x29, local copies, waits for them, and re-layouts  3.74 us
  transfers between devices with their start and end apart: 26, of which 5 were waited for; matrix products, arithmetic and copies ran while one was open for 3% of the time, Pallas kernels for 6%

profile of v1, /device:TPU:0, one launch (start us, length us, event | category | flops | bytes accessed | tf_op | source)
XLA Modules:
  0.0 144.9 jit_solution(9795085270847864178)
XLA Ops:
  0.6 4.3 %kv.1 = bf16[8,256,256]{2,1,0:T(8,128)(2,1)} custom-call(bf16[256,3072]{1,0:T(8,128)(2,1)} %x_ref.1, bf16[3072,256]{1,0:T(8,128)(2,1)} %w_ref.1), custom_call_target="tpu_custom_call" | custom-call | tf_op jit(solution)/shard_map/kv/pallas_call | solution.py:152
  5.0 5.7 %all-to-all-start = ((bf16[8,256,256]{2,1,0:T(8,128)(2,1)}), bf16[8,256,256]{2,1,0:T(8,128)(2,1)S(1)}, u32[]{:S(2)}, u32[]{:S(2)}) async-start(bf16[8,256,256]{2,1,0:T(8,128)(2,1)} %kv.1), calls=%async_computation | async-start | bytes 2097152 | tf_op jit(solution)/shard_map/all_to_all | solution.py:258
  12.7 1.8 %collective-permute-done.ints_p = s32[128]{0:T(128)S(1)} collective-permute-done((s32[128]{0:T(128)S(1)}, s32[128]{0:T(128)S(1)}, u32[]{:S(2)}, u32[]{:S(2)}) %collective-permute-start) | collective-permute-done | bytes 544 | tf_op jit(solution)/shard_map/ppermute | solution.py:233
  14.5 10.9 %all-to-all-done = bf16[8,256,256]{2,1,0:T(8,128)(2,1)S(1)} async-done(((bf16[8,256,256]{2,1,0:T(8,128)(2,1)}), bf16[8,256,256]{2,1,0:T(8,128)(2,1)S(1)}, u32[]{:S(2)}, u32[]{:S(2)}) %all-to-all-start) | async-done | bytes 1048608 | tf_op jit(solution)/shard_map/all_to_all | solution.py:258
  25.4 32.8 %attn.1 = (bf16[16,128,256]{2,1,0:T(8,128)(2,1)}, f32[3,128,1152]{2,1,0:T(8,128)}, bf16[3,128,1152]{2,1,0:T(8,128)(2,1)}) custom-call(s32[128]{0:T(128)} %copy-done.12, s32[128]{0:T(128)} %copy-done.13, s32[1]{0:T(128)} %bitcast.co_ref, f32[3,18,128]{2,1,0:T(8,128)S(1)} %copy.20.small_o, f32[3,18,128]{2,1,0:T(8,128)S(1)} %collective-permute-done.1.small_p, ...), custom_call_target="tpu_custom_call" | custom-call | tf_op jit(solution)/shard_map/attn/pallas_call | solution.py:116
  58.2 8.5 %all-to-all-start.1 = ((bf16[8,256,256]{2,1,0:T(8,128)(2,1)}), bf16[8,256,256]{2,1,0:T(8,128)(2,1)S(1)}, u32[]{:S(2)}, u32[]{:S(2)}) async-start(bf16[8,256,256]{2,1,0:T(8,128)(2,1)} %bitcast.31), calls=%async_computation.1 | async-start | bytes 2097152 | tf_op jit(solution)/shard_map/all_to_all | solution.py:258
  66.7 1.7 %copy.21 = bf16[256,3072]{0,1:T(8,128)(2,1)S(1)} copy(bf16[256,3072]{1,0:T(8,128)(2,1)} %x_ref.1) | data formatting | bytes 3145728 | tf_op args[0]
  68.4 1.0 dynamic-slice_bitcast_fusion
  69.9 1.3 dynamic-slice_bitcast_fusion.2
  71.2 1.3 collective-permute-start.12
  72.5 7.0 %all-to-all-done.1.r_ref = bf16[8,256,256]{2,1,0:T(8,128)(2,1)S(1)} async-done(((bf16[8,256,256]{2,1,0:T(8,128)(2,1)}), bf16[8,256,256]{2,1,0:T(8,128)(2,1)S(1)}, u32[]{:S(2)}, u32[]{:S(2)}) %all-to-all-start.1) | async-done | bytes 1048608 | tf_op jit(solution)/shard_map/all_to_all | solution.py:258
  79.8 1.3 collective-permute-done.21.gb_ref
  81.1 2.4 %shard_map.106 = bf16[8,192,256]{2,1,0:T(8,128)(2,1)} custom-call(bf16[8,192,256]{2,1,0:T(8,128)(2,1)S(1)} %get-tuple-element.14.xa_ref, bf16[8,192,256]{2,1,0:T(8,128)(2,1)S(1)} %collective-permute-done.20.xb_ref, bf16[256,256]{1,0:T(8,128)(2,1)} %copy-done, bf16[256,256]{1,0:T(8,128)(2,1)S(1)} %collective-permute-done.21.gb_ref), custom_call_target="tpu_custom_call" | custom-call | tf_op jit(solution)/shard_map/pallas_call | solution.py:286
  83.5 4.2 %all-to-all-start.2 = ((bf16[8,192,256]{2,1,0:T(8,128)(2,1)}), bf16[8,192,256]{2,1,0:T(8,128)(2,1)S(1)}, u32[]{:S(2)}, u32[]{:S(2)}) async-start(bf16[8,192,256]{2,1,0:T(8,128)(2,1)} %shard_map.106), calls=%async_computation.2 | async-start | bytes 1572864 | tf_op jit(solution)/shard_map/all_to_all | solution.py:258
  87.7 1.9 %collective-permute-start.13 = (bf16[384,256]{1,0:T(8,128)(2,1)S(1)}, bf16[384,256]{1,0:T(8,128)(2,1)S(1)}, u32[]{:S(2)}, u32[]{:S(2)}) collective-permute-start(bf16[384,256]{1,0:T(8,128)(2,1)S(1)} %get-tuple-element.17), channel_id=1, source_target_pairs={{0,1},{8,13},{1,2},{9,14},{2,3},{10,15},{3,0},{11,12},{4,5},{12,9}... | collective-permute-start | bytes 589832 | tf_op jit(solution)/shard_map/ppermute | solution.py:254
  89.6 3.6 %collective-permute-start.14 = (bf16[384,256]{1,0:T(8,128)(2,1)S(1)}, bf16[384,256]{1,0:T(8,128)(2,1)S(1)}, u32[]{:S(2)}, u32[]{:S(2)}) collective-permute-start(bf16[384,256]{1,0:T(8,128)(2,1)S(1)} %get-tuple-element.16), channel_id=1, source_target_pairs={{0,2},{8,14},{1,3},{9,15},{2,0},{10,12},{3,1},{11,13},{4,6},{12,10... | collective-permute-start | bytes 589832 | tf_op jit(solution)/shard_map/ppermute | solution.py:254
  93.2 1.0 collective-permute-start.15
  94.2 5.5 %collective-permute-start.16 = (bf16[384,256]{1,0:T(8,128)(2,1)S(1)}, bf16[384,256]{1,0:T(8,128)(2,1)S(1)}, u32[]{:S(2)}, u32[]{:S(2)}) collective-permute-start(bf16[384,256]{1,0:T(8,128)(2,1)S(1)} %broadcast_select_fusion.refs_8_), channel_id=1, source_target_pairs={{0,8},{8,0},{1,9},{9,1},{2,10},{10,2},{3,11},{11,3},{4,12},{12,4},... | collective-permute-start | bytes 589832 | tf_op jit(solution)/shard_map/ppermute | solution.py:233
  99.7 6.5 %collective-permute-start.17 = (bf16[384,256]{1,0:T(8,128)(2,1)S(1)}, bf16[384,256]{1,0:T(8,128)(2,1)S(1)}, u32[]{:S(2)}, u32[]{:S(2)}) collective-permute-start(bf16[384,256]{1,0:T(8,128)(2,1)S(1)} %collective-permute-done.13.refs_9_), channel_id=1, source_target_pairs={{0,8},{8,0},{1,9},{9,1},{2,10},{10,2},{3,11},{11,3},{4,12},{12,4},... | collective-permute-start | bytes 589832 | tf_op jit(solution)/shard_map/ppermute | solution.py:233
  106.3 1.9 %collective-permute-start.18 = (bf16[384,256]{1,0:T(8,128)(2,1)S(1)}, bf16[384,256]{1,0:T(8,128)(2,1)S(1)}, u32[]{:S(2)}, u32[]{:S(2)}) collective-permute-start(bf16[384,256]{1,0:T(8,128)(2,1)S(1)} %collective-permute-done.14.refs_10_), channel_id=1, source_target_pairs={{0,8},{8,0},{1,9},{9,1},{2,10},{10,2},{3,11},{11,3},{4,12},{12,4},... | collective-permute-start | bytes 589832 | tf_op jit(solution)/shard_map/ppermute | solution.py:233
  108.6 2.6 %collective-permute-start.5 = (bf16[256,256]{1,0:T(8,128)(2,1)S(1)}, bf16[256,256]{1,0:T(8,128)(2,1)S(1)}, u32[]{:S(2)}, u32[]{:S(2)}) collective-permute-start(bf16[256,256]{1,0:T(8,128)(2,1)S(1)} %copy-done.1), channel_id=1, source_target_pairs={{0,1},{1,2},{2,3},{3,0},{4,5},{5,6},{6,7},{7,4},{8,9},{9,10},{10,1... | collective-permute-start | bytes 393224 | tf_op jit(solution)/shard_map/ppermute | solution.py:244
  111.2 1.2 collective-permute-start.6
  112.4 2.1 %collective-permute-start.7 = (bf16[256,256]{1,0:T(8,128)(2,1)S(1)}, bf16[256,256]{1,0:T(8,128)(2,1)S(1)}, u32[]{:S(2)}, u32[]{:S(2)}) collective-permute-start(bf16[256,256]{1,0:T(8,128)(2,1)S(1)} %copy-done.1), channel_id=1, source_target_pairs={{0,3},{1,0},{2,1},{3,2},{4,7},{5,4},{6,5},{7,6},{8,11},{9,8},{10,9... | collective-permute-start | bytes 393224 | tf_op jit(solution)/shard_map/ppermute | solution.py:244
  114.5 2.9 %collective-permute-start.9 = (bf16[256,256]{1,0:T(8,128)(2,1)S(1)}, bf16[256,256]{1,0:T(8,128)(2,1)S(1)}, u32[]{:S(2)}, u32[]{:S(2)}) collective-permute-start(bf16[256,256]{1,0:T(8,128)(2,1)S(1)} %copy-done.1), channel_id=1, source_target_pairs={{0,5},{1,6},{2,7},{3,4},{4,1},{5,2},{6,3},{7,0},{8,13},{9,14},{10,... | collective-permute-start | bytes 393224 | tf_op jit(solution)/shard_map/ppermute | solution.py:244
  118.0 1.9 %collective-permute-start.10 = (bf16[256,256]{1,0:T(8,128)(2,1)S(1)}, bf16[256,256]{1,0:T(8,128)(2,1)S(1)}, u32[]{:S(2)}, u32[]{:S(2)}) collective-permute-start(bf16[256,256]{1,0:T(8,128)(2,1)S(1)} %copy-done.1), channel_id=1, source_target_pairs={{0,6},{1,7},{2,4},{3,5},{4,2},{5,3},{6,0},{7,1},{8,14},{9,15},{10,... | collective-permute-start | bytes 393224 | tf_op jit(solution)/shard_map/ppermute | solution.py:244
  120.6 3.6 %collective-permute-start.11 = (bf16[256,256]{1,0:T(8,128)(2,1)S(1)}, bf16[256,256]{1,0:T(8,128)(2,1)}, u32[]{:S(2)}, u32[]{:S(2)}) collective-permute-start(bf16[256,256]{1,0:T(8,128)(2,1)S(1)} %copy-done.1), channel_id=1, source_target_pairs={{0,7},{1,4},{2,5},{3,6},{4,3},{5,0},{6,1},{7,2},{8,15},{9,12},{10,... | collective-permute-start | bytes 393224 | tf_op jit(solution)/shard_map/ppermute | solution.py:244
  124.2 0.9 shard_map.107
  125.7 8.1 %all-to-all-start.3 = ((f32[128,1,128]{2,1,0:T(1,128)}), f32[128,1,128]{2,1,0:T(1,128)S(1)}, u32[]{:S(2)}, u32[]{:S(2)}) async-start(f32[128,1,128]{2,1,0:T(1,128)} %bitcast.16), calls=%async_computation.3 | async-start | bytes 131072 | tf_op jit(solution)/shard_map/all_to_all | solution.py:258
  133.9 3.0 %shard_map.103 = bf16[3,384,384]{2,1,0:T(8,128)(2,1)} custom-call(f32[3,128,1152]{2,1,0:T(8,128)} %get-tuple-element.8.a_ref, bf16[3,128,1152]{2,1,0:T(8,128)(2,1)} %collective-permute-done.4.b_ref), custom_call_target="tpu_custom_call" | custom-call | tf_op jit(solution)/shard_map/pallas_call | solution.py:297
  136.9 2.3 %shard_map.105 = bf16[256,384]{1,0:T(8,128)(2,1)} custom-call(s32[1]{0:T(128)} %bitcast.co_ref, bf16[256,256]{1,0:T(8,128)(2,1)S(1)} %copy-done.1, bf16[256,256]{1,0:T(8,128)(2,1)S(1)} %copy-done.4, bf16[256,256]{1,0:T(8,128)(2,1)S(1)} %copy-done.6, bf16[256,256]{1,0:T(8,128)(2,1)S(1)} %collective-permute-done.7.refs_3_, ...), custom_call_target="tpu_custom_call" | custom-call | tf_op jit(solution)/shard_map/pallas_call | solution.py:294
  139.2 4.0 %all-to-all-done.3 = f32[128,1,128]{2,1,0:T(1,128)S(1)} async-done(((f32[128,1,128]{2,1,0:T(1,128)}), f32[128,1,128]{2,1,0:T(1,128)S(1)}, u32[]{:S(2)}, u32[]{:S(2)}) %all-to-all-start.3) | async-done | bytes 65568 | tf_op jit(solution)/shard_map/all_to_all | solution.py:258
  143.2 1.7 %shard_map.108 = f32[192,256]{1,0:T(8,128)} custom-call(f32[192,256]{1,0:T(8,128)} %copy-done.2, f32[128,128]{1,0:T(8,128)S(1)} %bitcast.28), custom_call_target="tpu_custom_call" | custom-call | tf_op jit(solution)/shard_map/pallas_call | solution.py:300
  (67 shorter events, 4.6 us)
Async XLA Ops:
  4.9 6.3 %copy-start.9 = (f32[3,384,3]{1,2,0:T(4,128)S(1)}, f32[3,384,3]{1,2,0:T(4,128)}, u32[]{:S(2)}) copy-start(f32[3,384,3]{1,2,0:T(4,128)} %param.13) | copy-start | bytes 41476
  4.9 6.3 %copy-start.10 = (f32[3,384,3]{1,2,0:T(4,128)S(1)}, f32[3,384,3]{1,2,0:T(4,128)}, u32[]{:S(2)}) copy-start(f32[3,384,3]{1,2,0:T(4,128)} %param.12) | copy-start | bytes 41476
  4.9 7.2 %copy-start.11 = (s32[3,32]{1,0:T(4,128)S(1)}, s32[3,32]{1,0:T(4,128)}, u32[]{:S(2)}) copy-start(s32[3,32]{1,0:T(4,128)} %param.15) | copy-start | bytes 1156
  5.0 20.5 %all-to-all-start = ((bf16[8,256,256]{2,1,0:T(8,128)(2,1)}), bf16[8,256,256]{2,1,0:T(8,128)(2,1)S(1)}, u32[]{:S(2)}, u32[]{:S(2)}) async-start(bf16[8,256,256]{2,1,0:T(8,128)(2,1)} %kv.1), calls=%async_computation | async-start | bytes 2097152 | tf_op jit(solution)/shard_map/all_to_all | solution.py:258
  10.6 3.9 %collective-permute-start.2 = (bf16[3,384,384]{2,1,0:T(8,128)(2,1)S(1)}, bf16[3,384,384]{2,1,0:T(8,128)(2,1)}, u32[]{:S(2)}, u32[]{:S(2)}) collective-permute-start(bf16[3,384,384]{2,1,0:T(8,128)(2,1)S(1)} %copy-done.7), channel_id=1, source_target_pairs={{0,8},{8,0},{1,9},{9,1},{2,10},{10,2},{3,11},{11,3},{4,12},{12,4},... | collective-permute-start | bytes 2654216 | tf_op jit(solution)/shard_map/ppermute | solution.py:233
  10.7 3.8 %collective-permute-start.3 = (bf16[3,384,384]{2,1,0:T(8,128)(2,1)S(1)}, bf16[3,384,384]{2,1,0:T(8,128)(2,1)}, u32[]{:S(2)}, u32[]{:S(2)}) collective-permute-start(bf16[3,384,384]{2,1,0:T(8,128)(2,1)S(1)} %copy-done.8), channel_id=1, source_target_pairs={{0,8},{8,0},{1,9},{9,1},{2,10},{10,2},{3,11},{11,3},{4,12},{12,4},... | collective-permute-start | bytes 2654216 | tf_op jit(solution)/shard_map/ppermute | solution.py:233
  11.3 3.2 %collective-permute-start.1 = (f32[3,18,128]{2,1,0:T(8,128)S(1)}, f32[3,18,128]{2,1,0:T(8,128)S(1)}, u32[]{:S(2)}, u32[]{:S(2)}) collective-permute-start(f32[3,18,128]{2,1,0:T(8,128)S(1)} %copy.20.small_o), channel_id=1, source_target_pairs={{0,8},{8,0},{1,9},{9,1},{2,10},{10,2},{3,11},{11,3},{4,12},{12,4},... | collective-permute-start | bytes 82952 | tf_op jit(solution)/shard_map/ppermute | solution.py:233
  12.3 13.1 %copy-start.12 = (s32[128]{0:T(128)}, s32[128]{0:T(128)S(1)}, u32[]{:S(2)}) copy-start(s32[128]{0:T(128)S(1)} %pad_add_fusion.ints_o) | copy-start | bytes 1540
  12.3 2.2 %collective-permute-start = (s32[128]{0:T(128)S(1)}, s32[128]{0:T(128)S(1)}, u32[]{:S(2)}, u32[]{:S(2)}) collective-permute-start(s32[128]{0:T(128)S(1)} %pad_add_fusion.ints_o), channel_id=1, source_target_pairs={{0,8},{8,0},{1,9},{9,1},{2,10},{10,2},{3,11},{11,3},{4,12},{12,4},... | collective-permute-start | bytes 1544 | tf_op jit(solution)/shard_map/ppermute | solution.py:233
  14.5 10.9 %copy-start.13 = (s32[128]{0:T(128)}, s32[128]{0:T(128)S(1)}, u32[]{:S(2)}) copy-start(s32[128]{0:T(128)S(1)} %collective-permute-done.ints_p) | copy-start | bytes 1540
  58.2 21.3 %all-to-all-start.1 = ((bf16[8,256,256]{2,1,0:T(8,128)(2,1)}), bf16[8,256,256]{2,1,0:T(8,128)(2,1)S(1)}, u32[]{:S(2)}, u32[]{:S(2)}) async-start(bf16[8,256,256]{2,1,0:T(8,128)(2,1)} %bitcast.31), calls=%async_computation.1 | async-start | bytes 2097152 | tf_op jit(solution)/shard_map/all_to_all | solution.py:258
  69.4 10.3 %collective-permute-start.20 = (bf16[8,192,256]{2,1,0:T(8,128)(2,1)}, bf16[8,192,256]{2,1,0:T(8,128)(2,1)S(1)}, u32[]{:S(2)}, u32[]{:S(2)}) collective-permute-start(bf16[8,192,256]{2,1,0:T(8,128)(2,1)} %get-tuple-element.13), channel_id=1, source_target_pairs={{0,8},{8,0},{1,9},{9,1},{2,10},{10,2},{3,11},{11,3},{4,12},{12,4},... | collective-permute-start | bytes 2359304 | tf_op jit(solution)/shard_map/ppermute | solution.py:233
  69.4 45.1 %collective-permute-start.4 = (bf16[3,128,1152]{2,1,0:T(8,128)(2,1)}, bf16[3,128,1152]{2,1,0:T(8,128)(2,1)}, u32[]{:S(2)}, u32[]{:S(2)}) collective-permute-start(bf16[3,128,1152]{2,1,0:T(8,128)(2,1)} %get-tuple-element.9), channel_id=1, source_target_pairs={{0,8},{8,0},{1,9},{9,1},{2,10},{10,2},{3,11},{11,3},{4,12},{12,4},... | collective-permute-start | bytes 2654216 | tf_op jit(solution)/shard_map/ppermute | solution.py:233
  71.2 23.0 %collective-permute-start.12 = (bf16[384,256]{1,0:T(8,128)(2,1)S(1)}, bf16[384,256]{1,0:T(8,128)(2,1)}, u32[]{:S(2)}, u32[]{:S(2)}) collective-permute-start(bf16[384,256]{1,0:T(8,128)(2,1)S(1)} %get-tuple-element.18), channel_id=1, source_target_pairs={{8,12},{9,13},{10,14},{11,15},{12,8},{13,9},{14,10},{15,11},{24,28... | collective-permute-start | bytes 589832 | tf_op jit(solution)/shard_map/ppermute | solution.py:254
  79.7 1.4 collective-permute-start.21
  83.5 25.1 %copy-start.1 = (bf16[256,256]{1,0:T(8,128)(2,1)S(1)}, bf16[256,256]{1,0:T(8,128)(2,1)}, u32[]{:S(2)}) copy-start(bf16[256,256]{1,0:T(8,128)(2,1)} %copy-done) | copy-start | bytes 393220
  83.5 40.7 %all-to-all-start.2 = ((bf16[8,192,256]{2,1,0:T(8,128)(2,1)}), bf16[8,192,256]{2,1,0:T(8,128)(2,1)S(1)}, u32[]{:S(2)}, u32[]{:S(2)}) async-start(bf16[8,192,256]{2,1,0:T(8,128)(2,1)} %shard_map.106), calls=%async_computation.2 | async-start | bytes 1572864 | tf_op jit(solution)/shard_map/all_to_all | solution.py:258
  87.7 12.1 %collective-permute-start.13 = (bf16[384,256]{1,0:T(8,128)(2,1)S(1)}, bf16[384,256]{1,0:T(8,128)(2,1)S(1)}, u32[]{:S(2)}, u32[]{:S(2)}) collective-permute-start(bf16[384,256]{1,0:T(8,128)(2,1)S(1)} %get-tuple-element.17), channel_id=1, source_target_pairs={{0,1},{8,13},{1,2},{9,14},{2,3},{10,15},{3,0},{11,12},{4,5},{12,9}... | collective-permute-start | bytes 589832 | tf_op jit(solution)/shard_map/ppermute | solution.py:254
  89.6 16.7 %collective-permute-start.14 = (bf16[384,256]{1,0:T(8,128)(2,1)S(1)}, bf16[384,256]{1,0:T(8,128)(2,1)S(1)}, u32[]{:S(2)}, u32[]{:S(2)}) collective-permute-start(bf16[384,256]{1,0:T(8,128)(2,1)S(1)} %get-tuple-element.16), channel_id=1, source_target_pairs={{0,2},{8,14},{1,3},{9,15},{2,0},{10,12},{3,1},{11,13},{4,6},{12,10... | collective-permute-start | bytes 589832 | tf_op jit(solution)/shard_map/ppermute | solution.py:254
  93.2 15.1 %collective-permute-start.15 = (bf16[384,256]{1,0:T(8,128)(2,1)S(1)}, bf16[384,256]{1,0:T(8,128)(2,1)S(1)}, u32[]{:S(2)}, u32[]{:S(2)}) collective-permute-start(bf16[384,256]{1,0:T(8,128)(2,1)S(1)} %get-tuple-element.15), channel_id=1, source_target_pairs={{0,3},{8,15},{1,0},{9,12},{2,1},{10,13},{3,2},{11,14},{4,7},{12,11... | collective-permute-start | bytes 589832 | tf_op jit(solution)/shard_map/ppermute | solution.py:254
  94.2 14.4 %collective-permute-start.16 = (bf16[384,256]{1,0:T(8,128)(2,1)S(1)}, bf16[384,256]{1,0:T(8,128)(2,1)S(1)}, u32[]{:S(2)}, u32[]{:S(2)}) collective-permute-start(bf16[384,256]{1,0:T(8,128)(2,1)S(1)} %broadcast_select_fusion.refs_8_), channel_id=1, source_target_pairs={{0,8},{8,0},{1,9},{9,1},{2,10},{10,2},{3,11},{11,3},{4,12},{12,4},... | collective-permute-start | bytes 589832 | tf_op jit(solution)/shard_map/ppermute | solution.py:233
  99.7 11.5 %collective-permute-start.17 = (bf16[384,256]{1,0:T(8,128)(2,1)S(1)}, bf16[384,256]{1,0:T(8,128)(2,1)S(1)}, u32[]{:S(2)}, u32[]{:S(2)}) collective-permute-start(bf16[384,256]{1,0:T(8,128)(2,1)S(1)} %collective-permute-done.13.refs_9_), channel_id=1, source_target_pairs={{0,8},{8,0},{1,9},{9,1},{2,10},{10,2},{3,11},{11,3},{4,12},{12,4},... | collective-permute-start | bytes 589832 | tf_op jit(solution)/shard_map/ppermute | solution.py:233
  106.3 6.1 %collective-permute-start.18 = (bf16[384,256]{1,0:T(8,128)(2,1)S(1)}, bf16[384,256]{1,0:T(8,128)(2,1)S(1)}, u32[]{:S(2)}, u32[]{:S(2)}) collective-permute-start(bf16[384,256]{1,0:T(8,128)(2,1)S(1)} %collective-permute-done.14.refs_10_), channel_id=1, source_target_pairs={{0,8},{8,0},{1,9},{9,1},{2,10},{10,2},{3,11},{11,3},{4,12},{12,4},... | collective-permute-start | bytes 589832 | tf_op jit(solution)/shard_map/ppermute | solution.py:233
  108.2 6.3 %collective-permute-start.19 = (bf16[384,256]{1,0:T(8,128)(2,1)S(1)}, bf16[384,256]{1,0:T(8,128)(2,1)S(1)}, u32[]{:S(2)}, u32[]{:S(2)}) collective-permute-start(bf16[384,256]{1,0:T(8,128)(2,1)S(1)} %collective-permute-done.15.refs_11_), channel_id=1, source_target_pairs={{0,8},{8,0},{1,9},{9,1},{2,10},{10,2},{3,11},{11,3},{4,12},{12,4},... | collective-permute-start | bytes 589832 | tf_op jit(solution)/shard_map/ppermute | solution.py:233
  108.6 8.8 %collective-permute-start.5 = (bf16[256,256]{1,0:T(8,128)(2,1)S(1)}, bf16[256,256]{1,0:T(8,128)(2,1)S(1)}, u32[]{:S(2)}, u32[]{:S(2)}) collective-permute-start(bf16[256,256]{1,0:T(8,128)(2,1)S(1)} %copy-done.1), channel_id=1, source_target_pairs={{0,1},{1,2},{2,3},{3,0},{4,5},{5,6},{6,7},{7,4},{8,9},{9,10},{10,1... | collective-permute-start | bytes 393224 | tf_op jit(solution)/shard_map/ppermute | solution.py:244
  111.2 8.7 %collective-permute-start.6 = (bf16[256,256]{1,0:T(8,128)(2,1)S(1)}, bf16[256,256]{1,0:T(8,128)(2,1)S(1)}, u32[]{:S(2)}, u32[]{:S(2)}) collective-permute-start(bf16[256,256]{1,0:T(8,128)(2,1)S(1)} %copy-done.1), channel_id=1, source_target_pairs={{0,2},{1,3},{2,0},{3,1},{4,6},{5,7},{6,4},{7,5},{8,10},{9,11},{10,... | collective-permute-start | bytes 393224 | tf_op jit(solution)/shard_map/ppermute | solution.py:244
  112.4 24.5 %collective-permute-start.7 = (bf16[256,256]{1,0:T(8,128)(2,1)S(1)}, bf16[256,256]{1,0:T(8,128)(2,1)S(1)}, u32[]{:S(2)}, u32[]{:S(2)}) collective-permute-start(bf16[256,256]{1,0:T(8,128)(2,1)S(1)} %copy-done.1), channel_id=1, source_target_pairs={{0,3},{1,0},{2,1},{3,2},{4,7},{5,4},{6,5},{7,6},{8,11},{9,8},{10,9... | collective-permute-start | bytes 393224 | tf_op jit(solution)/shard_map/ppermute | solution.py:244
  114.5 22.3 %collective-permute-start.8 = (bf16[256,256]{1,0:T(8,128)(2,1)S(1)}, bf16[256,256]{1,0:T(8,128)(2,1)S(1)}, u32[]{:S(2)}, u32[]{:S(2)}) collective-permute-start(bf16[256,256]{1,0:T(8,128)(2,1)S(1)} %copy-done.1), channel_id=1, source_target_pairs={{0,4},{1,5},{2,6},{3,7},{4,0},{5,1},{6,2},{7,3},{8,12},{9,13},{10,... | collective-permute-start | bytes 393224 | tf_op jit(solution)/shard_map/ppermute | solution.py:244
  114.5 22.3 %collective-permute-start.9 = (bf16[256,256]{1,0:T(8,128)(2,1)S(1)}, bf16[256,256]{1,0:T(8,128)(2,1)S(1)}, u32[]{:S(2)}, u32[]{:S(2)}) collective-permute-start(bf16[256,256]{1,0:T(8,128)(2,1)S(1)} %copy-done.1), channel_id=1, source_target_pairs={{0,5},{1,6},{2,7},{3,4},{4,1},{5,2},{6,3},{7,0},{8,13},{9,14},{10,... | collective-permute-start | bytes 393224 | tf_op jit(solution)/shard_map/ppermute | solution.py:244
  118.0 18.8 %collective-permute-start.10 = (bf16[256,256]{1,0:T(8,128)(2,1)S(1)}, bf16[256,256]{1,0:T(8,128)(2,1)S(1)}, u32[]{:S(2)}, u32[]{:S(2)}) collective-permute-start(bf16[256,256]{1,0:T(8,128)(2,1)S(1)} %copy-done.1), channel_id=1, source_target_pairs={{0,6},{1,7},{2,4},{3,5},{4,2},{5,3},{6,0},{7,1},{8,14},{9,15},{10,... | collective-permute-start | bytes 393224 | tf_op jit(solution)/shard_map/ppermute | solution.py:244
  120.6 16.3 %collective-permute-start.11 = (bf16[256,256]{1,0:T(8,128)(2,1)S(1)}, bf16[256,256]{1,0:T(8,128)(2,1)}, u32[]{:S(2)}, u32[]{:S(2)}) collective-permute-start(bf16[256,256]{1,0:T(8,128)(2,1)S(1)} %copy-done.1), channel_id=1, source_target_pairs={{0,7},{1,4},{2,5},{3,6},{4,3},{5,0},{6,1},{7,2},{8,15},{9,12},{10,... | collective-permute-start | bytes 393224 | tf_op jit(solution)/shard_map/ppermute | solution.py:244
  125.7 17.5 %all-to-all-start.3 = ((f32[128,1,128]{2,1,0:T(1,128)}), f32[128,1,128]{2,1,0:T(1,128)S(1)}, u32[]{:S(2)}, u32[]{:S(2)}) async-start(f32[128,1,128]{2,1,0:T(1,128)} %bitcast.16), calls=%async_computation.3 | async-start | bytes 131072 | tf_op jit(solution)/shard_map/all_to_all | solution.py:258
  (8 other events, 21.0 us)

commit v2 on v1

--- a/solution.py
+++ b/solution.py
@@ -24,104 +24,147 @@
 ALL = ("xl", "y", "co", "xh", "z")
 
 
-def attn_kernel(groups, ints_o, ints_p, co_ref, small_o, small_p, kv_ref, qo, qp, oo, op, dkv_ref, dqo_ref, dqp_ref,
-                q_s, o_s, kT_s, acc_s, dq_s, p_s, ds_s, bias_s, lst, cnt, sem):
-    f32=jnp.float32; bf=jnp.bfloat16
-    copies=[pltpu.make_async_copy(a, d, sem.at[i]) for i,(a,d) in enumerate(
-        [(qo,q_s.at[0]),(oo,o_s.at[0]),(qp,q_s.at[1]),(op,o_s.at[1])])]
-    for c in copies: c.start()
-    co=co_ref[0]
-    acc_s[...]=jnp.zeros(acc_s.shape,f32)
+def attn_kernel(groups, unroll, ints_o, ints_p, co_ref, small_o, small_p, kv_ref, qo, qp, oo, op, dkv_ref, dqo_ref, dqp_ref,
+                q_s, o_s, kT_s, acc_s, dq_s, sm_s, p_s, ds_s, bias_s, lst, one_s, sem):
+    f32 = jnp.float32
+    bf = jnp.bfloat16
+    copies = [
+        pltpu.make_async_copy(a, d, sem.at[i])
+        for i, (a, d) in enumerate(
+            [(qo, q_s.at[0]), (oo, o_s.at[0]), (qp, q_s.at[1]), (op, o_s.at[1])]
+        )
+    ]
+    for c in copies:
+        c.start()
+    co = co_ref[0]
+    acc_s[...] = jnp.zeros(acc_s.shape, f32)
+    dq_s[...] = jnp.zeros(dq_s.shape, f32)
+    sm_s[0:3] = small_o[...]
+    sm_s[3:6] = small_p[...]
     for kb in range(KB):
-        kT_s[kb]=kv_ref[kb,:,:HD].T
-    for s,ints in ((0,ints_o),(1,ints_p)):
-        off=ints[96]
+        kT_s[kb] = kv_ref[kb, :, :HD].T
+
+    def key_start(kb):
+        j = kb // 2
+        return ((j // 4) * 8 + (j % 4) * 2 + co) * 256 + (kb - 2 * j) * 128
+
+    def clear(i, _):
+        one_s[i] = jnp.int32(0)
+        return 0
+
+    lax.fori_loop(0, one_s.shape[0], clear, 0)
+    n = jnp.int32(0)
+    for s, ints in ((0, ints_o), (1, ints_p)):
         for b in range(3):
-            n=jnp.int32(0)
+            low = ints[96] + b * 128
+            n = n + (n & 1)
             for kb in range(KB):
-                j,c=divmod(kb,2)
-                i=(j//4)*8+(j%4)*2+co
-                st=i*256+c*128
-                vis=(ints[b*32+2*i+c]==1)&(st<off+(b*128+127))
-                lst[s*3+b,n]=jnp.int32(kb)
-                n=n+vis.astype(jnp.int32)
-            cnt[s*3+b]=n
-            lst[s*3+b,n]=jnp.int32(KB)
-    for c in copies: c.wait()
-
-    rowi=lax.broadcasted_iota(jnp.int32,(HD,HD),0)
-    coli=lax.broadcasted_iota(jnp.int32,(HD,HD),1)
-    dif=coli-rowi
-
-    def qb_body(qb,_):
-        s=qb//3; b=qb-3*s
-        rows=pl.ds(pl.multiple_of(b*128,128),128)
-        n=cnt[qb]
-        off=jnp.where(s==0,ints_o[96],ints_p[96])+b*128
-        dq_s[...]=jnp.zeros(dq_s.shape,f32)
-        def qg(ref,lhs):
-            return jnp.concatenate([ref[s,lh//3,rows,(lh%3)*HD:(lh%3+1)*HD] for lh in lhs],axis=0)
-        def pair(t,_):
-            kb0=lst[qb,2*t]
-            kb1r=lst[qb,2*t+1]
-            one=2*t+1>=n
-            kb1=jnp.where(one,kb0,kb1r)
-            def start(kb):
-                j=kb//2
-                return ((j//4)*8+(j%4)*2+co)*256+(kb-2*j)*128
-            st0=start(kb0)
-            st1=jnp.where(one,jnp.int32(1<<20),start(kb1))
-            bias_s[0:HD]=jnp.where(dif>st0-off,f32(0),f32(NEG))
-            bias_s[HD:]=jnp.where(dif>st1-off,f32(0),f32(NEG))
-            K2=jnp.concatenate([kv_ref[kb0,:,:HD],kv_ref[kb1,:,:HD]],axis=0)
-            V2=jnp.concatenate([kv_ref[kb0,:,HD:],kv_ref[kb1,:,HD:]],axis=0)
-            K2T=jnp.concatenate([kT_s[kb0],kT_s[kb1]],axis=1)
-            bias=bias_s[...]
-            for g in groups:
-                Q=qg(q_s,g); O=qg(o_s,g)
-                ST=lax.dot_general(K2,Q,NT,preferred_element_type=f32)
-                DP=lax.dot_general(V2,O,NT,preferred_element_type=f32)
-                for u,lh in enumerate(g):
-                    cs=slice(u*HD,(u+1)*HD)
-                    lse=jnp.where(s==0,small_o[b,lh],small_p[b,lh])[None,:]*f32(LOG2E)
-                    dl=jnp.where(s==0,small_o[b,9+lh],small_p[b,9+lh])[None,:]
-                    p=jnp.exp2(ST[:,cs]*f32(C1)-lse+bias)
-                    p_s[:,lh*HD:(lh+1)*HD]=p.astype(bf)
-                    ds_s[:,lh*HD:(lh+1)*HD]=(p*(DP[:,cs]-dl)).astype(bf)
-            allq=tuple(range(NLH))
-            dv=lax.dot_general(p_s[...],qg(o_s,allq),NN,preferred_element_type=f32)
-            dk=lax.dot_general(ds_s[...],qg(q_s,allq),NN,preferred_element_type=f32)
-            acc_s[kb0,:,:HD]+=dk[:HD]
-            acc_s[kb0,:,HD:]+=dv[:HD]
-            acc_s[kb1,:,:HD]+=dk[HD:]
-            acc_s[kb1,:,HD:]+=dv[HD:]
-            dq_s[...]+=lax.dot_general(K2T,ds_s[...],NN,preferred_element_type=f32)
-            return 0
-        lax.fori_loop(0,(n+1)//2,pair,0)
-        sc=f32(HD**(-0.5))
-        @pl.when(s==0)
-        def _(): dqo_ref[b]=dq_s[...]*sc
-        @pl.when(s==1)
-        def _(): dqp_ref[b]=(dq_s[...]*sc).astype(bf)
+                j, c = divmod(kb, 2)
+                gk = 2 * ((j // 4) * 8 + (j % 4) * 2 + co) + c
+                vis = (ints[b * 32 + gk] == 1) & (gk * 128 < low + 127)
+                lst[n] = jnp.int32((3 * s + b) * KB + kb)
+                n = n + vis.astype(jnp.int32)
+            lst[n] = jnp.int32((3 * s + b) * KB)
+            one_s[n // 2] = n & 1
+    items = (n + 1) // 2
+    for extra in range(unroll):
+        lst[2 * (items + extra)] = jnp.int32(0)
+        lst[2 * (items + extra) + 1] = jnp.int32(0)
+        one_s[items + extra] = jnp.int32(2)
+    for c in copies:
+        c.wait()
+
+    dif = lax.broadcasted_iota(jnp.int32, (HD, HD), 1) - lax.broadcasted_iota(jnp.int32, (HD, HD), 0)
+    everything = tuple(range(NLH))
+
+    def item(t, slot):
+        code = lst[2 * t]
+        qb = code // KB
+        kb0 = code - qb * KB
+        kb1 = lst[2 * t + 1] - qb * KB
+        hide = one_s[t]
+        kb1 = jnp.where(hide > 0, kb0, kb1)
+        s = qb // 3
+        b = qb - 3 * s
+        low = jnp.where(s == 0, ints_o[96], ints_p[96]) + b * 128
+        far = jnp.int32(1 << 20)
+        st0 = jnp.where(hide > 1, far, key_start(kb0)) - low
+        st1 = jnp.where(hide > 0, far, key_start(kb1)) - low
+        bias_s[slot, 0:HD] = jnp.where(dif > st0, f32(0), f32(NEG))
+        bias_s[slot, HD:] = jnp.where(dif > st1, f32(0), f32(NEG))
+        rows = pl.ds(pl.multiple_of(b * 128, 128), 128)
+
+        def stack(ref, lhs):
+            return jnp.concatenate(
+                [ref[s, lh // 3, rows, (lh % 3) * HD : (lh % 3 + 1) * HD] for lh in lhs], axis=0
+            )
+
+        k2 = jnp.concatenate([kv_ref[kb0, :, :HD], kv_ref[kb1, :, :HD]], axis=0)
+        v2 = jnp.concatenate([kv_ref[kb0, :, HD:], kv_ref[kb1, :, HD:]], axis=0)
+        for g in groups:
+            st = lax.dot_general(k2, stack(q_s, g), NT, preferred_element_type=f32)
+            dp = lax.dot_general(v2, stack(o_s, g), NT, preferred_element_type=f32)
+            for u, lh in enumerate(g):
+                cs = slice(u * HD, (u + 1) * HD)
+                out = slice(lh * HD, (lh + 1) * HD)
+                lse = sm_s[qb, lh][None, :] * f32(LOG2E)
+                p = jnp.exp2(st[:, cs] * f32(C1) - lse + bias_s[slot])
+                p_s[slot, :, out] = p.astype(bf)
+                ds_s[slot, :, out] = (p * (dp[:, cs] - sm_s[qb, NLH + lh][None, :])).astype(bf)
+        dv = lax.dot_general(p_s[slot], stack(o_s, everything), NN, preferred_element_type=f32)
+        dk = lax.dot_general(ds_s[slot], stack(q_s, everything), NN, preferred_element_type=f32)
+        acc_s[kb0, :, :HD] += dk[:HD]
+        acc_s[kb0, :, HD:] += dv[:HD]
+        acc_s[kb1, :, :HD] += dk[HD:]
+        acc_s[kb1, :, HD:] += dv[HD:]
+        k2t = jnp.concatenate([kT_s[kb0], kT_s[kb1]], axis=1)
+        dq_s[qb] += lax.dot_general(k2t, ds_s[slot], NN, preferred_element_type=f32)
+
+    def trip(r, _):
+        for slot in range(unroll):
+            item(r * unroll + slot, slot)
         return 0
-    lax.fori_loop(0,QB,qb_body,0)
-    sc=f32(HD**(-0.5))
-    dkv_ref[:,:,:HD]=(acc_s[:,:,:HD]*sc).astype(bf)
-    dkv_ref[:,:,HD:]=acc_s[:,:,HD:].astype(bf)
-
-
-def attn(ints_o,ints_p,co,small_o,small_p,kv,qo,qp,oo,op,groups=((0,1),(2,3),(4,5),(6,7),(8,))):
-    f32=jnp.float32; bf=jnp.bfloat16
-    S=pl.BlockSpec(memory_space=pltpu.SMEM); V=pl.BlockSpec(memory_space=pltpu.VMEM); A=pl.BlockSpec(memory_space=pl.ANY)
+
+    lax.fori_loop(0, (items + unroll - 1) // unroll, trip, 0)
+    scale = f32(HD ** (-0.5))
+    dqo_ref[...] = dq_s[0:3] * scale
+    dqp_ref[...] = (dq_s[3:6] * scale).astype(bf)
+    dkv_ref[:, :, :HD] = (acc_s[:, :, :HD] * scale).astype(bf)
+    dkv_ref[:, :, HD:] = acc_s[:, :, HD:].astype(bf)
+
+
+def attn(ints_o, ints_p, co, small_o, small_p, kv, qo, qp, oo, op, groups=((0, 1), (2, 3), (4, 5), (6, 7), (8,)), unroll=2, near=False):
+    f32 = jnp.float32
+    bf = jnp.bfloat16
+    smem = pl.BlockSpec(memory_space=pltpu.SMEM)
+    vmem = pl.BlockSpec(memory_space=pltpu.VMEM)
+    anym = pl.BlockSpec(memory_space=pl.ANY)
+    kind = pltpu.VMEM if near else jax.ShapeDtypeStruct
     return pl.pallas_call(
-        functools.partial(attn_kernel,groups),
-        out_shape=(jax.ShapeDtypeStruct((KB,HD,2*HD),bf),jax.ShapeDtypeStruct((3,HD,NLH*HD),f32),jax.ShapeDtypeStruct((3,HD,NLH*HD),bf)),
-        in_specs=[S,S,S,V,V,V,A,A,A,A], out_specs=(V,V,V),
-        scratch_shapes=[pltpu.VMEM((2,NL,384,384),bf),pltpu.VMEM((2,NL,384,384),bf),pltpu.VMEM((KB,HD,HD),bf),
-            pltpu.VMEM((KB,HD,2*HD),f32),pltpu.VMEM((HD,NLH*HD),f32),pltpu.VMEM((2*HD,NLH*HD),bf),pltpu.VMEM((2*HD,NLH*HD),bf),
-            pltpu.VMEM((2*HD,HD),f32),pltpu.SMEM((QB,KB+1),jnp.int32),pltpu.SMEM((QB,),jnp.int32),pltpu.SemaphoreType.DMA((4,))],
+        functools.partial(attn_kernel, groups, unroll),
+        out_shape=(
+            jax.ShapeDtypeStruct((KB, HD, 2 * HD), bf),
+            kind((3, HD, NLH * HD), f32),
+            kind((3, HD, NLH * HD), bf),
+        ),
+        in_specs=[smem] * 3 + [vmem] * 3 + [anym] * 4,
+        out_specs=(vmem, vmem, vmem),
+        scratch_shapes=[
+            pltpu.VMEM((2, NL, 384, 384), bf),
+            pltpu.VMEM((2, NL, 384, 384), bf),
+            pltpu.VMEM((KB, HD, HD), bf),
+            pltpu.VMEM((KB, HD, 2 * HD), f32),
+            pltpu.VMEM((QB, HD, NLH * HD), f32),
+            pltpu.VMEM((QB, 2 * NLH, HD), f32),
+            pltpu.VMEM((unroll, 2 * HD, NLH * HD), bf),
+            pltpu.VMEM((unroll, 2 * HD, NLH * HD), bf),
+            pltpu.VMEM((unroll, 2 * HD, HD), f32),
+            pltpu.SMEM((QB * KB + 2 * unroll + 2,), jnp.int32),
+            pltpu.SMEM((QB * KB // 2 + unroll + 1,), jnp.int32),
+            pltpu.SemaphoreType.DMA((4,)),
+        ],
         name="attn",
-    )(ints_o,ints_p,co,small_o,small_p,kv,qo,qp,oo,op)
+    )(ints_o, ints_p, co, small_o, small_p, kv, qo, qp, oo, op)
 
 
 VM = pl.BlockSpec(memory_space=pltpu.VMEM)
@@ -295,9 +338,9 @@
         co1, *map(vm, gs + wa + wb)
     )
     (d_queries,) = call(dq_kernel, [VM] * 2, ((NL, 384, 384), bf), near=False)(
-        dqo, swap(dqp)
+        dqo, vm(swap(dqp))
     )
-    (d_w,) = call(scale_kernel, [VM] * 2, ((192, 256), f32), near=False)(grad, vm(parts.reshape(128, HD)))
+    (d_w,) = call(scale_kernel, [VM] * 2, ((192, 256), f32), near=False)(vm(grad), vm(parts.reshape(128, HD)))
     return (d_queries, d_x, d_w)
 
 

time: 146 us -> 141 us (0.966)
  Pallas kernels: 47.5 us -> 44.7 us
    pallas_call x2, Pallas kernels: 35.8 us -> 33.6 us  [the longest x1 30.6 us: attn(): pl.pallas_call(functools.partial(attn_kernel, groups, unroll), out_shape=...]
    unnamed x29 -> x31, local copies, waits for them, and re-layouts: 3.74 us -> 3.74 us
where the time goes in v2:
time: 141 us; the launch traced here: 140 us
  starting transfers between devices  63.8 us (45%)
  Pallas kernels  44.7 us (32%)
  waiting for transfers between devices  23.9 us (17%)
  local copies, waits for them, and re-layouts  6.15 us (4%)
  between operations  1.52 us (1%)
    pallas_call x1, Pallas kernels, attn(): pl.pallas_call(functools.partial(attn_kernel, groups, unroll), out_shape=...  30.6 us
    all_to_all x4, starting transfers between devices, exchange(): return lax.all_to_all(a, axes, 0, 0)  25.6 us
    all_to_all x4, waiting for transfers between devices, exchange(): return lax.all_to_all(a, axes, 0, 0)  20.8 us
    ppermute x11, starting transfers between devices, swap(): return lax.ppermute(a, 'co', [(0, 1), (1, 0)])  16.1 us
    ppermute x7, starting transfers between devices, shift(): return lax.ppermute(a, K8, perm)  14.3 us
    ppermute x4, starting transfers between devices, split_shift(): return lax.ppermute(a, ('co', 'xh', 'z'), perm)  7.87 us
    pallas_call x1, Pallas kernels, project(): pl.pallas_call(kv_kernel, grid=(steps,), out_shape=jax.ShapeDtypeStruct((...  4.28 us
    unnamed x31, local copies, waits for them, and re-layouts  3.74 us
  transfers between devices with their start and end apart: 26, of which 5 were waited for; matrix products, arithmetic and copies ran while one was open for 3% of the time, Pallas kernels for 6%

profile of v2, /device:TPU:0, one launch (start us, length us, event | category | flops | bytes accessed | tf_op | source)
XLA Modules:
  0.0 140.2 jit_solution(17652905300790442267)
XLA Ops:
  0.6 4.3 %kv.1 = bf16[8,256,256]{2,1,0:T(8,128)(2,1)} custom-call(bf16[256,3072]{1,0:T(8,128)(2,1)} %x_ref.1, bf16[3072,256]{1,0:T(8,128)(2,1)} %w_ref.1), custom_call_target="tpu_custom_call" | custom-call | tf_op jit(solution)/shard_map/kv/pallas_call | solution.py:195
  4.9 5.7 %all-to-all-start = ((bf16[8,256,256]{2,1,0:T(8,128)(2,1)}), bf16[8,256,256]{2,1,0:T(8,128)(2,1)S(1)}, u32[]{:S(2)}, u32[]{:S(2)}) async-start(bf16[8,256,256]{2,1,0:T(8,128)(2,1)} %kv.1), calls=%async_computation | async-start | bytes 2097152 | tf_op jit(solution)/shard_map/all_to_all | solution.py:301
  12.7 1.8 %collective-permute-done.ints_p = s32[128]{0:T(128)S(1)} collective-permute-done((s32[128]{0:T(128)S(1)}, s32[128]{0:T(128)S(1)}, u32[]{:S(2)}, u32[]{:S(2)}) %collective-permute-start) | collective-permute-done | bytes 544 | tf_op jit(solution)/shard_map/ppermute | solution.py:276
  14.5 10.9 %all-to-all-done = bf16[8,256,256]{2,1,0:T(8,128)(2,1)S(1)} async-done(((bf16[8,256,256]{2,1,0:T(8,128)(2,1)}), bf16[8,256,256]{2,1,0:T(8,128)(2,1)S(1)}, u32[]{:S(2)}, u32[]{:S(2)}) %all-to-all-start) | async-done | bytes 1048608 | tf_op jit(solution)/shard_map/all_to_all | solution.py:301
  25.4 30.6 %attn.1 = (bf16[16,128,256]{2,1,0:T(8,128)(2,1)}, f32[3,128,1152]{2,1,0:T(8,128)}, bf16[3,128,1152]{2,1,0:T(8,128)(2,1)}) custom-call(s32[128]{0:T(128)} %copy-done.13, s32[128]{0:T(128)} %copy-done.14, s32[1]{0:T(128)} %bitcast.co_ref, f32[3,18,128]{2,1,0:T(8,128)S(1)} %copy.20.small_o, f32[3,18,128]{2,1,0:T(8,128)S(1)} %collective-permute-done.1.small_p, ...), custom_call_target="tpu_custom_call" | custom-call | tf_op jit(solution)/shard_map/attn/pallas_call | solution.py:143
  56.1 8.0 %all-to-all-start.1 = ((bf16[8,256,256]{2,1,0:T(8,128)(2,1)}), bf16[8,256,256]{2,1,0:T(8,128)(2,1)S(1)}, u32[]{:S(2)}, u32[]{:S(2)}) async-start(bf16[8,256,256]{2,1,0:T(8,128)(2,1)} %bitcast.31), calls=%async_computation.1 | async-start | bytes 2097152 | tf_op jit(solution)/shard_map/all_to_all | solution.py:301
  64.1 1.7 %copy.21 = bf16[256,3072]{0,1:T(8,128)(2,1)S(1)} copy(bf16[256,3072]{1,0:T(8,128)(2,1)} %x_ref.1) | data formatting | bytes 3145728 | tf_op args[0]
  65.8 1.0 dynamic-slice_bitcast_fusion
  67.3 1.3 dynamic-slice_bitcast_fusion.2
  68.6 1.3 collective-permute-start.12
  69.9 6.2 %all-to-all-done.1.r_ref = bf16[8,256,256]{2,1,0:T(8,128)(2,1)S(1)} async-done(((bf16[8,256,256]{2,1,0:T(8,128)(2,1)}), bf16[8,256,256]{2,1,0:T(8,128)(2,1)S(1)}, u32[]{:S(2)}, u32[]{:S(2)}) %all-to-all-start.1) | async-done | bytes 1048608 | tf_op jit(solution)/shard_map/all_to_all | solution.py:301
  76.4 1.3 collective-permute-done.21.gb_ref
  77.7 2.4 %shard_map.106 = bf16[8,192,256]{2,1,0:T(8,128)(2,1)} custom-call(bf16[8,192,256]{2,1,0:T(8,128)(2,1)S(1)} %get-tuple-element.14.xa_ref, bf16[8,192,256]{2,1,0:T(8,128)(2,1)S(1)} %collective-permute-done.20.xb_ref, bf16[256,256]{1,0:T(8,128)(2,1)} %copy-done, bf16[256,256]{1,0:T(8,128)(2,1)S(1)} %collective-permute-done.21.gb_ref), custom_call_target="tpu_custom_call" | custom-call | tf_op jit(solution)/shard_map/pallas_call | solution.py:329
  80.1 3.8 %all-to-all-start.2 = ((bf16[8,192,256]{2,1,0:T(8,128)(2,1)}), bf16[8,192,256]{2,1,0:T(8,128)(2,1)S(1)}, u32[]{:S(2)}, u32[]{:S(2)}) async-start(bf16[8,192,256]{2,1,0:T(8,128)(2,1)} %shard_map.106), calls=%async_computation.2 | async-start | bytes 1572864 | tf_op jit(solution)/shard_map/all_to_all | solution.py:301
  83.9 1.9 %collective-permute-start.13 = (bf16[384,256]{1,0:T(8,128)(2,1)S(1)}, bf16[384,256]{1,0:T(8,128)(2,1)S(1)}, u32[]{:S(2)}, u32[]{:S(2)}) collective-permute-start(bf16[384,256]{1,0:T(8,128)(2,1)S(1)} %get-tuple-element.17), channel_id=1, source_target_pairs={{0,1},{8,13},{1,2},{9,14},{2,3},{10,15},{3,0},{11,12},{4,5},{12,9}... | collective-permute-start | bytes 589832 | tf_op jit(solution)/shard_map/ppermute | solution.py:297
  85.8 3.6 %collective-permute-start.14 = (bf16[384,256]{1,0:T(8,128)(2,1)S(1)}, bf16[384,256]{1,0:T(8,128)(2,1)S(1)}, u32[]{:S(2)}, u32[]{:S(2)}) collective-permute-start(bf16[384,256]{1,0:T(8,128)(2,1)S(1)} %get-tuple-element.16), channel_id=1, source_target_pairs={{0,2},{8,14},{1,3},{9,15},{2,0},{10,12},{3,1},{11,13},{4,6},{12,10... | collective-permute-start | bytes 589832 | tf_op jit(solution)/shard_map/ppermute | solution.py:297
  89.4 1.0 collective-permute-start.15
  90.4 5.5 %collective-permute-start.16 = (bf16[384,256]{1,0:T(8,128)(2,1)S(1)}, bf16[384,256]{1,0:T(8,128)(2,1)S(1)}, u32[]{:S(2)}, u32[]{:S(2)}) collective-permute-start(bf16[384,256]{1,0:T(8,128)(2,1)S(1)} %broadcast_select_fusion.refs_8_), channel_id=1, source_target_pairs={{0,8},{8,0},{1,9},{9,1},{2,10},{10,2},{3,11},{11,3},{4,12},{12,4},... | collective-permute-start | bytes 589832 | tf_op jit(solution)/shard_map/ppermute | solution.py:276
  95.9 6.5 %collective-permute-start.17 = (bf16[384,256]{1,0:T(8,128)(2,1)S(1)}, bf16[384,256]{1,0:T(8,128)(2,1)S(1)}, u32[]{:S(2)}, u32[]{:S(2)}) collective-permute-start(bf16[384,256]{1,0:T(8,128)(2,1)S(1)} %collective-permute-done.13.refs_9_), channel_id=1, source_target_pairs={{0,8},{8,0},{1,9},{9,1},{2,10},{10,2},{3,11},{11,3},{4,12},{12,4},... | collective-permute-start | bytes 589832 | tf_op jit(solution)/shard_map/ppermute | solution.py:276
  102.5 1.9 %collective-permute-start.18 = (bf16[384,256]{1,0:T(8,128)(2,1)S(1)}, bf16[384,256]{1,0:T(8,128)(2,1)S(1)}, u32[]{:S(2)}, u32[]{:S(2)}) collective-permute-start(bf16[384,256]{1,0:T(8,128)(2,1)S(1)} %collective-permute-done.14.refs_10_), channel_id=1, source_target_pairs={{0,8},{8,0},{1,9},{9,1},{2,10},{10,2},{3,11},{11,3},{4,12},{12,4},... | collective-permute-start | bytes 589832 | tf_op jit(solution)/shard_map/ppermute | solution.py:276
  104.8 2.6 %collective-permute-start.5 = (bf16[256,256]{1,0:T(8,128)(2,1)S(1)}, bf16[256,256]{1,0:T(8,128)(2,1)S(1)}, u32[]{:S(2)}, u32[]{:S(2)}) collective-permute-start(bf16[256,256]{1,0:T(8,128)(2,1)S(1)} %copy-done.1), channel_id=1, source_target_pairs={{0,1},{1,2},{2,3},{3,0},{4,5},{5,6},{6,7},{7,4},{8,9},{9,10},{10,1... | collective-permute-start | bytes 393224 | tf_op jit(solution)/shard_map/ppermute | solution.py:287
  107.4 1.2 collective-permute-start.6
  108.6 2.1 %collective-permute-start.7 = (bf16[256,256]{1,0:T(8,128)(2,1)S(1)}, bf16[256,256]{1,0:T(8,128)(2,1)}, u32[]{:S(2)}, u32[]{:S(2)}) collective-permute-start(bf16[256,256]{1,0:T(8,128)(2,1)S(1)} %copy-done.1), channel_id=1, source_target_pairs={{0,3},{1,0},{2,1},{3,2},{4,7},{5,4},{6,5},{7,6},{8,11},{9,8},{10,9... | collective-permute-start | bytes 393224 | tf_op jit(solution)/shard_map/ppermute | solution.py:287
  110.7 2.9 %collective-permute-start.9 = (bf16[256,256]{1,0:T(8,128)(2,1)S(1)}, bf16[256,256]{1,0:T(8,128)(2,1)}, u32[]{:S(2)}, u32[]{:S(2)}) collective-permute-start(bf16[256,256]{1,0:T(8,128)(2,1)S(1)} %copy-done.1), channel_id=1, source_target_pairs={{0,5},{1,6},{2,7},{3,4},{4,1},{5,2},{6,3},{7,0},{8,13},{9,14},{10,... | collective-permute-start | bytes 393224 | tf_op jit(solution)/shard_map/ppermute | solution.py:287
  114.2 1.9 %collective-permute-start.10 = (bf16[256,256]{1,0:T(8,128)(2,1)S(1)}, bf16[256,256]{1,0:T(8,128)(2,1)}, u32[]{:S(2)}, u32[]{:S(2)}) collective-permute-start(bf16[256,256]{1,0:T(8,128)(2,1)S(1)} %copy-done.1), channel_id=1, source_target_pairs={{0,6},{1,7},{2,4},{3,5},{4,2},{5,3},{6,0},{7,1},{8,14},{9,15},{10,... | collective-permute-start | bytes 393224 | tf_op jit(solution)/shard_map/ppermute | solution.py:287
  116.8 3.6 %collective-permute-start.11 = (bf16[256,256]{1,0:T(8,128)(2,1)S(1)}, bf16[256,256]{1,0:T(8,128)(2,1)}, u32[]{:S(2)}, u32[]{:S(2)}) collective-permute-start(bf16[256,256]{1,0:T(8,128)(2,1)S(1)} %copy-done.1), channel_id=1, source_target_pairs={{0,7},{1,4},{2,5},{3,6},{4,3},{5,0},{6,1},{7,2},{8,15},{9,12},{10,... | collective-permute-start | bytes 393224 | tf_op jit(solution)/shard_map/ppermute | solution.py:287
  120.3 0.9 shard_map.107
  121.9 8.1 %all-to-all-start.3 = ((f32[128,1,128]{2,1,0:T(1,128)}), f32[128,1,128]{2,1,0:T(1,128)S(1)}, u32[]{:S(2)}, u32[]{:S(2)}) async-start(f32[128,1,128]{2,1,0:T(1,128)} %bitcast.16), calls=%async_computation.3 | async-start | bytes 131072 | tf_op jit(solution)/shard_map/all_to_all | solution.py:301
  130.0 3.0 %shard_map.103 = bf16[3,384,384]{2,1,0:T(8,128)(2,1)} custom-call(f32[3,128,1152]{2,1,0:T(8,128)} %get-tuple-element.8.a_ref, bf16[3,128,1152]{2,1,0:T(8,128)(2,1)} %collective-permute-done.4.b_ref), custom_call_target="tpu_custom_call" | custom-call | tf_op jit(solution)/shard_map/pallas_call | solution.py:340
  133.1 2.6 %shard_map.105 = bf16[256,384]{1,0:T(8,128)(2,1)} custom-call(s32[1]{0:T(128)} %bitcast.co_ref, bf16[256,256]{1,0:T(8,128)(2,1)S(1)} %copy-done.1, bf16[256,256]{1,0:T(8,128)(2,1)S(1)} %copy-done.5, bf16[256,256]{1,0:T(8,128)(2,1)S(1)} %copy-done.7, bf16[256,256]{1,0:T(8,128)(2,1)} %collective-permute-done.7.refs_3_, ...), custom_call_target="tpu_custom_call" | custom-call | tf_op jit(solution)/shard_map/pallas_call | solution.py:337
  135.7 3.7 %all-to-all-done.3 = f32[128,1,128]{2,1,0:T(1,128)S(1)} async-done(((f32[128,1,128]{2,1,0:T(1,128)}), f32[128,1,128]{2,1,0:T(1,128)S(1)}, u32[]{:S(2)}, u32[]{:S(2)}) %all-to-all-start.3) | async-done | bytes 65568 | tf_op jit(solution)/shard_map/all_to_all | solution.py:301
  139.4 0.8 shard_map.108
  (69 shorter events, 4.6 us)
Async XLA Ops:
  4.9 6.3 %copy-start.10 = (f32[3,384,3]{1,2,0:T(4,128)S(1)}, f32[3,384,3]{1,2,0:T(4,128)}, u32[]{:S(2)}) copy-start(f32[3,384,3]{1,2,0:T(4,128)} %param.13) | copy-start | bytes 41476
  4.9 7.2 %copy-start.12 = (s32[3,32]{1,0:T(4,128)S(1)}, s32[3,32]{1,0:T(4,128)}, u32[]{:S(2)}) copy-start(s32[3,32]{1,0:T(4,128)} %param.15) | copy-start | bytes 1156
  4.9 20.5 %all-to-all-start = ((bf16[8,256,256]{2,1,0:T(8,128)(2,1)}), bf16[8,256,256]{2,1,0:T(8,128)(2,1)S(1)}, u32[]{:S(2)}, u32[]{:S(2)}) async-start(bf16[8,256,256]{2,1,0:T(8,128)(2,1)} %kv.1), calls=%async_computation | async-start | bytes 2097152 | tf_op jit(solution)/shard_map/all_to_all | solution.py:301
  10.6 3.9 %collective-permute-start.2 = (bf16[3,384,384]{2,1,0:T(8,128)(2,1)S(1)}, bf16[3,384,384]{2,1,0:T(8,128)(2,1)}, u32[]{:S(2)}, u32[]{:S(2)}) collective-permute-start(bf16[3,384,384]{2,1,0:T(8,128)(2,1)S(1)} %copy-done.8), channel_id=1, source_target_pairs={{0,8},{8,0},{1,9},{9,1},{2,10},{10,2},{3,11},{11,3},{4,12},{12,4},... | collective-permute-start | bytes 2654216 | tf_op jit(solution)/shard_map/ppermute | solution.py:276
  10.7 3.8 %collective-permute-start.3 = (bf16[3,384,384]{2,1,0:T(8,128)(2,1)S(1)}, bf16[3,384,384]{2,1,0:T(8,128)(2,1)}, u32[]{:S(2)}, u32[]{:S(2)}) collective-permute-start(bf16[3,384,384]{2,1,0:T(8,128)(2,1)S(1)} %copy-done.9), channel_id=1, source_target_pairs={{0,8},{8,0},{1,9},{9,1},{2,10},{10,2},{3,11},{11,3},{4,12},{12,4},... | collective-permute-start | bytes 2654216 | tf_op jit(solution)/shard_map/ppermute | solution.py:276
  11.3 3.2 %collective-permute-start.1 = (f32[3,18,128]{2,1,0:T(8,128)S(1)}, f32[3,18,128]{2,1,0:T(8,128)S(1)}, u32[]{:S(2)}, u32[]{:S(2)}) collective-permute-start(f32[3,18,128]{2,1,0:T(8,128)S(1)} %copy.20.small_o), channel_id=1, source_target_pairs={{0,8},{8,0},{1,9},{9,1},{2,10},{10,2},{3,11},{11,3},{4,12},{12,4},... | collective-permute-start | bytes 82952 | tf_op jit(solution)/shard_map/ppermute | solution.py:276
  12.3 13.1 %copy-start.13 = (s32[128]{0:T(128)}, s32[128]{0:T(128)S(1)}, u32[]{:S(2)}) copy-start(s32[128]{0:T(128)S(1)} %pad_add_fusion.ints_o) | copy-start | bytes 1540
  12.3 2.2 %collective-permute-start = (s32[128]{0:T(128)S(1)}, s32[128]{0:T(128)S(1)}, u32[]{:S(2)}, u32[]{:S(2)}) collective-permute-start(s32[128]{0:T(128)S(1)} %pad_add_fusion.ints_o), channel_id=1, source_target_pairs={{0,8},{8,0},{1,9},{9,1},{2,10},{10,2},{3,11},{11,3},{4,12},{12,4},... | collective-permute-start | bytes 1544 | tf_op jit(solution)/shard_map/ppermute | solution.py:276
  14.5 10.9 %copy-start.14 = (s32[128]{0:T(128)}, s32[128]{0:T(128)S(1)}, u32[]{:S(2)}) copy-start(s32[128]{0:T(128)S(1)} %collective-permute-done.ints_p) | copy-start | bytes 1540
  56.1 20.1 %all-to-all-start.1 = ((bf16[8,256,256]{2,1,0:T(8,128)(2,1)}), bf16[8,256,256]{2,1,0:T(8,128)(2,1)S(1)}, u32[]{:S(2)}, u32[]{:S(2)}) async-start(bf16[8,256,256]{2,1,0:T(8,128)(2,1)} %bitcast.31), calls=%async_computation.1 | async-start | bytes 2097152 | tf_op jit(solution)/shard_map/all_to_all | solution.py:301
  66.8 9.6 %collective-permute-start.20 = (bf16[8,192,256]{2,1,0:T(8,128)(2,1)}, bf16[8,192,256]{2,1,0:T(8,128)(2,1)S(1)}, u32[]{:S(2)}, u32[]{:S(2)}) collective-permute-start(bf16[8,192,256]{2,1,0:T(8,128)(2,1)} %get-tuple-element.13), channel_id=1, source_target_pairs={{0,8},{8,0},{1,9},{9,1},{2,10},{10,2},{3,11},{11,3},{4,12},{12,4},... | collective-permute-start | bytes 2359304 | tf_op jit(solution)/shard_map/ppermute | solution.py:276
  66.8 43.9 %collective-permute-start.4 = (bf16[3,128,1152]{2,1,0:T(8,128)(2,1)}, bf16[3,128,1152]{2,1,0:T(8,128)(2,1)}, u32[]{:S(2)}, u32[]{:S(2)}) collective-permute-start(bf16[3,128,1152]{2,1,0:T(8,128)(2,1)} %get-tuple-element.9), channel_id=1, source_target_pairs={{0,8},{8,0},{1,9},{9,1},{2,10},{10,2},{3,11},{11,3},{4,12},{12,4},... | collective-permute-start | bytes 2654216 | tf_op jit(solution)/shard_map/ppermute | solution.py:276
  68.6 21.8 %collective-permute-start.12 = (bf16[384,256]{1,0:T(8,128)(2,1)S(1)}, bf16[384,256]{1,0:T(8,128)(2,1)}, u32[]{:S(2)}, u32[]{:S(2)}) collective-permute-start(bf16[384,256]{1,0:T(8,128)(2,1)S(1)} %get-tuple-element.18), channel_id=1, source_target_pairs={{8,12},{9,13},{10,14},{11,15},{12,8},{13,9},{14,10},{15,11},{24,28... | collective-permute-start | bytes 589832 | tf_op jit(solution)/shard_map/ppermute | solution.py:297
  76.3 1.4 %collective-permute-start.21 = (bf16[256,256]{1,0:T(8,128)(2,1)S(1)}, bf16[256,256]{1,0:T(8,128)(2,1)S(1)}, u32[]{:S(2)}, u32[]{:S(2)}) collective-permute-start(bf16[256,256]{1,0:T(8,128)(2,1)S(1)} %shard_map.104.refs_0_.ga_ref), channel_id=1, source_target_pairs={{0,8},{8,0},{1,9},{9,1},{2,10},{10,2},{3,11},{11,3},{4,12},{12,4},... | collective-permute-start | bytes 393224 | tf_op jit(solution)/shard_map/ppermute | solution.py:276
  80.1 24.6 %copy-start.1 = (bf16[256,256]{1,0:T(8,128)(2,1)S(1)}, bf16[256,256]{1,0:T(8,128)(2,1)}, u32[]{:S(2)}) copy-start(bf16[256,256]{1,0:T(8,128)(2,1)} %copy-done) | copy-start | bytes 393220
  80.1 40.2 %all-to-all-start.2 = ((bf16[8,192,256]{2,1,0:T(8,128)(2,1)}), bf16[8,192,256]{2,1,0:T(8,128)(2,1)S(1)}, u32[]{:S(2)}, u32[]{:S(2)}) async-start(bf16[8,192,256]{2,1,0:T(8,128)(2,1)} %shard_map.106), calls=%async_computation.2 | async-start | bytes 1572864 | tf_op jit(solution)/shard_map/all_to_all | solution.py:301
  83.9 12.1 %collective-permute-start.13 = (bf16[384,256]{1,0:T(8,128)(2,1)S(1)}, bf16[384,256]{1,0:T(8,128)(2,1)S(1)}, u32[]{:S(2)}, u32[]{:S(2)}) collective-permute-start(bf16[384,256]{1,0:T(8,128)(2,1)S(1)} %get-tuple-element.17), channel_id=1, source_target_pairs={{0,1},{8,13},{1,2},{9,14},{2,3},{10,15},{3,0},{11,12},{4,5},{12,9}... | collective-permute-start | bytes 589832 | tf_op jit(solution)/shard_map/ppermute | solution.py:297
  85.8 16.7 %collective-permute-start.14 = (bf16[384,256]{1,0:T(8,128)(2,1)S(1)}, bf16[384,256]{1,0:T(8,128)(2,1)S(1)}, u32[]{:S(2)}, u32[]{:S(2)}) collective-permute-start(bf16[384,256]{1,0:T(8,128)(2,1)S(1)} %get-tuple-element.16), channel_id=1, source_target_pairs={{0,2},{8,14},{1,3},{9,15},{2,0},{10,12},{3,1},{11,13},{4,6},{12,10... | collective-permute-start | bytes 589832 | tf_op jit(solution)/shard_map/ppermute | solution.py:297
  89.4 15.0 %collective-permute-start.15 = (bf16[384,256]{1,0:T(8,128)(2,1)S(1)}, bf16[384,256]{1,0:T(8,128)(2,1)S(1)}, u32[]{:S(2)}, u32[]{:S(2)}) collective-permute-start(bf16[384,256]{1,0:T(8,128)(2,1)S(1)} %get-tuple-element.15), channel_id=1, source_target_pairs={{0,3},{8,15},{1,0},{9,12},{2,1},{10,13},{3,2},{11,14},{4,7},{12,11... | collective-permute-start | bytes 589832 | tf_op jit(solution)/shard_map/ppermute | solution.py:297
  90.4 14.3 %collective-permute-start.16 = (bf16[384,256]{1,0:T(8,128)(2,1)S(1)}, bf16[384,256]{1,0:T(8,128)(2,1)S(1)}, u32[]{:S(2)}, u32[]{:S(2)}) collective-permute-start(bf16[384,256]{1,0:T(8,128)(2,1)S(1)} %broadcast_select_fusion.refs_8_), channel_id=1, source_target_pairs={{0,8},{8,0},{1,9},{9,1},{2,10},{10,2},{3,11},{11,3},{4,12},{12,4},... | collective-permute-start | bytes 589832 | tf_op jit(solution)/shard_map/ppermute | solution.py:276
  95.9 11.5 %collective-permute-start.17 = (bf16[384,256]{1,0:T(8,128)(2,1)S(1)}, bf16[384,256]{1,0:T(8,128)(2,1)S(1)}, u32[]{:S(2)}, u32[]{:S(2)}) collective-permute-start(bf16[384,256]{1,0:T(8,128)(2,1)S(1)} %collective-permute-done.13.refs_9_), channel_id=1, source_target_pairs={{0,8},{8,0},{1,9},{9,1},{2,10},{10,2},{3,11},{11,3},{4,12},{12,4},... | collective-permute-start | bytes 589832 | tf_op jit(solution)/shard_map/ppermute | solution.py:276
  102.5 6.1 %collective-permute-start.18 = (bf16[384,256]{1,0:T(8,128)(2,1)S(1)}, bf16[384,256]{1,0:T(8,128)(2,1)S(1)}, u32[]{:S(2)}, u32[]{:S(2)}) collective-permute-start(bf16[384,256]{1,0:T(8,128)(2,1)S(1)} %collective-permute-done.14.refs_10_), channel_id=1, source_target_pairs={{0,8},{8,0},{1,9},{9,1},{2,10},{10,2},{3,11},{11,3},{4,12},{12,4},... | collective-permute-start | bytes 589832 | tf_op jit(solution)/shard_map/ppermute | solution.py:276
  104.4 6.3 %collective-permute-start.19 = (bf16[384,256]{1,0:T(8,128)(2,1)S(1)}, bf16[384,256]{1,0:T(8,128)(2,1)S(1)}, u32[]{:S(2)}, u32[]{:S(2)}) collective-permute-start(bf16[384,256]{1,0:T(8,128)(2,1)S(1)} %collective-permute-done.15.refs_11_), channel_id=1, source_target_pairs={{0,8},{8,0},{1,9},{9,1},{2,10},{10,2},{3,11},{11,3},{4,12},{12,4},... | collective-permute-start | bytes 589832 | tf_op jit(solution)/shard_map/ppermute | solution.py:276
  104.8 8.8 %collective-permute-start.5 = (bf16[256,256]{1,0:T(8,128)(2,1)S(1)}, bf16[256,256]{1,0:T(8,128)(2,1)S(1)}, u32[]{:S(2)}, u32[]{:S(2)}) collective-permute-start(bf16[256,256]{1,0:T(8,128)(2,1)S(1)} %copy-done.1), channel_id=1, source_target_pairs={{0,1},{1,2},{2,3},{3,0},{4,5},{5,6},{6,7},{7,4},{8,9},{9,10},{10,1... | collective-permute-start | bytes 393224 | tf_op jit(solution)/shard_map/ppermute | solution.py:287
  107.4 8.7 %collective-permute-start.6 = (bf16[256,256]{1,0:T(8,128)(2,1)S(1)}, bf16[256,256]{1,0:T(8,128)(2,1)S(1)}, u32[]{:S(2)}, u32[]{:S(2)}) collective-permute-start(bf16[256,256]{1,0:T(8,128)(2,1)S(1)} %copy-done.1), channel_id=1, source_target_pairs={{0,2},{1,3},{2,0},{3,1},{4,6},{5,7},{6,4},{7,5},{8,10},{9,11},{10,... | collective-permute-start | bytes 393224 | tf_op jit(solution)/shard_map/ppermute | solution.py:287
  108.6 24.5 %collective-permute-start.7 = (bf16[256,256]{1,0:T(8,128)(2,1)S(1)}, bf16[256,256]{1,0:T(8,128)(2,1)}, u32[]{:S(2)}, u32[]{:S(2)}) collective-permute-start(bf16[256,256]{1,0:T(8,128)(2,1)S(1)} %copy-done.1), channel_id=1, source_target_pairs={{0,3},{1,0},{2,1},{3,2},{4,7},{5,4},{6,5},{7,6},{8,11},{9,8},{10,9... | collective-permute-start | bytes 393224 | tf_op jit(solution)/shard_map/ppermute | solution.py:287
  110.7 22.3 %collective-permute-start.8 = (bf16[256,256]{1,0:T(8,128)(2,1)S(1)}, bf16[256,256]{1,0:T(8,128)(2,1)}, u32[]{:S(2)}, u32[]{:S(2)}) collective-permute-start(bf16[256,256]{1,0:T(8,128)(2,1)S(1)} %copy-done.1), channel_id=1, source_target_pairs={{0,4},{1,5},{2,6},{3,7},{4,0},{5,1},{6,2},{7,3},{8,12},{9,13},{10,... | collective-permute-start | bytes 393224 | tf_op jit(solution)/shard_map/ppermute | solution.py:287
  110.7 22.3 %collective-permute-start.9 = (bf16[256,256]{1,0:T(8,128)(2,1)S(1)}, bf16[256,256]{1,0:T(8,128)(2,1)}, u32[]{:S(2)}, u32[]{:S(2)}) collective-permute-start(bf16[256,256]{1,0:T(8,128)(2,1)S(1)} %copy-done.1), channel_id=1, source_target_pairs={{0,5},{1,6},{2,7},{3,4},{4,1},{5,2},{6,3},{7,0},{8,13},{9,14},{10,... | collective-permute-start | bytes 393224 | tf_op jit(solution)/shard_map/ppermute | solution.py:287
  114.2 18.8 %collective-permute-start.10 = (bf16[256,256]{1,0:T(8,128)(2,1)S(1)}, bf16[256,256]{1,0:T(8,128)(2,1)}, u32[]{:S(2)}, u32[]{:S(2)}) collective-permute-start(bf16[256,256]{1,0:T(8,128)(2,1)S(1)} %copy-done.1), channel_id=1, source_target_pairs={{0,6},{1,7},{2,4},{3,5},{4,2},{5,3},{6,0},{7,1},{8,14},{9,15},{10,... | collective-permute-start | bytes 393224 | tf_op jit(solution)/shard_map/ppermute | solution.py:287
  116.8 16.3 %collective-permute-start.11 = (bf16[256,256]{1,0:T(8,128)(2,1)S(1)}, bf16[256,256]{1,0:T(8,128)(2,1)}, u32[]{:S(2)}, u32[]{:S(2)}) collective-permute-start(bf16[256,256]{1,0:T(8,128)(2,1)S(1)} %copy-done.1), channel_id=1, source_target_pairs={{0,7},{1,4},{2,5},{3,6},{4,3},{5,0},{6,1},{7,2},{8,15},{9,12},{10,... | collective-permute-start | bytes 393224 | tf_op jit(solution)/shard_map/ppermute | solution.py:287
  121.9 17.5 %all-to-all-start.3 = ((f32[128,1,128]{2,1,0:T(1,128)}), f32[128,1,128]{2,1,0:T(1,128)S(1)}, u32[]{:S(2)}, u32[]{:S(2)}) async-start(f32[128,1,128]{2,1,0:T(1,128)} %bitcast.16), calls=%async_computation.3 | async-start | bytes 131072 | tf_op jit(solution)/shard_map/all_to_all | solution.py:301
  133.0 6.4 %copy-start.3 = (f32[192,256]{1,0:T(8,128)S(1)}, f32[192,256]{1,0:T(8,128)}, u32[]{:S(2)}) copy-start(f32[192,256]{1,0:T(8,128)} %copy-done.2) | copy-start | bytes 589828
  (9 other events, 27.3 us)

commit v3 on v2

--- a/solution.py
+++ b/solution.py
@@ -24,8 +24,8 @@
 ALL = ("xl", "y", "co", "xh", "z")
 
 
-def attn_kernel(groups, unroll, ints_o, ints_p, co_ref, small_o, small_p, kv_ref, qo, qp, oo, op, dkv_ref, dqo_ref, dqp_ref,
-                q_s, o_s, kT_s, acc_s, dq_s, sm_s, p_s, ds_s, bias_s, lst, one_s, sem):
+def attn_kernel(groups, unroll, late, ints_o, ints_p, co_ref, small_o, small_p, kv_ref, qo, qp, oo, op, dkv_ref, dqo_ref, dqp_ref,
+                q_s, o_s, kT_s, acc_s, dq_s, sm_s, bias_s, lst, one_s, sem):
     f32 = jnp.float32
     bf = jnp.bfloat16
     copies = [
@@ -101,28 +101,42 @@
 
         k2 = jnp.concatenate([kv_ref[kb0, :, :HD], kv_ref[kb1, :, :HD]], axis=0)
         v2 = jnp.concatenate([kv_ref[kb0, :, HD:], kv_ref[kb1, :, HD:]], axis=0)
+        ps, dss = [], []
         for g in groups:
             st = lax.dot_general(k2, stack(q_s, g), NT, preferred_element_type=f32)
             dp = lax.dot_general(v2, stack(o_s, g), NT, preferred_element_type=f32)
             for u, lh in enumerate(g):
                 cs = slice(u * HD, (u + 1) * HD)
-                out = slice(lh * HD, (lh + 1) * HD)
                 lse = sm_s[qb, lh][None, :] * f32(LOG2E)
                 p = jnp.exp2(st[:, cs] * f32(C1) - lse + bias_s[slot])
-                p_s[slot, :, out] = p.astype(bf)
-                ds_s[slot, :, out] = (p * (dp[:, cs] - sm_s[qb, NLH + lh][None, :])).astype(bf)
-        dv = lax.dot_general(p_s[slot], stack(o_s, everything), NN, preferred_element_type=f32)
-        dk = lax.dot_general(ds_s[slot], stack(q_s, everything), NN, preferred_element_type=f32)
-        acc_s[kb0, :, :HD] += dk[:HD]
-        acc_s[kb0, :, HD:] += dv[:HD]
-        acc_s[kb1, :, :HD] += dk[HD:]
-        acc_s[kb1, :, HD:] += dv[HD:]
-        k2t = jnp.concatenate([kT_s[kb0], kT_s[kb1]], axis=1)
-        dq_s[qb] += lax.dot_general(k2t, ds_s[slot], NN, preferred_element_type=f32)
+                ps.append(p.astype(bf))
+                dss.append((p * (dp[:, cs] - sm_s[qb, NLH + lh][None, :])).astype(bf))
+        pv = jnp.concatenate(ps, axis=1)
+        dsv = jnp.concatenate(dss, axis=1)
+
+        def finish():
+            dv = lax.dot_general(pv, stack(o_s, everything), NN, preferred_element_type=f32)
+            dk = lax.dot_general(dsv, stack(q_s, everything), NN, preferred_element_type=f32)
+            acc_s[kb0, :, :HD] += dk[:HD]
+            acc_s[kb0, :, HD:] += dv[:HD]
+            acc_s[kb1, :, :HD] += dk[HD:]
+            acc_s[kb1, :, HD:] += dv[HD:]
+            k2t = jnp.concatenate([kT_s[kb0], kT_s[kb1]], axis=1)
+            dq_s[qb] += lax.dot_general(k2t, dsv, NN, preferred_element_type=f32)
+
+        return finish
 
     def trip(r, _):
+        last = None
         for slot in range(unroll):
-            item(r * unroll + slot, slot)
+            finish = item(r * unroll + slot, slot)
+            if not late:
+                finish()
+            elif last is not None:
+                last()
+            last = finish
+        if late:
+            last()
         return 0
 
     lax.fori_loop(0, (items + unroll - 1) // unroll, trip, 0)
@@ -133,7 +147,7 @@
     dkv_ref[:, :, HD:] = acc_s[:, :, HD:].astype(bf)
 
 
-def attn(ints_o, ints_p, co, small_o, small_p, kv, qo, qp, oo, op, groups=((0, 1), (2, 3), (4, 5), (6, 7), (8,)), unroll=2, near=False):
+def attn(ints_o, ints_p, co, small_o, small_p, kv, qo, qp, oo, op, groups=((0, 1), (2, 3), (4, 5), (6, 7), (8,)), unroll=2, late=False, near=False):
     f32 = jnp.float32
     bf = jnp.bfloat16
     smem = pl.BlockSpec(memory_space=pltpu.SMEM)
@@ -141,7 +155,7 @@
     anym = pl.BlockSpec(memory_space=pl.ANY)
     kind = pltpu.VMEM if near else jax.ShapeDtypeStruct
     return pl.pallas_call(
-        functools.partial(attn_kernel, groups, unroll),
+        functools.partial(attn_kernel, groups, unroll, late),
         out_shape=(
             jax.ShapeDtypeStruct((KB, HD, 2 * HD), bf),
             kind((3, HD, NLH * HD), f32),
@@ -156,8 +170,6 @@
             pltpu.VMEM((KB, HD, 2 * HD), f32),
             pltpu.VMEM((QB, HD, NLH * HD), f32),
             pltpu.VMEM((QB, 2 * NLH, HD), f32),
-            pltpu.VMEM((unroll, 2 * HD, NLH * HD), bf),
-            pltpu.VMEM((unroll, 2 * HD, NLH * HD), bf),
             pltpu.VMEM((unroll, 2 * HD, HD), f32),
             pltpu.SMEM((QB * KB + 2 * unroll + 2,), jnp.int32),
             pltpu.SMEM((QB * KB // 2 + unroll + 1,), jnp.int32),
@@ -190,7 +202,7 @@
             out_ref[k] = kv
 
 
-def project(x, w, steps=4):
+def project(x, w, steps=2):
     depth = D // steps
     return pl.pallas_call(
         kv_kernel,
@@ -213,11 +225,31 @@
     out_ref[...] = acc.astype(jnp.bfloat16)
 
 
-def dw_kernel(xa_ref, xb_ref, ga_ref, gb_ref, out_ref):
+def dw_kernel(xa_ref, xb_ref, ga_ref, gb_ref, out_ref, near_ref, sem):
+    g = jnp.concatenate([ga_ref[...], gb_ref[...]], axis=0)
+    copies = []
     for k in range(8):
-        acc = lax.dot_general(xa_ref[k], ga_ref[...], NN, preferred_element_type=jnp.float32)
-        acc += lax.dot_general(xb_ref[k], gb_ref[...], NN, preferred_element_type=jnp.float32)
-        out_ref[k] = acc.astype(jnp.bfloat16)
+        x = jnp.concatenate([xa_ref[k], xb_ref[k]], axis=1)
+        near_ref[k] = jnp.dot(x, g, preferred_element_type=jnp.float32).astype(jnp.bfloat16)
+        copy = pltpu.make_async_copy(near_ref.at[k], out_ref.at[k], sem.at[k])
+        copy.start()
+        copies.append(copy)
+    for copy in copies:
+        copy.wait()
+
+
+def weight_parts(xa, xb, ga, gb):
+    return pl.pallas_call(
+        dw_kernel,
+        out_shape=jax.ShapeDtypeStruct((8, 192, 256), jnp.bfloat16),
+        in_specs=[pl.BlockSpec(memory_space=pltpu.VMEM)] * 4,
+        out_specs=pl.BlockSpec(memory_space=pl.ANY),
+        scratch_shapes=[
+            pltpu.VMEM((8, 192, 256), jnp.bfloat16),
+            pltpu.SemaphoreType.DMA((8,)),
+        ],
+        name="dw",
+    )(xa, xb, ga, gb)
 
 
 def grad_kernel(r_ref, grad_ref, sq_ref):
@@ -326,7 +358,7 @@
     )
     dkv_r = exchange(dkv.reshape(8, 256, 256), C8)
     (g,) = call(sum_kernel, [VM], ((256, 256), bf))(vm(dkv_r))
-    (dw_part,) = call(dw_kernel, [VM] * 4, ((8, 192, 256), bf))(vm(xa), vm(xb), g, vm(swap(g)))
+    dw_part = weight_parts(vm(xa), vm(xb), g, vm(swap(g)))
     dw_r = exchange(dw_part, C8)
     grad, sq = call(grad_kernel, [VM], ((192, 256), f32), ((128, HD), f32))(vm(dw_r))
     parts = exchange(sq.reshape(128, 1, HD), ALL)
@@ -337,9 +369,7 @@
     (d_x,) = call(dx_kernel, [SM] + [VM] * 16, ((256, 384), bf), near=False)(
         co1, *map(vm, gs + wa + wb)
     )
-    (d_queries,) = call(dq_kernel, [VM] * 2, ((NL, 384, 384), bf), near=False)(
-        dqo, vm(swap(dqp))
-    )
+    (d_queries,) = call(dq_kernel, [VM] * 2, ((NL, 384, 384), bf), near=False)(dqo, vm(swap(dqp)))
     (d_w,) = call(scale_kernel, [VM] * 2, ((192, 256), f32), near=False)(vm(grad), vm(parts.reshape(128, HD)))
     return (d_queries, d_x, d_w)
 

time: 141 us -> 140 us (level)
  no operation moved by 1% of the time
where the time goes in v3:
time: 140 us; the launch traced here: 139 us
  starting transfers between devices  63.8 us (46%)
  Pallas kernels  43.3 us (31%)
  waiting for transfers between devices  24 us (17%)
  local copies, waits for them, and re-layouts  6.16 us (4%)
  between operations  1.54 us (1%)
    pallas_call x1, Pallas kernels, attn(): pl.pallas_call(functools.partial(attn_kernel, groups, unroll, late), out_...  30.3 us
    all_to_all x4, starting transfers between devices, exchange(): return lax.all_to_all(a, axes, 0, 0)  25.5 us
    all_to_all x4, waiting for transfers between devices, exchange(): return lax.all_to_all(a, axes, 0, 0)  20.8 us
    ppermute x11, starting transfers between devices, swap(): return lax.ppermute(a, 'co', [(0, 1), (1, 0)])  16.1 us
    ppermute x7, starting transfers between devices, shift(): return lax.ppermute(a, K8, perm)  14.3 us
    ppermute x4, starting transfers between devices, split_shift(): return lax.ppermute(a, ('co', 'xh', 'z'), perm)  7.88 us
    unnamed x31, local copies, waits for them, and re-layouts  3.74 us
    pallas_call x1, Pallas kernels, project(): pl.pallas_call(kv_kernel, grid=(steps,), out_shape=jax.ShapeDtypeStruct((...  3.34 us
  transfers between devices with their start and end apart: 26, of which 5 were waited for; matrix products, arithmetic and copies ran while one was open for 3% of the time, Pallas kernels for 6%

profile of v3, /device:TPU:0, one launch (start us, length us, event | category | flops | bytes accessed | tf_op | source)
XLA Modules:
  0.0 138.8 jit_solution(3621477383150805480)
XLA Ops:
  0.6 3.3 %kv.1 = bf16[8,256,256]{2,1,0:T(8,128)(2,1)} custom-call(bf16[256,3072]{1,0:T(8,128)(2,1)} %x_ref.1, bf16[3072,256]{1,0:T(8,128)(2,1)} %w_ref.1), custom_call_target="tpu_custom_call" | custom-call | tf_op jit(solution)/shard_map/kv/pallas_call | solution.py:207
  4.0 5.7 %all-to-all-start = ((bf16[8,256,256]{2,1,0:T(8,128)(2,1)}), bf16[8,256,256]{2,1,0:T(8,128)(2,1)S(1)}, u32[]{:S(2)}, u32[]{:S(2)}) async-start(bf16[8,256,256]{2,1,0:T(8,128)(2,1)} %kv.1), calls=%async_computation | async-start | bytes 2097152 | tf_op jit(solution)/shard_map/all_to_all | solution.py:333
  11.8 1.8 %collective-permute-done.ints_p = s32[128]{0:T(128)S(1)} collective-permute-done((s32[128]{0:T(128)S(1)}, s32[128]{0:T(128)S(1)}, u32[]{:S(2)}, u32[]{:S(2)}) %collective-permute-start) | collective-permute-done | bytes 544 | tf_op jit(solution)/shard_map/ppermute | solution.py:308
  13.6 10.9 %all-to-all-done = bf16[8,256,256]{2,1,0:T(8,128)(2,1)S(1)} async-done(((bf16[8,256,256]{2,1,0:T(8,128)(2,1)}), bf16[8,256,256]{2,1,0:T(8,128)(2,1)S(1)}, u32[]{:S(2)}, u32[]{:S(2)}) %all-to-all-start) | async-done | bytes 1048608 | tf_op jit(solution)/shard_map/all_to_all | solution.py:333
  24.5 30.3 %attn.1 = (bf16[16,128,256]{2,1,0:T(8,128)(2,1)}, f32[3,128,1152]{2,1,0:T(8,128)}, bf16[3,128,1152]{2,1,0:T(8,128)(2,1)}) custom-call(s32[128]{0:T(128)} %copy-done.13, s32[128]{0:T(128)} %copy-done.14, s32[1]{0:T(128)} %bitcast.co_ref, f32[3,18,128]{2,1,0:T(8,128)S(1)} %copy.20.small_o, f32[3,18,128]{2,1,0:T(8,128)S(1)} %collective-permute-done.1.small_p, ...), custom_call_target="tpu_custom_call" | custom-call | tf_op jit(solution)/shard_map/attn/pallas_call | solution.py:157
  54.8 7.9 %all-to-all-start.1 = ((bf16[8,256,256]{2,1,0:T(8,128)(2,1)}), bf16[8,256,256]{2,1,0:T(8,128)(2,1)S(1)}, u32[]{:S(2)}, u32[]{:S(2)}) async-start(bf16[8,256,256]{2,1,0:T(8,128)(2,1)} %bitcast.31), calls=%async_computation.1 | async-start | bytes 2097152 | tf_op jit(solution)/shard_map/all_to_all | solution.py:333
  62.7 1.7 %copy.21 = bf16[256,3072]{0,1:T(8,128)(2,1)S(1)} copy(bf16[256,3072]{1,0:T(8,128)(2,1)} %x_ref.1) | data formatting | bytes 3145728 | tf_op args[0]
  64.4 1.0 dynamic-slice_bitcast_fusion
  66.0 1.3 dynamic-slice_bitcast_fusion.2
  67.2 1.3 collective-permute-start.12
  68.6 6.2 %all-to-all-done.1.r_ref = bf16[8,256,256]{2,1,0:T(8,128)(2,1)S(1)} async-done(((bf16[8,256,256]{2,1,0:T(8,128)(2,1)}), bf16[8,256,256]{2,1,0:T(8,128)(2,1)S(1)}, u32[]{:S(2)}, u32[]{:S(2)}) %all-to-all-start.1) | async-done | bytes 1048608 | tf_op jit(solution)/shard_map/all_to_all | solution.py:333
  75.1 1.3 collective-permute-done.21.gb_ref
  76.4 2.3 %dw.1 = bf16[8,192,256]{2,1,0:T(8,128)(2,1)} custom-call(bf16[8,192,256]{2,1,0:T(8,128)(2,1)S(1)} %get-tuple-element.14.xa_ref, bf16[8,192,256]{2,1,0:T(8,128)(2,1)S(1)} %collective-permute-done.20.xb_ref, bf16[256,256]{1,0:T(8,128)(2,1)} %copy-done, bf16[256,256]{1,0:T(8,128)(2,1)S(1)} %collective-permute-done.21.gb_ref), custom_call_target="tpu_custom_call" | custom-call | tf_op jit(solution)/shard_map/dw/pallas_call | solution.py:242
  78.7 3.8 %all-to-all-start.2 = ((bf16[8,192,256]{2,1,0:T(8,128)(2,1)}), bf16[8,192,256]{2,1,0:T(8,128)(2,1)S(1)}, u32[]{:S(2)}, u32[]{:S(2)}) async-start(bf16[8,192,256]{2,1,0:T(8,128)(2,1)} %dw.1), calls=%async_computation.2 | async-start | bytes 1572864 | tf_op jit(solution)/shard_map/all_to_all | solution.py:333
  82.5 1.9 %collective-permute-start.13 = (bf16[384,256]{1,0:T(8,128)(2,1)S(1)}, bf16[384,256]{1,0:T(8,128)(2,1)S(1)}, u32[]{:S(2)}, u32[]{:S(2)}) collective-permute-start(bf16[384,256]{1,0:T(8,128)(2,1)S(1)} %get-tuple-element.17), channel_id=1, source_target_pairs={{0,1},{8,13},{1,2},{9,14},{2,3},{10,15},{3,0},{11,12},{4,5},{12,9}... | collective-permute-start | bytes 589832 | tf_op jit(solution)/shard_map/ppermute | solution.py:329
  84.4 3.6 %collective-permute-start.14 = (bf16[384,256]{1,0:T(8,128)(2,1)S(1)}, bf16[384,256]{1,0:T(8,128)(2,1)S(1)}, u32[]{:S(2)}, u32[]{:S(2)}) collective-permute-start(bf16[384,256]{1,0:T(8,128)(2,1)S(1)} %get-tuple-element.16), channel_id=1, source_target_pairs={{0,2},{8,14},{1,3},{9,15},{2,0},{10,12},{3,1},{11,13},{4,6},{12,10... | collective-permute-start | bytes 589832 | tf_op jit(solution)/shard_map/ppermute | solution.py:329
  88.0 1.0 collective-permute-start.15
  89.0 5.5 %collective-permute-start.16 = (bf16[384,256]{1,0:T(8,128)(2,1)S(1)}, bf16[384,256]{1,0:T(8,128)(2,1)S(1)}, u32[]{:S(2)}, u32[]{:S(2)}) collective-permute-start(bf16[384,256]{1,0:T(8,128)(2,1)S(1)} %broadcast_select_fusion.refs_8_), channel_id=1, source_target_pairs={{0,8},{8,0},{1,9},{9,1},{2,10},{10,2},{3,11},{11,3},{4,12},{12,4},... | collective-permute-start | bytes 589832 | tf_op jit(solution)/shard_map/ppermute | solution.py:308
  94.6 6.5 %collective-permute-start.17 = (bf16[384,256]{1,0:T(8,128)(2,1)S(1)}, bf16[384,256]{1,0:T(8,128)(2,1)S(1)}, u32[]{:S(2)}, u32[]{:S(2)}) collective-permute-start(bf16[384,256]{1,0:T(8,128)(2,1)S(1)} %collective-permute-done.13.refs_9_), channel_id=1, source_target_pairs={{0,8},{8,0},{1,9},{9,1},{2,10},{10,2},{3,11},{11,3},{4,12},{12,4},... | collective-permute-start | bytes 589832 | tf_op jit(solution)/shard_map/ppermute | solution.py:308
  101.1 1.9 %collective-permute-start.18 = (bf16[384,256]{1,0:T(8,128)(2,1)S(1)}, bf16[384,256]{1,0:T(8,128)(2,1)S(1)}, u32[]{:S(2)}, u32[]{:S(2)}) collective-permute-start(bf16[384,256]{1,0:T(8,128)(2,1)S(1)} %collective-permute-done.14.refs_10_), channel_id=1, source_target_pairs={{0,8},{8,0},{1,9},{9,1},{2,10},{10,2},{3,11},{11,3},{4,12},{12,4},... | collective-permute-start | bytes 589832 | tf_op jit(solution)/shard_map/ppermute | solution.py:308
  103.4 2.6 %collective-permute-start.5 = (bf16[256,256]{1,0:T(8,128)(2,1)S(1)}, bf16[256,256]{1,0:T(8,128)(2,1)S(1)}, u32[]{:S(2)}, u32[]{:S(2)}) collective-permute-start(bf16[256,256]{1,0:T(8,128)(2,1)S(1)} %copy-done.1), channel_id=1, source_target_pairs={{0,1},{1,2},{2,3},{3,0},{4,5},{5,6},{6,7},{7,4},{8,9},{9,10},{10,1... | collective-permute-start | bytes 393224 | tf_op jit(solution)/shard_map/ppermute | solution.py:319
  106.0 1.2 collective-permute-start.6
  107.2 2.1 %collective-permute-start.7 = (bf16[256,256]{1,0:T(8,128)(2,1)S(1)}, bf16[256,256]{1,0:T(8,128)(2,1)}, u32[]{:S(2)}, u32[]{:S(2)}) collective-permute-start(bf16[256,256]{1,0:T(8,128)(2,1)S(1)} %copy-done.1), channel_id=1, source_target_pairs={{0,3},{1,0},{2,1},{3,2},{4,7},{5,4},{6,5},{7,6},{8,11},{9,8},{10,9... | collective-permute-start | bytes 393224 | tf_op jit(solution)/shard_map/ppermute | solution.py:319
  109.3 2.9 %collective-permute-start.9 = (bf16[256,256]{1,0:T(8,128)(2,1)S(1)}, bf16[256,256]{1,0:T(8,128)(2,1)}, u32[]{:S(2)}, u32[]{:S(2)}) collective-permute-start(bf16[256,256]{1,0:T(8,128)(2,1)S(1)} %copy-done.1), channel_id=1, source_target_pairs={{0,5},{1,6},{2,7},{3,4},{4,1},{5,2},{6,3},{7,0},{8,13},{9,14},{10,... | collective-permute-start | bytes 393224 | tf_op jit(solution)/shard_map/ppermute | solution.py:319
  112.9 1.9 %collective-permute-start.10 = (bf16[256,256]{1,0:T(8,128)(2,1)S(1)}, bf16[256,256]{1,0:T(8,128)(2,1)}, u32[]{:S(2)}, u32[]{:S(2)}) collective-permute-start(bf16[256,256]{1,0:T(8,128)(2,1)S(1)} %copy-done.1), channel_id=1, source_target_pairs={{0,6},{1,7},{2,4},{3,5},{4,2},{5,3},{6,0},{7,1},{8,14},{9,15},{10,... | collective-permute-start | bytes 393224 | tf_op jit(solution)/shard_map/ppermute | solution.py:319
  115.4 3.6 %collective-permute-start.11 = (bf16[256,256]{1,0:T(8,128)(2,1)S(1)}, bf16[256,256]{1,0:T(8,128)(2,1)}, u32[]{:S(2)}, u32[]{:S(2)}) collective-permute-start(bf16[256,256]{1,0:T(8,128)(2,1)S(1)} %copy-done.1), channel_id=1, source_target_pairs={{0,7},{1,4},{2,5},{3,6},{4,3},{5,0},{6,1},{7,2},{8,15},{9,12},{10,... | collective-permute-start | bytes 393224 | tf_op jit(solution)/shard_map/ppermute | solution.py:319
  119.0 0.9 shard_map.106
  120.5 8.1 %all-to-all-start.3 = ((f32[128,1,128]{2,1,0:T(1,128)}), f32[128,1,128]{2,1,0:T(1,128)S(1)}, u32[]{:S(2)}, u32[]{:S(2)}) async-start(f32[128,1,128]{2,1,0:T(1,128)} %bitcast.16), calls=%async_computation.3 | async-start | bytes 131072 | tf_op jit(solution)/shard_map/all_to_all | solution.py:333
  128.7 3.0 %shard_map.103 = bf16[3,384,384]{2,1,0:T(8,128)(2,1)} custom-call(f32[3,128,1152]{2,1,0:T(8,128)} %get-tuple-element.8.a_ref, bf16[3,128,1152]{2,1,0:T(8,128)(2,1)} %collective-permute-done.4.b_ref), custom_call_target="tpu_custom_call" | custom-call | tf_op jit(solution)/shard_map/pallas_call | solution.py:372
  131.7 2.6 %shard_map.105 = bf16[256,384]{1,0:T(8,128)(2,1)} custom-call(s32[1]{0:T(128)} %bitcast.co_ref, bf16[256,256]{1,0:T(8,128)(2,1)S(1)} %copy-done.1, bf16[256,256]{1,0:T(8,128)(2,1)S(1)} %copy-done.5, bf16[256,256]{1,0:T(8,128)(2,1)S(1)} %copy-done.7, bf16[256,256]{1,0:T(8,128)(2,1)} %collective-permute-done.7.refs_3_, ...), custom_call_target="tpu_custom_call" | custom-call | tf_op jit(solution)/shard_map/pallas_call | solution.py:369
  134.3 3.7 %all-to-all-done.3 = f32[128,1,128]{2,1,0:T(1,128)S(1)} async-done(((f32[128,1,128]{2,1,0:T(1,128)}), f32[128,1,128]{2,1,0:T(1,128)S(1)}, u32[]{:S(2)}, u32[]{:S(2)}) %all-to-all-start.3) | async-done | bytes 65568 | tf_op jit(solution)/shard_map/all_to_all | solution.py:333
  138.0 0.8 shard_map.107
  (69 shorter events, 4.6 us)
Async XLA Ops:
  4.0 6.3 %copy-start.10 = (f32[3,384,3]{1,2,0:T(4,128)S(1)}, f32[3,384,3]{1,2,0:T(4,128)}, u32[]{:S(2)}) copy-start(f32[3,384,3]{1,2,0:T(4,128)} %param.13) | copy-start | bytes 41476
  4.0 7.2 %copy-start.12 = (s32[3,32]{1,0:T(4,128)S(1)}, s32[3,32]{1,0:T(4,128)}, u32[]{:S(2)}) copy-start(s32[3,32]{1,0:T(4,128)} %param.15) | copy-start | bytes 1156
  4.0 20.5 %all-to-all-start = ((bf16[8,256,256]{2,1,0:T(8,128)(2,1)}), bf16[8,256,256]{2,1,0:T(8,128)(2,1)S(1)}, u32[]{:S(2)}, u32[]{:S(2)}) async-start(bf16[8,256,256]{2,1,0:T(8,128)(2,1)} %kv.1), calls=%async_computation | async-start | bytes 2097152 | tf_op jit(solution)/shard_map/all_to_all | solution.py:333
  9.7 3.9 %collective-permute-start.2 = (bf16[3,384,384]{2,1,0:T(8,128)(2,1)S(1)}, bf16[3,384,384]{2,1,0:T(8,128)(2,1)}, u32[]{:S(2)}, u32[]{:S(2)}) collective-permute-start(bf16[3,384,384]{2,1,0:T(8,128)(2,1)S(1)} %copy-done.8), channel_id=1, source_target_pairs={{0,8},{8,0},{1,9},{9,1},{2,10},{10,2},{3,11},{11,3},{4,12},{12,4},... | collective-permute-start | bytes 2654216 | tf_op jit(solution)/shard_map/ppermute | solution.py:308
  9.8 3.8 %collective-permute-start.3 = (bf16[3,384,384]{2,1,0:T(8,128)(2,1)S(1)}, bf16[3,384,384]{2,1,0:T(8,128)(2,1)}, u32[]{:S(2)}, u32[]{:S(2)}) collective-permute-start(bf16[3,384,384]{2,1,0:T(8,128)(2,1)S(1)} %copy-done.9), channel_id=1, source_target_pairs={{0,8},{8,0},{1,9},{9,1},{2,10},{10,2},{3,11},{11,3},{4,12},{12,4},... | collective-permute-start | bytes 2654216 | tf_op jit(solution)/shard_map/ppermute | solution.py:308
  10.3 3.2 %collective-permute-start.1 = (f32[3,18,128]{2,1,0:T(8,128)S(1)}, f32[3,18,128]{2,1,0:T(8,128)S(1)}, u32[]{:S(2)}, u32[]{:S(2)}) collective-permute-start(f32[3,18,128]{2,1,0:T(8,128)S(1)} %copy.20.small_o), channel_id=1, source_target_pairs={{0,8},{8,0},{1,9},{9,1},{2,10},{10,2},{3,11},{11,3},{4,12},{12,4},... | collective-permute-start | bytes 82952 | tf_op jit(solution)/shard_map/ppermute | solution.py:308
  11.3 13.1 %copy-start.13 = (s32[128]{0:T(128)}, s32[128]{0:T(128)S(1)}, u32[]{:S(2)}) copy-start(s32[128]{0:T(128)S(1)} %pad_add_fusion.ints_o) | copy-start | bytes 1540
  11.3 2.2 %collective-permute-start = (s32[128]{0:T(128)S(1)}, s32[128]{0:T(128)S(1)}, u32[]{:S(2)}, u32[]{:S(2)}) collective-permute-start(s32[128]{0:T(128)S(1)} %pad_add_fusion.ints_o), channel_id=1, source_target_pairs={{0,8},{8,0},{1,9},{9,1},{2,10},{10,2},{3,11},{11,3},{4,12},{12,4},... | collective-permute-start | bytes 1544 | tf_op jit(solution)/shard_map/ppermute | solution.py:308
  13.6 10.9 %copy-start.14 = (s32[128]{0:T(128)}, s32[128]{0:T(128)S(1)}, u32[]{:S(2)}) copy-start(s32[128]{0:T(128)S(1)} %collective-permute-done.ints_p) | copy-start | bytes 1540
  54.8 20.1 %all-to-all-start.1 = ((bf16[8,256,256]{2,1,0:T(8,128)(2,1)}), bf16[8,256,256]{2,1,0:T(8,128)(2,1)S(1)}, u32[]{:S(2)}, u32[]{:S(2)}) async-start(bf16[8,256,256]{2,1,0:T(8,128)(2,1)} %bitcast.31), calls=%async_computation.1 | async-start | bytes 2097152 | tf_op jit(solution)/shard_map/all_to_all | solution.py:333
  65.5 9.6 %collective-permute-start.20 = (bf16[8,192,256]{2,1,0:T(8,128)(2,1)}, bf16[8,192,256]{2,1,0:T(8,128)(2,1)S(1)}, u32[]{:S(2)}, u32[]{:S(2)}) collective-permute-start(bf16[8,192,256]{2,1,0:T(8,128)(2,1)} %get-tuple-element.13), channel_id=1, source_target_pairs={{0,8},{8,0},{1,9},{9,1},{2,10},{10,2},{3,11},{11,3},{4,12},{12,4},... | collective-permute-start | bytes 2359304 | tf_op jit(solution)/shard_map/ppermute | solution.py:308
  65.5 43.9 %collective-permute-start.4 = (bf16[3,128,1152]{2,1,0:T(8,128)(2,1)}, bf16[3,128,1152]{2,1,0:T(8,128)(2,1)}, u32[]{:S(2)}, u32[]{:S(2)}) collective-permute-start(bf16[3,128,1152]{2,1,0:T(8,128)(2,1)} %get-tuple-element.9), channel_id=1, source_target_pairs={{0,8},{8,0},{1,9},{9,1},{2,10},{10,2},{3,11},{11,3},{4,12},{12,4},... | collective-permute-start | bytes 2654216 | tf_op jit(solution)/shard_map/ppermute | solution.py:308
  67.2 21.8 %collective-permute-start.12 = (bf16[384,256]{1,0:T(8,128)(2,1)S(1)}, bf16[384,256]{1,0:T(8,128)(2,1)}, u32[]{:S(2)}, u32[]{:S(2)}) collective-permute-start(bf16[384,256]{1,0:T(8,128)(2,1)S(1)} %get-tuple-element.18), channel_id=1, source_target_pairs={{8,12},{9,13},{10,14},{11,15},{12,8},{13,9},{14,10},{15,11},{24,28... | collective-permute-start | bytes 589832 | tf_op jit(solution)/shard_map/ppermute | solution.py:329
  75.0 1.4 %collective-permute-start.21 = (bf16[256,256]{1,0:T(8,128)(2,1)S(1)}, bf16[256,256]{1,0:T(8,128)(2,1)S(1)}, u32[]{:S(2)}, u32[]{:S(2)}) collective-permute-start(bf16[256,256]{1,0:T(8,128)(2,1)S(1)} %shard_map.104.refs_0_.ga_ref), channel_id=1, source_target_pairs={{0,8},{8,0},{1,9},{9,1},{2,10},{10,2},{3,11},{11,3},{4,12},{12,4},... | collective-permute-start | bytes 393224 | tf_op jit(solution)/shard_map/ppermute | solution.py:308
  78.7 24.7 %copy-start.1 = (bf16[256,256]{1,0:T(8,128)(2,1)S(1)}, bf16[256,256]{1,0:T(8,128)(2,1)}, u32[]{:S(2)}) copy-start(bf16[256,256]{1,0:T(8,128)(2,1)} %copy-done) | copy-start | bytes 393220
  78.7 40.3 %all-to-all-start.2 = ((bf16[8,192,256]{2,1,0:T(8,128)(2,1)}), bf16[8,192,256]{2,1,0:T(8,128)(2,1)S(1)}, u32[]{:S(2)}, u32[]{:S(2)}) async-start(bf16[8,192,256]{2,1,0:T(8,128)(2,1)} %dw.1), calls=%async_computation.2 | async-start | bytes 1572864 | tf_op jit(solution)/shard_map/all_to_all | solution.py:333
  82.5 12.1 %collective-permute-start.13 = (bf16[384,256]{1,0:T(8,128)(2,1)S(1)}, bf16[384,256]{1,0:T(8,128)(2,1)S(1)}, u32[]{:S(2)}, u32[]{:S(2)}) collective-permute-start(bf16[384,256]{1,0:T(8,128)(2,1)S(1)} %get-tuple-element.17), channel_id=1, source_target_pairs={{0,1},{8,13},{1,2},{9,14},{2,3},{10,15},{3,0},{11,12},{4,5},{12,9}... | collective-permute-start | bytes 589832 | tf_op jit(solution)/shard_map/ppermute | solution.py:329
  84.4 16.7 %collective-permute-start.14 = (bf16[384,256]{1,0:T(8,128)(2,1)S(1)}, bf16[384,256]{1,0:T(8,128)(2,1)S(1)}, u32[]{:S(2)}, u32[]{:S(2)}) collective-permute-start(bf16[384,256]{1,0:T(8,128)(2,1)S(1)} %get-tuple-element.16), channel_id=1, source_target_pairs={{0,2},{8,14},{1,3},{9,15},{2,0},{10,12},{3,1},{11,13},{4,6},{12,10... | collective-permute-start | bytes 589832 | tf_op jit(solution)/shard_map/ppermute | solution.py:329
  88.0 15.1 %collective-permute-start.15 = (bf16[384,256]{1,0:T(8,128)(2,1)S(1)}, bf16[384,256]{1,0:T(8,128)(2,1)S(1)}, u32[]{:S(2)}, u32[]{:S(2)}) collective-permute-start(bf16[384,256]{1,0:T(8,128)(2,1)S(1)} %get-tuple-element.15), channel_id=1, source_target_pairs={{0,3},{8,15},{1,0},{9,12},{2,1},{10,13},{3,2},{11,14},{4,7},{12,11... | collective-permute-start | bytes 589832 | tf_op jit(solution)/shard_map/ppermute | solution.py:329
  89.0 14.3 %collective-permute-start.16 = (bf16[384,256]{1,0:T(8,128)(2,1)S(1)}, bf16[384,256]{1,0:T(8,128)(2,1)S(1)}, u32[]{:S(2)}, u32[]{:S(2)}) collective-permute-start(bf16[384,256]{1,0:T(8,128)(2,1)S(1)} %broadcast_select_fusion.refs_8_), channel_id=1, source_target_pairs={{0,8},{8,0},{1,9},{9,1},{2,10},{10,2},{3,11},{11,3},{4,12},{12,4},... | collective-permute-start | bytes 589832 | tf_op jit(solution)/shard_map/ppermute | solution.py:308
  94.6 11.5 %collective-permute-start.17 = (bf16[384,256]{1,0:T(8,128)(2,1)S(1)}, bf16[384,256]{1,0:T(8,128)(2,1)S(1)}, u32[]{:S(2)}, u32[]{:S(2)}) collective-permute-start(bf16[384,256]{1,0:T(8,128)(2,1)S(1)} %collective-permute-done.13.refs_9_), channel_id=1, source_target_pairs={{0,8},{8,0},{1,9},{9,1},{2,10},{10,2},{3,11},{11,3},{4,12},{12,4},... | collective-permute-start | bytes 589832 | tf_op jit(solution)/shard_map/ppermute | solution.py:308
  101.1 6.1 %collective-permute-start.18 = (bf16[384,256]{1,0:T(8,128)(2,1)S(1)}, bf16[384,256]{1,0:T(8,128)(2,1)S(1)}, u32[]{:S(2)}, u32[]{:S(2)}) collective-permute-start(bf16[384,256]{1,0:T(8,128)(2,1)S(1)} %collective-permute-done.14.refs_10_), channel_id=1, source_target_pairs={{0,8},{8,0},{1,9},{9,1},{2,10},{10,2},{3,11},{11,3},{4,12},{12,4},... | collective-permute-start | bytes 589832 | tf_op jit(solution)/shard_map/ppermute | solution.py:308
  103.1 6.3 %collective-permute-start.19 = (bf16[384,256]{1,0:T(8,128)(2,1)S(1)}, bf16[384,256]{1,0:T(8,128)(2,1)S(1)}, u32[]{:S(2)}, u32[]{:S(2)}) collective-permute-start(bf16[384,256]{1,0:T(8,128)(2,1)S(1)} %collective-permute-done.15.refs_11_), channel_id=1, source_target_pairs={{0,8},{8,0},{1,9},{9,1},{2,10},{10,2},{3,11},{11,3},{4,12},{12,4},... | collective-permute-start | bytes 589832 | tf_op jit(solution)/shard_map/ppermute | solution.py:308
  103.4 8.8 %collective-permute-start.5 = (bf16[256,256]{1,0:T(8,128)(2,1)S(1)}, bf16[256,256]{1,0:T(8,128)(2,1)S(1)}, u32[]{:S(2)}, u32[]{:S(2)}) collective-permute-start(bf16[256,256]{1,0:T(8,128)(2,1)S(1)} %copy-done.1), channel_id=1, source_target_pairs={{0,1},{1,2},{2,3},{3,0},{4,5},{5,6},{6,7},{7,4},{8,9},{9,10},{10,1... | collective-permute-start | bytes 393224 | tf_op jit(solution)/shard_map/ppermute | solution.py:319
  106.0 8.7 %collective-permute-start.6 = (bf16[256,256]{1,0:T(8,128)(2,1)S(1)}, bf16[256,256]{1,0:T(8,128)(2,1)S(1)}, u32[]{:S(2)}, u32[]{:S(2)}) collective-permute-start(bf16[256,256]{1,0:T(8,128)(2,1)S(1)} %copy-done.1), channel_id=1, source_target_pairs={{0,2},{1,3},{2,0},{3,1},{4,6},{5,7},{6,4},{7,5},{8,10},{9,11},{10,... | collective-permute-start | bytes 393224 | tf_op jit(solution)/shard_map/ppermute | solution.py:319
  107.2 24.5 %collective-permute-start.7 = (bf16[256,256]{1,0:T(8,128)(2,1)S(1)}, bf16[256,256]{1,0:T(8,128)(2,1)}, u32[]{:S(2)}, u32[]{:S(2)}) collective-permute-start(bf16[256,256]{1,0:T(8,128)(2,1)S(1)} %copy-done.1), channel_id=1, source_target_pairs={{0,3},{1,0},{2,1},{3,2},{4,7},{5,4},{6,5},{7,6},{8,11},{9,8},{10,9... | collective-permute-start | bytes 393224 | tf_op jit(solution)/shard_map/ppermute | solution.py:319
  109.3 22.3 %collective-permute-start.8 = (bf16[256,256]{1,0:T(8,128)(2,1)S(1)}, bf16[256,256]{1,0:T(8,128)(2,1)}, u32[]{:S(2)}, u32[]{:S(2)}) collective-permute-start(bf16[256,256]{1,0:T(8,128)(2,1)S(1)} %copy-done.1), channel_id=1, source_target_pairs={{0,4},{1,5},{2,6},{3,7},{4,0},{5,1},{6,2},{7,3},{8,12},{9,13},{10,... | collective-permute-start | bytes 393224 | tf_op jit(solution)/shard_map/ppermute | solution.py:319
  109.3 22.3 %collective-permute-start.9 = (bf16[256,256]{1,0:T(8,128)(2,1)S(1)}, bf16[256,256]{1,0:T(8,128)(2,1)}, u32[]{:S(2)}, u32[]{:S(2)}) collective-permute-start(bf16[256,256]{1,0:T(8,128)(2,1)S(1)} %copy-done.1), channel_id=1, source_target_pairs={{0,5},{1,6},{2,7},{3,4},{4,1},{5,2},{6,3},{7,0},{8,13},{9,14},{10,... | collective-permute-start | bytes 393224 | tf_op jit(solution)/shard_map/ppermute | solution.py:319
  112.9 18.8 %collective-permute-start.10 = (bf16[256,256]{1,0:T(8,128)(2,1)S(1)}, bf16[256,256]{1,0:T(8,128)(2,1)}, u32[]{:S(2)}, u32[]{:S(2)}) collective-permute-start(bf16[256,256]{1,0:T(8,128)(2,1)S(1)} %copy-done.1), channel_id=1, source_target_pairs={{0,6},{1,7},{2,4},{3,5},{4,2},{5,3},{6,0},{7,1},{8,14},{9,15},{10,... | collective-permute-start | bytes 393224 | tf_op jit(solution)/shard_map/ppermute | solution.py:319
  115.4 16.3 %collective-permute-start.11 = (bf16[256,256]{1,0:T(8,128)(2,1)S(1)}, bf16[256,256]{1,0:T(8,128)(2,1)}, u32[]{:S(2)}, u32[]{:S(2)}) collective-permute-start(bf16[256,256]{1,0:T(8,128)(2,1)S(1)} %copy-done.1), channel_id=1, source_target_pairs={{0,7},{1,4},{2,5},{3,6},{4,3},{5,0},{6,1},{7,2},{8,15},{9,12},{10,... | collective-permute-start | bytes 393224 | tf_op jit(solution)/shard_map/ppermute | solution.py:319
  120.5 17.5 %all-to-all-start.3 = ((f32[128,1,128]{2,1,0:T(1,128)}), f32[128,1,128]{2,1,0:T(1,128)S(1)}, u32[]{:S(2)}, u32[]{:S(2)}) async-start(f32[128,1,128]{2,1,0:T(1,128)} %bitcast.16), calls=%async_computation.3 | async-start | bytes 131072 | tf_op jit(solution)/shard_map/all_to_all | solution.py:333
  131.7 6.4 %copy-start.3 = (f32[192,256]{1,0:T(8,128)S(1)}, f32[192,256]{1,0:T(8,128)}, u32[]{:S(2)}) copy-start(f32[192,256]{1,0:T(8,128)} %copy-done.2) | copy-start | bytes 589828
  (9 other events, 27.3 us)

commit v4 on v3

--- a/solution.py
+++ b/solution.py
@@ -181,6 +181,7 @@
 
 VM = pl.BlockSpec(memory_space=pltpu.VMEM)
 SM = pl.BlockSpec(memory_space=pltpu.SMEM)
+ANY = pl.BlockSpec(memory_space=pl.ANY)
 
 
 def kv_kernel(x_ref, w_ref, out_ref, acc_ref):
@@ -225,6 +226,27 @@
     out_ref[...] = acc.astype(jnp.bfloat16)
 
 
+def xt_kernel(co_ref, x_ref, mine_ref, other_ref, flip_ref):
+    mine = pl.ds(pl.multiple_of(co_ref[0] * 192, 64), 192)
+    other = pl.ds(pl.multiple_of((1 - co_ref[0]) * 192, 64), 192)
+    for k in range(8):
+        flip_ref[k] = x_ref[:, k * 384 : (k + 1) * 384].T
+        mine_ref[k] = flip_ref[k, mine]
+        other_ref[k] = flip_ref[k, other]
+
+
+def split_tokens(co, x):
+    part = jax.ShapeDtypeStruct((8, 192, 256), jnp.bfloat16)
+    return pl.pallas_call(
+        xt_kernel,
+        out_shape=(part, part),
+        in_specs=[SM, VM],
+        out_specs=(VM, VM),
+        scratch_shapes=[pltpu.VMEM((8, 384, 256), jnp.bfloat16)],
+        name="xt",
+    )(co, x)
+
+
 def dw_kernel(xa_ref, xb_ref, ga_ref, gb_ref, out_ref, near_ref, sem):
     g = jnp.concatenate([ga_ref[...], gb_ref[...]], axis=0)
     copies = []
@@ -248,6 +270,7 @@
             pltpu.VMEM((8, 192, 256), jnp.bfloat16),
             pltpu.SemaphoreType.DMA((8,)),
         ],
+        compiler_params=pltpu.CompilerParams(vmem_limit_bytes=20 << 20),
         name="dw",
     )(xa, xb, ga, gb)
 
@@ -285,7 +308,8 @@
         total(wb, wa)
 
 
-def dq_kernel(a_ref, b_ref, out_ref):
+def dq_kernel(a_ref, b_ref, w0, w1, w2, w3, out_ref):
+    del w0, w1, w2, w3
     for b in range(3):
         for lh in range(NLH):
             cs = slice(lh * HD, (lh + 1) * HD)
@@ -349,9 +373,8 @@
     ints = jnp.concatenate([block_mask.reshape(96), offsets, jnp.zeros((31,), jnp.int32)])
     rows = jnp.concatenate([lse, delta], axis=2).reshape(NL, 3, HD, 2, 3)
     small = jnp.transpose(rows, (1, 3, 0, 4, 2)).reshape(3, 2 * NLH, HD)
-    x_t = x_kv.T.reshape(8, 2, 192, 256)
-    xa = lax.dynamic_index_in_dim(x_t, co, 1, False)
-    xb = swap(lax.dynamic_index_in_dim(x_t, 1 - co, 1, False))
+    xa, xb = split_tokens(co1, x_kv)
+    xb = swap(xb)
     dkv, dqo, dqp = attn(
         ints, swap(ints), co1, vm(small), vm(swap(small)),
         vm(kv_all.reshape(KB, HD, 2 * HD)), queries, swap(queries), d_out, swap(d_out),
@@ -369,7 +392,9 @@
     (d_x,) = call(dx_kernel, [SM] + [VM] * 16, ((256, 384), bf), near=False)(
         co1, *map(vm, gs + wa + wb)
     )
-    (d_queries,) = call(dq_kernel, [VM] * 2, ((NL, 384, 384), bf), near=False)(dqo, vm(swap(dqp)))
+    (d_queries,) = call(dq_kernel, [VM] * 2 + [ANY] * 4, ((NL, 384, 384), bf), near=False)(
+        dqo, vm(swap(dqp)), *wb
+    )
     (d_w,) = call(scale_kernel, [VM] * 2, ((192, 256), f32), near=False)(vm(grad), vm(parts.reshape(128, HD)))
     return (d_queries, d_x, d_w)
 

time: 140 us -> 144 us (1.029)
  waiting for transfers between devices: 24 us -> 19.3 us
  local copies, waits for them, and re-layouts: 6.16 us -> 10.8 us
  Pallas kernels: 43.3 us -> 47.1 us
    unnamed x31 -> x48, local copies, waits for them, and re-layouts: 3.74 us -> 8.75 us
    all_to_all x4, waiting for transfers between devices: 20.8 us -> 16.1 us  [exchange(): return lax.all_to_all(a, axes, 0, 0)]
    pallas_call x1 -> x2, Pallas kernels: 2.97 us -> 5.82 us  [the longest x1 3.07 us: split_tokens(): pl.pallas_call(xt_kernel, out_shape=(part, part), in_specs=[SM, VM], out_...]
  transfers between devices with their start and end apart: 26 -> 26, of which waited for: 5 -> 4; matrix products, arithmetic and copies ran while one was open for 3% -> 2% of each run, Pallas kernels for 6% -> 8%
where the time goes in v4:
time: 144 us; the launch traced here: 143 us
  starting transfers between devices  63.9 us (44%)
  Pallas kernels  47.1 us (33%)
  waiting for transfers between devices  19.3 us (13%)
  local copies, waits for them, and re-layouts  10.8 us (8%)
  between operations  1.54 us (1%)
    pallas_call x1, Pallas kernels, attn(): pl.pallas_call(functools.partial(attn_kernel, groups, unroll, late), out_...  30.3 us
    all_to_all x4, starting transfers between devices, exchange(): return lax.all_to_all(a, axes, 0, 0)  26.4 us
    all_to_all x4, waiting for transfers between devices, exchange(): return lax.all_to_all(a, axes, 0, 0)  16.1 us
    ppermute x11, starting transfers between devices, swap(): return lax.ppermute(a, 'co', [(0, 1), (1, 0)])  15.3 us
    ppermute x7, starting transfers between devices, shift(): return lax.ppermute(a, K8, perm)  14.3 us
    unnamed x48, local copies, waits for them, and re-layouts  8.75 us
    ppermute x4, starting transfers between devices, split_shift(): return lax.ppermute(a, ('co', 'xh', 'z'), perm)  7.86 us
    pallas_call x1, Pallas kernels, project(): pl.pallas_call(kv_kernel, grid=(steps,), out_shape=jax.ShapeDtypeStruct((...  3.35 us
  transfers between devices with their start and end apart: 26, of which 4 were waited for; matrix products, arithmetic and copies ran while one was open for 2% of the time, Pallas kernels for 8%

profile of v4, /device:TPU:0, one launch (start us, length us, event | category | flops | bytes accessed | tf_op | source)
XLA Modules:
  0.0 142.8 jit_solution(10418893586960556337)
XLA Ops:
  0.6 3.3 %kv.1 = bf16[8,256,256]{2,1,0:T(8,128)(2,1)} custom-call(bf16[256,3072]{1,0:T(8,128)(2,1)} %x_ref.3, bf16[3072,256]{1,0:T(8,128)(2,1)} %w_ref.1), custom_call_target="tpu_custom_call" | custom-call | tf_op jit(solution)/shard_map/kv/pallas_call | solution.py:208
  4.0 5.7 %all-to-all-start = ((bf16[8,256,256]{2,1,0:T(8,128)(2,1)}), bf16[8,256,256]{2,1,0:T(8,128)(2,1)S(1)}, u32[]{:S(2)}, u32[]{:S(2)}) async-start(bf16[8,256,256]{2,1,0:T(8,128)(2,1)} %kv.1), calls=%async_computation | async-start | bytes 2097152 | tf_op jit(solution)/shard_map/all_to_all | solution.py:357
  11.8 1.8 %collective-permute-done.ints_p = s32[128]{0:T(128)S(1)} collective-permute-done((s32[128]{0:T(128)S(1)}, s32[128]{0:T(128)S(1)}, u32[]{:S(2)}, u32[]{:S(2)}) %collective-permute-start) | collective-permute-done | bytes 544 | tf_op jit(solution)/shard_map/ppermute | solution.py:332
  13.6 10.9 %all-to-all-done = bf16[8,256,256]{2,1,0:T(8,128)(2,1)S(1)} async-done(((bf16[8,256,256]{2,1,0:T(8,128)(2,1)}), bf16[8,256,256]{2,1,0:T(8,128)(2,1)S(1)}, u32[]{:S(2)}, u32[]{:S(2)}) %all-to-all-start) | async-done | bytes 1048608 | tf_op jit(solution)/shard_map/all_to_all | solution.py:357
  24.5 30.3 %attn.1 = (bf16[16,128,256]{2,1,0:T(8,128)(2,1)}, f32[3,128,1152]{2,1,0:T(8,128)}, bf16[3,128,1152]{2,1,0:T(8,128)(2,1)}) custom-call(s32[128]{0:T(128)} %copy-done.22, s32[128]{0:T(128)} %copy-done.23, s32[1]{0:T(128)} %bitcast.co_ref, f32[3,18,128]{2,1,0:T(8,128)S(1)} %copy.17.small_o, f32[3,18,128]{2,1,0:T(8,128)S(1)} %collective-permute-done.1.small_p, ...), custom_call_target="tpu_custom_call" | custom-call | tf_op jit(solution)/shard_map/attn/pallas_call | solution.py:157
  54.8 7.9 %all-to-all-start.1 = ((bf16[8,256,256]{2,1,0:T(8,128)(2,1)}), bf16[8,256,256]{2,1,0:T(8,128)(2,1)S(1)}, u32[]{:S(2)}, u32[]{:S(2)}) async-start(bf16[8,256,256]{2,1,0:T(8,128)(2,1)} %bitcast.22), calls=%async_computation.1 | async-start | bytes 2097152 | tf_op jit(solution)/shard_map/all_to_all | solution.py:357
  62.7 3.1 %xt.1 = (bf16[8,192,256]{2,1,0:T(8,128)(2,1)}, bf16[8,192,256]{2,1,0:T(8,128)(2,1)}) custom-call(s32[1]{0:T(128)} %bitcast.co_ref, bf16[256,3072]{1,0:T(8,128)(2,1)} %x_ref.3), custom_call_target="tpu_custom_call" | custom-call | tf_op jit(solution)/shard_map/xt/pallas_call | solution.py:240
  66.3 1.9 %dynamic-slice_bitcast_fusion = (bf16[384,256]{1,0:T(8,128)(2,1)S(1)}, bf16[384,256]{1,0:T(8,128)(2,1)S(1)}, bf16[384,256]{1,0:T(8,128)(2,1)}, bf16[384,256]{1,0:T(8,128)(2,1)S(1)}) fusion(bf16[8,384,256]{2,1,0:T(8,128)(2,1)} %bitcast.21, s32[]{:T(128)S(6)} %select_n.60, s32[]{:T(128)S(6)} %select_n.58, s32[]{:T(128)S(6)} %select_n.56, s32[]{:T(128)S(6)} %select_n.53), kind=kLoop, calls=%fused_computation | loop fusion | bytes 1572880 | tf_op jit(solution)/shard_map/jit(dynamic_index_in_dim)/squeeze | solution.py:370
  68.3 1.3 collective-permute-start.5
  69.6 5.3 %all-to-all-done.1.r_ref = bf16[8,256,256]{2,1,0:T(8,128)(2,1)S(1)} async-done(((bf16[8,256,256]{2,1,0:T(8,128)(2,1)}), bf16[8,256,256]{2,1,0:T(8,128)(2,1)S(1)}, u32[]{:S(2)}, u32[]{:S(2)}) %all-to-all-start.1) | async-done | bytes 1048608 | tf_op jit(solution)/shard_map/all_to_all | solution.py:357
  75.1 1.3 collective-permute-done.21.gb_ref
  76.4 2.5 %dw.1 = bf16[8,192,256]{2,1,0:T(8,128)(2,1)} custom-call(bf16[8,192,256]{2,1,0:T(8,128)(2,1)S(1)} %copy-done.10, bf16[8,192,256]{2,1,0:T(8,128)(2,1)} %collective-permute-done.20.xb_ref, bf16[256,256]{1,0:T(8,128)(2,1)S(1)} %shard_map.104.refs_0_.ga_ref, bf16[256,256]{1,0:T(8,128)(2,1)S(1)} %collective-permute-done.21.gb_ref), custom_call_target="tpu_custom_call" | custom-call | tf_op jit(solution)/shard_map/dw/pallas_call | solution.py:264
  78.9 3.6 %all-to-all-start.2 = ((bf16[8,192,256]{2,1,0:T(8,128)(2,1)}), bf16[8,192,256]{2,1,0:T(8,128)(2,1)S(1)}, u32[]{:S(2)}, u32[]{:S(2)}) async-start(bf16[8,192,256]{2,1,0:T(8,128)(2,1)} %dw.1), calls=%async_computation.2 | async-start | bytes 1572864 | tf_op jit(solution)/shard_map/all_to_all | solution.py:357
  82.5 1.9 %collective-permute-start.7 = (bf16[384,256]{1,0:T(8,128)(2,1)}, bf16[384,256]{1,0:T(8,128)(2,1)S(1)}, u32[]{:S(2)}, u32[]{:S(2)}) collective-permute-start(bf16[384,256]{1,0:T(8,128)(2,1)} %get-tuple-element.19), channel_id=1, source_target_pairs={{0,1},{8,13},{1,2},{9,14},{2,3},{10,15},{3,0},{11,12},{4,5},{12,9}... | collective-permute-start | bytes 589832 | tf_op jit(solution)/shard_map/ppermute | solution.py:353
  84.5 3.6 %collective-permute-start.9 = (bf16[384,256]{1,0:T(8,128)(2,1)S(1)}, bf16[384,256]{1,0:T(8,128)(2,1)S(1)}, u32[]{:S(2)}, u32[]{:S(2)}) collective-permute-start(bf16[384,256]{1,0:T(8,128)(2,1)S(1)} %get-tuple-element.18), channel_id=1, source_target_pairs={{0,2},{8,14},{1,3},{9,15},{2,0},{10,12},{3,1},{11,13},{4,6},{12,10... | collective-permute-start | bytes 589832 | tf_op jit(solution)/shard_map/ppermute | solution.py:353
  88.1 1.0 collective-permute-start.11
  89.1 4.8 %collective-permute-start.6 = (bf16[384,256]{1,0:T(8,128)(2,1)S(1)}, bf16[384,256]{1,0:T(8,128)(2,1)S(1)}, u32[]{:S(2)}, u32[]{:S(2)}) collective-permute-start(bf16[384,256]{1,0:T(8,128)(2,1)S(1)} %broadcast_select_fusion.refs_8_), channel_id=1, source_target_pairs={{0,8},{8,0},{1,9},{9,1},{2,10},{10,2},{3,11},{11,3},{4,12},{12,4},... | collective-permute-start | bytes 589832 | tf_op jit(solution)/shard_map/ppermute | solution.py:332
  94.0 6.4 %collective-permute-start.8 = (bf16[384,256]{1,0:T(8,128)(2,1)S(1)}, bf16[384,256]{1,0:T(8,128)(2,1)S(1)}, u32[]{:S(2)}, u32[]{:S(2)}) collective-permute-start(bf16[384,256]{1,0:T(8,128)(2,1)S(1)} %collective-permute-done.7.refs_9_), channel_id=1, source_target_pairs={{0,8},{8,0},{1,9},{9,1},{2,10},{10,2},{3,11},{11,3},{4,12},{12,4},... | collective-permute-start | bytes 589832 | tf_op jit(solution)/shard_map/ppermute | solution.py:332
  100.4 1.9 %collective-permute-start.10 = (bf16[384,256]{1,0:T(8,128)(2,1)S(1)}, bf16[384,256]{1,0:T(8,128)(2,1)S(1)}, u32[]{:S(2)}, u32[]{:S(2)}) collective-permute-start(bf16[384,256]{1,0:T(8,128)(2,1)S(1)} %collective-permute-done.9.refs_10_), channel_id=1, source_target_pairs={{0,8},{8,0},{1,9},{9,1},{2,10},{10,2},{3,11},{11,3},{4,12},{12,4},... | collective-permute-start | bytes 589832 | tf_op jit(solution)/shard_map/ppermute | solution.py:332
  102.6 2.6 %collective-permute-start.13 = (bf16[256,256]{1,0:T(8,128)(2,1)S(1)}, bf16[256,256]{1,0:T(8,128)(2,1)S(1)}, u32[]{:S(2)}, u32[]{:S(2)}) collective-permute-start(bf16[256,256]{1,0:T(8,128)(2,1)S(1)} %shard_map.104.refs_0_.ga_ref), channel_id=1, source_target_pairs={{0,1},{1,2},{2,3},{3,0},{4,5},{5,6},{6,7},{7,4},{8,9},{9,10},{10,1... | collective-permute-start | bytes 393224 | tf_op jit(solution)/shard_map/ppermute | solution.py:343
  105.3 1.1 collective-permute-start.14
  106.5 2.1 %collective-permute-start.15 = (bf16[256,256]{1,0:T(8,128)(2,1)S(1)}, bf16[256,256]{1,0:T(8,128)(2,1)}, u32[]{:S(2)}, u32[]{:S(2)}) collective-permute-start(bf16[256,256]{1,0:T(8,128)(2,1)S(1)} %shard_map.104.refs_0_.ga_ref), channel_id=1, source_target_pairs={{0,3},{1,0},{2,1},{3,2},{4,7},{5,4},{6,5},{7,6},{8,11},{9,8},{10,9... | collective-permute-start | bytes 393224 | tf_op jit(solution)/shard_map/ppermute | solution.py:343
  110.3 2.1 %collective-permute-start.17 = (bf16[256,256]{1,0:T(8,128)(2,1)S(1)}, bf16[256,256]{1,0:T(8,128)(2,1)}, u32[]{:S(2)}, u32[]{:S(2)}) collective-permute-start(bf16[256,256]{1,0:T(8,128)(2,1)S(1)} %shard_map.104.refs_0_.ga_ref), channel_id=1, source_target_pairs={{0,5},{1,6},{2,7},{3,4},{4,1},{5,2},{6,3},{7,0},{8,13},{9,14},{10,... | collective-permute-start | bytes 393224 | tf_op jit(solution)/shard_map/ppermute | solution.py:343
  113.0 2.6 %collective-permute-start.18 = (bf16[256,256]{1,0:T(8,128)(2,1)S(1)}, bf16[256,256]{1,0:T(8,128)(2,1)}, u32[]{:S(2)}, u32[]{:S(2)}) collective-permute-start(bf16[256,256]{1,0:T(8,128)(2,1)S(1)} %shard_map.104.refs_0_.ga_ref), channel_id=1, source_target_pairs={{0,6},{1,7},{2,4},{3,5},{4,2},{5,3},{6,0},{7,1},{8,14},{9,15},{10,... | collective-permute-start | bytes 393224 | tf_op jit(solution)/shard_map/ppermute | solution.py:343
  116.3 2.9 %collective-permute-start.19 = (bf16[256,256]{1,0:T(8,128)(2,1)S(1)}, bf16[256,256]{1,0:T(8,128)(2,1)}, u32[]{:S(2)}, u32[]{:S(2)}) collective-permute-start(bf16[256,256]{1,0:T(8,128)(2,1)S(1)} %shard_map.104.refs_0_.ga_ref), channel_id=1, source_target_pairs={{0,7},{1,4},{2,5},{3,6},{4,3},{5,0},{6,1},{7,2},{8,15},{9,12},{10,... | collective-permute-start | bytes 393224 | tf_op jit(solution)/shard_map/ppermute | solution.py:343
  120.7 9.2 %all-to-all-start.3 = ((f32[128,1,128]{2,1,0:T(1,128)}), f32[128,1,128]{2,1,0:T(1,128)}, u32[]{:S(2)}, u32[]{:S(2)}) async-start(f32[128,1,128]{2,1,0:T(1,128)} %bitcast.11), calls=%async_computation.3 | async-start | bytes 131072 | tf_op jit(solution)/shard_map/all_to_all | solution.py:357
  130.0 1.2 copy-done.1
  131.1 2.7 %shard_map.103 = bf16[3,384,384]{2,1,0:T(8,128)(2,1)} custom-call(f32[3,128,1152]{2,1,0:T(8,128)} %get-tuple-element.10.a_ref, bf16[3,128,1152]{2,1,0:T(8,128)(2,1)S(1)} %copy-done.1, bf16[384,256]{1,0:T(8,128)(2,1)} %copy-done.2, bf16[384,256]{1,0:T(8,128)(2,1)} %copy-done.4, bf16[384,256]{1,0:T(8,128)(2,1)} %copy-done.6, bf16[384,256]{1,0:T(8,128)(2,1)} %copy-done.8), custom_call_target="tpu_custom_call" | custom-call | tf_op jit(solution)/shard_map/pallas_call | solution.py:395
  134.9 0.9 copy-done.5
  137.6 2.6 %shard_map.105 = bf16[256,384]{1,0:T(8,128)(2,1)} custom-call(s32[1]{0:T(128)} %bitcast.co_ref, bf16[256,256]{1,0:T(8,128)(2,1)S(1)} %shard_map.104.refs_0_.ga_ref, bf16[256,256]{1,0:T(8,128)(2,1)S(1)} %copy-done.14, bf16[256,256]{1,0:T(8,128)(2,1)S(1)} %copy-done.16, bf16[256,256]{1,0:T(8,128)(2,1)} %collective-permute-done.15.refs_3_, ...), custom_call_target="tpu_custom_call" | custom-call | tf_op jit(solution)/shard_map/pallas_call | solution.py:392
  140.2 0.9 copy-done.12
  141.2 1.6 %shard_map.107 = f32[192,256]{1,0:T(8,128)} custom-call(f32[192,256]{1,0:T(8,128)S(1)} %copy-done.12, f32[128,128]{1,0:T(8,128)} %bitcast.12.parts_ref), custom_call_target="tpu_custom_call" | custom-call | tf_op jit(solution)/shard_map/pallas_call | solution.py:398
  (86 shorter events, 9.9 us)
Async XLA Ops:
  4.0 20.5 %all-to-all-start = ((bf16[8,256,256]{2,1,0:T(8,128)(2,1)}), bf16[8,256,256]{2,1,0:T(8,128)(2,1)S(1)}, u32[]{:S(2)}, u32[]{:S(2)}) async-start(bf16[8,256,256]{2,1,0:T(8,128)(2,1)} %kv.1), calls=%async_computation | async-start | bytes 2097152 | tf_op jit(solution)/shard_map/all_to_all | solution.py:357
  9.7 3.9 %collective-permute-start.2 = (bf16[3,384,384]{2,1,0:T(8,128)(2,1)S(1)}, bf16[3,384,384]{2,1,0:T(8,128)(2,1)}, u32[]{:S(2)}, u32[]{:S(2)}) collective-permute-start(bf16[3,384,384]{2,1,0:T(8,128)(2,1)S(1)} %copy-done.17), channel_id=1, source_target_pairs={{0,8},{8,0},{1,9},{9,1},{2,10},{10,2},{3,11},{11,3},{4,12},{12,4},... | collective-permute-start | bytes 2654216 | tf_op jit(solution)/shard_map/ppermute | solution.py:332
  9.8 3.8 %collective-permute-start.3 = (bf16[3,384,384]{2,1,0:T(8,128)(2,1)S(1)}, bf16[3,384,384]{2,1,0:T(8,128)(2,1)}, u32[]{:S(2)}, u32[]{:S(2)}) collective-permute-start(bf16[3,384,384]{2,1,0:T(8,128)(2,1)S(1)} %copy-done.18), channel_id=1, source_target_pairs={{0,8},{8,0},{1,9},{9,1},{2,10},{10,2},{3,11},{11,3},{4,12},{12,4},... | collective-permute-start | bytes 2654216 | tf_op jit(solution)/shard_map/ppermute | solution.py:332
  10.3 3.2 %collective-permute-start.1 = (f32[3,18,128]{2,1,0:T(8,128)S(1)}, f32[3,18,128]{2,1,0:T(8,128)S(1)}, u32[]{:S(2)}, u32[]{:S(2)}) collective-permute-start(f32[3,18,128]{2,1,0:T(8,128)S(1)} %copy.17.small_o), channel_id=1, source_target_pairs={{0,8},{8,0},{1,9},{9,1},{2,10},{10,2},{3,11},{11,3},{4,12},{12,4},... | collective-permute-start | bytes 82952 | tf_op jit(solution)/shard_map/ppermute | solution.py:332
  11.3 13.1 %copy-start.22 = (s32[128]{0:T(128)}, s32[128]{0:T(128)S(1)}, u32[]{:S(2)}) copy-start(s32[128]{0:T(128)S(1)} %pad_add_fusion.ints_o) | copy-start | bytes 1540
  11.3 2.2 %collective-permute-start = (s32[128]{0:T(128)S(1)}, s32[128]{0:T(128)S(1)}, u32[]{:S(2)}, u32[]{:S(2)}) collective-permute-start(s32[128]{0:T(128)S(1)} %pad_add_fusion.ints_o), channel_id=1, source_target_pairs={{0,8},{8,0},{1,9},{9,1},{2,10},{10,2},{3,11},{11,3},{4,12},{12,4},... | collective-permute-start | bytes 1544 | tf_op jit(solution)/shard_map/ppermute | solution.py:332
  13.6 10.9 %copy-start.23 = (s32[128]{0:T(128)}, s32[128]{0:T(128)S(1)}, u32[]{:S(2)}) copy-start(s32[128]{0:T(128)S(1)} %collective-permute-done.ints_p) | copy-start | bytes 1540
  54.8 20.1 %all-to-all-start.1 = ((bf16[8,256,256]{2,1,0:T(8,128)(2,1)}), bf16[8,256,256]{2,1,0:T(8,128)(2,1)S(1)}, u32[]{:S(2)}, u32[]{:S(2)}) async-start(bf16[8,256,256]{2,1,0:T(8,128)(2,1)} %bitcast.22), calls=%async_computation.1 | async-start | bytes 2097152 | tf_op jit(solution)/shard_map/all_to_all | solution.py:357
  65.8 9.3 %collective-permute-start.20 = (bf16[8,192,256]{2,1,0:T(8,128)(2,1)}, bf16[8,192,256]{2,1,0:T(8,128)(2,1)}, u32[]{:S(2)}, u32[]{:S(2)}) collective-permute-start(bf16[8,192,256]{2,1,0:T(8,128)(2,1)} %get-tuple-element.14), channel_id=1, source_target_pairs={{0,8},{8,0},{1,9},{9,1},{2,10},{10,2},{3,11},{11,3},{4,12},{12,4},... | collective-permute-start | bytes 2359304 | tf_op jit(solution)/shard_map/ppermute | solution.py:332
  65.8 43.6 %collective-permute-start.4 = (bf16[3,128,1152]{2,1,0:T(8,128)(2,1)}, bf16[3,128,1152]{2,1,0:T(8,128)(2,1)S(1)}, u32[]{:S(2)}, u32[]{:S(2)}) collective-permute-start(bf16[3,128,1152]{2,1,0:T(8,128)(2,1)} %get-tuple-element.11), channel_id=1, source_target_pairs={{0,8},{8,0},{1,9},{9,1},{2,10},{10,2},{3,11},{11,3},{4,12},{12,4},... | collective-permute-start | bytes 2654216 | tf_op jit(solution)/shard_map/ppermute | solution.py:332
  68.3 20.8 %collective-permute-start.5 = (bf16[384,256]{1,0:T(8,128)(2,1)S(1)}, bf16[384,256]{1,0:T(8,128)(2,1)}, u32[]{:S(2)}, u32[]{:S(2)}) collective-permute-start(bf16[384,256]{1,0:T(8,128)(2,1)S(1)} %get-tuple-element.20), channel_id=1, source_target_pairs={{8,12},{9,13},{10,14},{11,15},{12,8},{13,9},{14,10},{15,11},{24,28... | collective-permute-start | bytes 589832 | tf_op jit(solution)/shard_map/ppermute | solution.py:353
  75.0 1.4 %collective-permute-start.21 = (bf16[256,256]{1,0:T(8,128)(2,1)S(1)}, bf16[256,256]{1,0:T(8,128)(2,1)S(1)}, u32[]{:S(2)}, u32[]{:S(2)}) collective-permute-start(bf16[256,256]{1,0:T(8,128)(2,1)S(1)} %shard_map.104.refs_0_.ga_ref), channel_id=1, source_target_pairs={{0,8},{8,0},{1,9},{9,1},{2,10},{10,2},{3,11},{11,3},{4,12},{12,4},... | collective-permute-start | bytes 393224 | tf_op jit(solution)/shard_map/ppermute | solution.py:332
  78.9 40.3 %all-to-all-start.2 = ((bf16[8,192,256]{2,1,0:T(8,128)(2,1)}), bf16[8,192,256]{2,1,0:T(8,128)(2,1)S(1)}, u32[]{:S(2)}, u32[]{:S(2)}) async-start(bf16[8,192,256]{2,1,0:T(8,128)(2,1)} %dw.1), calls=%async_computation.2 | async-start | bytes 1572864 | tf_op jit(solution)/shard_map/all_to_all | solution.py:357
  82.5 11.4 %collective-permute-start.7 = (bf16[384,256]{1,0:T(8,128)(2,1)}, bf16[384,256]{1,0:T(8,128)(2,1)S(1)}, u32[]{:S(2)}, u32[]{:S(2)}) collective-permute-start(bf16[384,256]{1,0:T(8,128)(2,1)} %get-tuple-element.19), channel_id=1, source_target_pairs={{0,1},{8,13},{1,2},{9,14},{2,3},{10,15},{3,0},{11,12},{4,5},{12,9}... | collective-permute-start | bytes 589832 | tf_op jit(solution)/shard_map/ppermute | solution.py:353
  84.5 15.9 %collective-permute-start.9 = (bf16[384,256]{1,0:T(8,128)(2,1)S(1)}, bf16[384,256]{1,0:T(8,128)(2,1)S(1)}, u32[]{:S(2)}, u32[]{:S(2)}) collective-permute-start(bf16[384,256]{1,0:T(8,128)(2,1)S(1)} %get-tuple-element.18), channel_id=1, source_target_pairs={{0,2},{8,14},{1,3},{9,15},{2,0},{10,12},{3,1},{11,13},{4,6},{12,10... | collective-permute-start | bytes 589832 | tf_op jit(solution)/shard_map/ppermute | solution.py:353
  88.1 14.3 %collective-permute-start.11 = (bf16[384,256]{1,0:T(8,128)(2,1)S(1)}, bf16[384,256]{1,0:T(8,128)(2,1)S(1)}, u32[]{:S(2)}, u32[]{:S(2)}) collective-permute-start(bf16[384,256]{1,0:T(8,128)(2,1)S(1)} %get-tuple-element.17), channel_id=1, source_target_pairs={{0,3},{8,15},{1,0},{9,12},{2,1},{10,13},{3,2},{11,14},{4,7},{12,11... | collective-permute-start | bytes 589832 | tf_op jit(solution)/shard_map/ppermute | solution.py:353
  89.1 13.5 %collective-permute-start.6 = (bf16[384,256]{1,0:T(8,128)(2,1)S(1)}, bf16[384,256]{1,0:T(8,128)(2,1)S(1)}, u32[]{:S(2)}, u32[]{:S(2)}) collective-permute-start(bf16[384,256]{1,0:T(8,128)(2,1)S(1)} %broadcast_select_fusion.refs_8_), channel_id=1, source_target_pairs={{0,8},{8,0},{1,9},{9,1},{2,10},{10,2},{3,11},{11,3},{4,12},{12,4},... | collective-permute-start | bytes 589832 | tf_op jit(solution)/shard_map/ppermute | solution.py:332
  94.0 11.3 %collective-permute-start.8 = (bf16[384,256]{1,0:T(8,128)(2,1)S(1)}, bf16[384,256]{1,0:T(8,128)(2,1)S(1)}, u32[]{:S(2)}, u32[]{:S(2)}) collective-permute-start(bf16[384,256]{1,0:T(8,128)(2,1)S(1)} %collective-permute-done.7.refs_9_), channel_id=1, source_target_pairs={{0,8},{8,0},{1,9},{9,1},{2,10},{10,2},{3,11},{11,3},{4,12},{12,4},... | collective-permute-start | bytes 589832 | tf_op jit(solution)/shard_map/ppermute | solution.py:332
  100.4 6.1 %collective-permute-start.10 = (bf16[384,256]{1,0:T(8,128)(2,1)S(1)}, bf16[384,256]{1,0:T(8,128)(2,1)S(1)}, u32[]{:S(2)}, u32[]{:S(2)}) collective-permute-start(bf16[384,256]{1,0:T(8,128)(2,1)S(1)} %collective-permute-done.9.refs_10_), channel_id=1, source_target_pairs={{0,8},{8,0},{1,9},{9,1},{2,10},{10,2},{3,11},{11,3},{4,12},{12,4},... | collective-permute-start | bytes 589832 | tf_op jit(solution)/shard_map/ppermute | solution.py:332
  102.3 6.3 %collective-permute-start.12 = (bf16[384,256]{1,0:T(8,128)(2,1)S(1)}, bf16[384,256]{1,0:T(8,128)(2,1)S(1)}, u32[]{:S(2)}, u32[]{:S(2)}) collective-permute-start(bf16[384,256]{1,0:T(8,128)(2,1)S(1)} %collective-permute-done.11.refs_11_), channel_id=1, source_target_pairs={{0,8},{8,0},{1,9},{9,1},{2,10},{10,2},{3,11},{11,3},{4,12},{12,4},... | collective-permute-start | bytes 589832 | tf_op jit(solution)/shard_map/ppermute | solution.py:332
  102.6 27.3 %copy-start.2 = (bf16[384,256]{1,0:T(8,128)(2,1)}, bf16[384,256]{1,0:T(8,128)(2,1)S(1)}, u32[]{:S(2)}) copy-start(bf16[384,256]{1,0:T(8,128)(2,1)S(1)} %collective-permute-done.6.w0.refs_12_) | copy-start | bytes 589828
  102.6 9.7 %collective-permute-start.13 = (bf16[256,256]{1,0:T(8,128)(2,1)S(1)}, bf16[256,256]{1,0:T(8,128)(2,1)S(1)}, u32[]{:S(2)}, u32[]{:S(2)}) collective-permute-start(bf16[256,256]{1,0:T(8,128)(2,1)S(1)} %shard_map.104.refs_0_.ga_ref), channel_id=1, source_target_pairs={{0,1},{1,2},{2,3},{3,0},{4,5},{5,6},{6,7},{7,4},{8,9},{9,10},{10,1... | collective-permute-start | bytes 393224 | tf_op jit(solution)/shard_map/ppermute | solution.py:343
  105.3 24.6 %copy-start.4 = (bf16[384,256]{1,0:T(8,128)(2,1)}, bf16[384,256]{1,0:T(8,128)(2,1)S(1)}, u32[]{:S(2)}) copy-start(bf16[384,256]{1,0:T(8,128)(2,1)S(1)} %collective-permute-done.8.w1.refs_13_) | copy-start | bytes 589828
  105.3 10.3 %collective-permute-start.14 = (bf16[256,256]{1,0:T(8,128)(2,1)S(1)}, bf16[256,256]{1,0:T(8,128)(2,1)S(1)}, u32[]{:S(2)}, u32[]{:S(2)}) collective-permute-start(bf16[256,256]{1,0:T(8,128)(2,1)S(1)} %shard_map.104.refs_0_.ga_ref), channel_id=1, source_target_pairs={{0,2},{1,3},{2,0},{3,1},{4,6},{5,7},{6,4},{7,5},{8,10},{9,11},{10,... | collective-permute-start | bytes 393224 | tf_op jit(solution)/shard_map/ppermute | solution.py:343
  106.5 23.5 %copy-start.6 = (bf16[384,256]{1,0:T(8,128)(2,1)}, bf16[384,256]{1,0:T(8,128)(2,1)S(1)}, u32[]{:S(2)}) copy-start(bf16[384,256]{1,0:T(8,128)(2,1)S(1)} %collective-permute-done.10.w2.refs_14_) | copy-start | bytes 589828
  106.5 27.4 %collective-permute-start.15 = (bf16[256,256]{1,0:T(8,128)(2,1)S(1)}, bf16[256,256]{1,0:T(8,128)(2,1)}, u32[]{:S(2)}, u32[]{:S(2)}) collective-permute-start(bf16[256,256]{1,0:T(8,128)(2,1)S(1)} %shard_map.104.refs_0_.ga_ref), channel_id=1, source_target_pairs={{0,3},{1,0},{2,1},{3,2},{4,7},{5,4},{6,5},{7,6},{8,11},{9,8},{10,9... | collective-permute-start | bytes 393224 | tf_op jit(solution)/shard_map/ppermute | solution.py:343
  108.6 21.4 %copy-start.8 = (bf16[384,256]{1,0:T(8,128)(2,1)}, bf16[384,256]{1,0:T(8,128)(2,1)S(1)}, u32[]{:S(2)}) copy-start(bf16[384,256]{1,0:T(8,128)(2,1)S(1)} %collective-permute-done.12.w3.refs_15_) | copy-start | bytes 589828
  108.6 25.3 %collective-permute-start.16 = (bf16[256,256]{1,0:T(8,128)(2,1)S(1)}, bf16[256,256]{1,0:T(8,128)(2,1)}, u32[]{:S(2)}, u32[]{:S(2)}) collective-permute-start(bf16[256,256]{1,0:T(8,128)(2,1)S(1)} %shard_map.104.refs_0_.ga_ref), channel_id=1, source_target_pairs={{0,4},{1,5},{2,6},{3,7},{4,0},{5,1},{6,2},{7,3},{8,12},{9,13},{10,... | collective-permute-start | bytes 393224 | tf_op jit(solution)/shard_map/ppermute | solution.py:343
  110.3 23.6 %collective-permute-start.17 = (bf16[256,256]{1,0:T(8,128)(2,1)S(1)}, bf16[256,256]{1,0:T(8,128)(2,1)}, u32[]{:S(2)}, u32[]{:S(2)}) collective-permute-start(bf16[256,256]{1,0:T(8,128)(2,1)S(1)} %shard_map.104.refs_0_.ga_ref), channel_id=1, source_target_pairs={{0,5},{1,6},{2,7},{3,4},{4,1},{5,2},{6,3},{7,0},{8,13},{9,14},{10,... | collective-permute-start | bytes 393224 | tf_op jit(solution)/shard_map/ppermute | solution.py:343
  113.0 20.9 %collective-permute-start.18 = (bf16[256,256]{1,0:T(8,128)(2,1)S(1)}, bf16[256,256]{1,0:T(8,128)(2,1)}, u32[]{:S(2)}, u32[]{:S(2)}) collective-permute-start(bf16[256,256]{1,0:T(8,128)(2,1)S(1)} %shard_map.104.refs_0_.ga_ref), channel_id=1, source_target_pairs={{0,6},{1,7},{2,4},{3,5},{4,2},{5,3},{6,0},{7,1},{8,14},{9,15},{10,... | collective-permute-start | bytes 393224 | tf_op jit(solution)/shard_map/ppermute | solution.py:343
  116.3 17.6 %collective-permute-start.19 = (bf16[256,256]{1,0:T(8,128)(2,1)S(1)}, bf16[256,256]{1,0:T(8,128)(2,1)}, u32[]{:S(2)}, u32[]{:S(2)}) collective-permute-start(bf16[256,256]{1,0:T(8,128)(2,1)S(1)} %shard_map.104.refs_0_.ga_ref), channel_id=1, source_target_pairs={{0,7},{1,4},{2,5},{3,6},{4,3},{5,0},{6,1},{7,2},{8,15},{9,12},{10,... | collective-permute-start | bytes 393224 | tf_op jit(solution)/shard_map/ppermute | solution.py:343
  120.7 19.5 %all-to-all-start.3 = ((f32[128,1,128]{2,1,0:T(1,128)}), f32[128,1,128]{2,1,0:T(1,128)}, u32[]{:S(2)}, u32[]{:S(2)}) async-start(f32[128,1,128]{2,1,0:T(1,128)} %bitcast.11), calls=%async_computation.3 | async-start | bytes 131072 | tf_op jit(solution)/shard_map/all_to_all | solution.py:357
  (18 other events, 56.1 us)

commit v5 on v4

--- a/solution.py
+++ b/solution.py
@@ -20,7 +20,6 @@
 NT = (((1,), (1,)), ((), ()))
 NN = (((1,), (0,)), ((), ()))
 C8 = ("xl", "y")
-K8 = ("xh", "z")
 ALL = ("xl", "y", "co", "xh", "z")
 
 
@@ -247,7 +246,9 @@
     )(co, x)
 
 
-def dw_kernel(xa_ref, xb_ref, ga_ref, gb_ref, out_ref, near_ref, sem):
+def dw_kernel(co_ref, xa_ref, xb_ref, ga_ref, gb_ref, out_ref, pair_ref, near_ref, sem):
+    pair_ref[co_ref[0]] = ga_ref[...]
+    pair_ref[1 - co_ref[0]] = gb_ref[...]
     g = jnp.concatenate([ga_ref[...], gb_ref[...]], axis=0)
     copies = []
     for k in range(8):
@@ -260,19 +261,22 @@
         copy.wait()
 
 
-def weight_parts(xa, xb, ga, gb):
+def weight_parts(co, xa, xb, ga, gb):
     return pl.pallas_call(
         dw_kernel,
-        out_shape=jax.ShapeDtypeStruct((8, 192, 256), jnp.bfloat16),
-        in_specs=[pl.BlockSpec(memory_space=pltpu.VMEM)] * 4,
-        out_specs=pl.BlockSpec(memory_space=pl.ANY),
+        out_shape=(
+            jax.ShapeDtypeStruct((8, 192, 256), jnp.bfloat16),
+            pltpu.VMEM((2, 256, 256), jnp.bfloat16),
+        ),
+        in_specs=[SM] + [VM] * 4,
+        out_specs=(ANY, VM),
         scratch_shapes=[
             pltpu.VMEM((8, 192, 256), jnp.bfloat16),
             pltpu.SemaphoreType.DMA((8,)),
         ],
         compiler_params=pltpu.CompilerParams(vmem_limit_bytes=20 << 20),
         name="dw",
-    )(xa, xb, ga, gb)
+    )(co, xa, xb, ga, gb)
 
 
 def grad_kernel(r_ref, grad_ref, sq_ref):
@@ -289,27 +293,27 @@
     out_ref[...] = grad_ref[...] / jnp.sqrt(total / (D * KVH * 2 * HD) + 1e-06)
 
 
-def dx_kernel(co_ref, *refs):
-    g, wa, wb, out_ref = refs[:8], refs[8:12], refs[12:16], refs[16]
-
-    def total(near, far):
-        acc = jnp.zeros((256, 384), jnp.float32)
+def dx_kernel(co_ref, g_ref, *refs):
+    ra, rb, wa, wb, out_ref = refs[:4], refs[4:8], refs[8:12], refs[12:16], refs[16]
+
+    def total(me, near, far, w_near, w_far):
+        acc = lax.dot_general(g_ref[...], w_near[0][...], NT, preferred_element_type=jnp.float32)
         for k in range(4):
-            acc += lax.dot_general(g[k][...], near[k][...], NT, preferred_element_type=jnp.float32)
-            acc += lax.dot_general(g[4 + k][...], far[k][...], NT, preferred_element_type=jnp.float32)
+            if k > 0:
+                acc += lax.dot_general(near[k][me], w_near[k][...], NT, preferred_element_type=jnp.float32)
+            acc += lax.dot_general(far[k][me], w_far[k][...], NT, preferred_element_type=jnp.float32)
         out_ref[...] = acc.astype(jnp.bfloat16)
 
     @pl.when(co_ref[0] == 0)
     def _():
-        total(wa, wb)
+        total(0, ra, rb, wa, wb)
 
     @pl.when(co_ref[0] == 1)
     def _():
-        total(wb, wa)
-
-
-def dq_kernel(a_ref, b_ref, w0, w1, w2, w3, out_ref):
-    del w0, w1, w2, w3
+        total(1, rb, ra, wb, wa)
+
+
+def dq_kernel(a_ref, b_ref, out_ref):
     for b in range(3):
         for lh in range(NLH):
             cs = slice(lh * HD, (lh + 1) * HD)
@@ -330,17 +334,6 @@
 
 def swap(a):
     return lax.ppermute(a, "co", [(0, 1), (1, 0)])
-
-
-DELTAS = [(i, j) for i in range(2) for j in range(4) if (i, j) != (0, 0)]
-
-
-def shift(a, delta):
-    perm = []
-    for i in range(2):
-        for j in range(4):
-            perm.append((4 * i + j, 4 * ((i + delta[0]) % 2) + (j + delta[1]) % 4))
-    return lax.ppermute(a, K8, perm)
 
 
 def split_shift(a, j):
@@ -381,20 +374,17 @@
     )
     dkv_r = exchange(dkv.reshape(8, 256, 256), C8)
     (g,) = call(sum_kernel, [VM], ((256, 256), bf))(vm(dkv_r))
-    dw_part = weight_parts(vm(xa), vm(xb), g, vm(swap(g)))
+    dw_part, pair = weight_parts(co1, vm(xa), vm(xb), g, vm(swap(g)))
     dw_r = exchange(dw_part, C8)
     grad, sq = call(grad_kernel, [VM], ((192, 256), f32), ((128, HD), f32))(vm(dw_r))
     parts = exchange(sq.reshape(128, 1, HD), ALL)
-    gs = [g]
-    for d in DELTAS:
-        gs.append(shift(g, d))
+    ra = [split_shift(pair, j) for j in range(4)]
+    rb = [swap(r) for r in ra]
     wb = [swap(w) for w in wa]
-    (d_x,) = call(dx_kernel, [SM] + [VM] * 16, ((256, 384), bf), near=False)(
-        co1, *map(vm, gs + wa + wb)
+    (d_x,) = call(dx_kernel, [SM] + [VM] * 17, ((256, 384), bf), near=False)(
+        co1, *map(vm, [g] + ra + rb), *wa, *map(vm, wb)
     )
-    (d_queries,) = call(dq_kernel, [VM] * 2 + [ANY] * 4, ((NL, 384, 384), bf), near=False)(
-        dqo, vm(swap(dqp)), *wb
-    )
+    (d_queries,) = call(dq_kernel, [VM] * 2, ((NL, 384, 384), bf), near=False)(dqo, vm(swap(dqp)))
     (d_w,) = call(scale_kernel, [VM] * 2, ((192, 256), f32), near=False)(vm(grad), vm(parts.reshape(128, HD)))
     return (d_queries, d_x, d_w)
 

time: 144 us -> 135 us (0.938)
  starting transfers between devices: 63.9 us -> 50.8 us
  waiting for transfers between devices: 19.3 us -> 26 us
  local copies, waits for them, and re-layouts: 10.8 us -> 7.58 us
    ppermute x7 -> x0, starting transfers between devices: 14.3 us -> none  [shift(): return lax.ppermute(a, K8, perm)]
    ppermute x4 -> x8, waiting for transfers between devices: 0.01 us -> 5.78 us  [split_shift(): return lax.ppermute(a, ('co', 'xh', 'z'), perm)]
    ppermute x4 -> x8, starting transfers between devices: 7.86 us -> 11.5 us  [split_shift(): return lax.ppermute(a, ('co', 'xh', 'z'), perm)]
    all_to_all x4, waiting for transfers between devices: 16.1 us -> 18.3 us  [exchange(): return lax.all_to_all(a, axes, 0, 0)]
    unnamed x48 -> x50, local copies, waits for them, and re-layouts: 8.75 us -> 6.56 us
    ppermute x11 -> x15, starting transfers between devices: 15.3 us -> 13.9 us  [swap(): return lax.ppermute(a, 'co', [(0, 1), (1, 0)])]
    ppermute x11 -> x15, waiting for transfers between devices: 3.14 us -> 1.83 us  [swap(): return lax.ppermute(a, 'co', [(0, 1), (1, 0)])]
  transfers between devices with their start and end apart: 26 -> 27, of which waited for: 4 -> 4; matrix products, arithmetic and copies ran while one was open for 2% -> 2% of each run, Pallas kernels for 8% -> 10%
where the time goes in v5:
time: 135 us; the launch traced here: 134 us
  starting transfers between devices  50.8 us (38%)
  Pallas kernels  47.4 us (35%)
  waiting for transfers between devices  26 us (19%)
  local copies, waits for them, and re-layouts  7.58 us (6%)
  between operations  1.58 us (1%)
    pallas_call x1, Pallas kernels, attn(): pl.pallas_call(functools.partial(attn_kernel, groups, unroll, late), out_...  30.3 us
    all_to_all x4, starting transfers between devices, exchange(): return lax.all_to_all(a, axes, 0, 0)  25.4 us
    all_to_all x4, waiting for transfers between devices, exchange(): return lax.all_to_all(a, axes, 0, 0)  18.3 us
    ppermute x15, starting transfers between devices, swap(): return lax.ppermute(a, 'co', [(0, 1), (1, 0)])  13.9 us
    ppermute x8, starting transfers between devices, split_shift(): return lax.ppermute(a, ('co', 'xh', 'z'), perm)  11.5 us
    unnamed x50, local copies, waits for them, and re-layouts  6.56 us
    ppermute x8, waiting for transfers between devices, split_shift(): return lax.ppermute(a, ('co', 'xh', 'z'), perm)  5.78 us
    pallas_call x1, Pallas kernels, project(): pl.pallas_call(kv_kernel, grid=(steps,), out_shape=jax.ShapeDtypeStruct((...  3.35 us
  transfers between devices with their start and end apart: 27, of which 4 were waited for; matrix products, arithmetic and copies ran while one was open for 2% of the time, Pallas kernels for 10%

profile of v5, /device:TPU:0, one launch (start us, length us, event | category | flops | bytes accessed | tf_op | source)
XLA Modules:
  0.0 134.3 jit_solution(8943197078085488148)
XLA Ops:
  0.6 3.3 %kv.1 = bf16[8,256,256]{2,1,0:T(8,128)(2,1)} custom-call(bf16[256,3072]{1,0:T(8,128)(2,1)} %x_ref.3, bf16[3072,256]{1,0:T(8,128)(2,1)} %w_ref.1), custom_call_target="tpu_custom_call" | custom-call | tf_op jit(solution)/shard_map/kv/pallas_call | solution.py:207
  4.0 5.7 %all-to-all-start = ((bf16[8,256,256]{2,1,0:T(8,128)(2,1)}), bf16[8,256,256]{2,1,0:T(8,128)(2,1)S(1)}, u32[]{:S(2)}, u32[]{:S(2)}) async-start(bf16[8,256,256]{2,1,0:T(8,128)(2,1)} %kv.1), calls=%async_computation | async-start | bytes 2097152 | tf_op jit(solution)/shard_map/all_to_all | solution.py:350
  11.8 1.8 %collective-permute-done.ints_p = s32[128]{0:T(128)S(1)} collective-permute-done((s32[128]{0:T(128)S(1)}, s32[128]{0:T(128)S(1)}, u32[]{:S(2)}, u32[]{:S(2)}) %collective-permute-start) | collective-permute-done | bytes 544 | tf_op jit(solution)/shard_map/ppermute | solution.py:336
  13.6 10.9 %all-to-all-done = bf16[8,256,256]{2,1,0:T(8,128)(2,1)S(1)} async-done(((bf16[8,256,256]{2,1,0:T(8,128)(2,1)}), bf16[8,256,256]{2,1,0:T(8,128)(2,1)S(1)}, u32[]{:S(2)}, u32[]{:S(2)}) %all-to-all-start) | async-done | bytes 1048608 | tf_op jit(solution)/shard_map/all_to_all | solution.py:350
  24.5 30.3 %attn.1 = (bf16[16,128,256]{2,1,0:T(8,128)(2,1)}, f32[3,128,1152]{2,1,0:T(8,128)}, bf16[3,128,1152]{2,1,0:T(8,128)(2,1)}) custom-call(s32[128]{0:T(128)} %copy-done.23, s32[128]{0:T(128)} %copy-done.24, s32[1]{0:T(128)} %bitcast.co_ref, f32[3,18,128]{2,1,0:T(8,128)S(1)} %copy.17.small_o, f32[3,18,128]{2,1,0:T(8,128)S(1)} %collective-permute-done.1.small_p, ...), custom_call_target="tpu_custom_call" | custom-call | tf_op jit(solution)/shard_map/attn/pallas_call | solution.py:156
  54.8 8.1 %all-to-all-start.1 = ((bf16[8,256,256]{2,1,0:T(8,128)(2,1)}), bf16[8,256,256]{2,1,0:T(8,128)(2,1)S(1)}, u32[]{:S(2)}, u32[]{:S(2)}) async-start(bf16[8,256,256]{2,1,0:T(8,128)(2,1)} %bitcast.23), calls=%async_computation.1 | async-start | bytes 2097152 | tf_op jit(solution)/shard_map/all_to_all | solution.py:350
  62.8 3.1 %xt.1 = (bf16[8,192,256]{2,1,0:T(8,128)(2,1)}, bf16[8,192,256]{2,1,0:T(8,128)(2,1)}) custom-call(s32[1]{0:T(128)} %bitcast.co_ref, bf16[256,3072]{1,0:T(8,128)(2,1)} %x_ref.3), custom_call_target="tpu_custom_call" | custom-call | tf_op jit(solution)/shard_map/xt/pallas_call | solution.py:239
  65.9 0.9 dynamic-slice_bitcast_fusion
  67.5 7.5 %all-to-all-done.1.r_ref = bf16[8,256,256]{2,1,0:T(8,128)(2,1)S(1)} async-done(((bf16[8,256,256]{2,1,0:T(8,128)(2,1)}), bf16[8,256,256]{2,1,0:T(8,128)(2,1)S(1)}, u32[]{:S(2)}, u32[]{:S(2)}) %all-to-all-start.1) | async-done | bytes 1048608 | tf_op jit(solution)/shard_map/all_to_all | solution.py:350
  75.7 1.9 %collective-permute-start.16 = (bf16[384,256]{1,0:T(8,128)(2,1)}, bf16[384,256]{1,0:T(8,128)(2,1)S(1)}, u32[]{:S(2)}, u32[]{:S(2)}) collective-permute-start(bf16[384,256]{1,0:T(8,128)(2,1)} %get-tuple-element.23), channel_id=1, source_target_pairs={{0,1},{8,13},{1,2},{9,14},{2,3},{10,15},{3,0},{11,12},{4,5},{12,9}... | collective-permute-start | bytes 589832 | tf_op jit(solution)/shard_map/ppermute | solution.py:346
  77.6 3.6 %collective-permute-start.17 = (bf16[384,256]{1,0:T(8,128)(2,1)}, bf16[384,256]{1,0:T(8,128)(2,1)S(1)}, u32[]{:S(2)}, u32[]{:S(2)}) collective-permute-start(bf16[384,256]{1,0:T(8,128)(2,1)} %get-tuple-element.22), channel_id=1, source_target_pairs={{0,2},{8,14},{1,3},{9,15},{2,0},{10,12},{3,1},{11,13},{4,6},{12,10... | collective-permute-start | bytes 589832 | tf_op jit(solution)/shard_map/ppermute | solution.py:346
  81.2 1.0 collective-permute-start.18
  82.2 3.2 %dw.1 = (bf16[8,192,256]{2,1,0:T(8,128)(2,1)}, bf16[2,256,256]{2,1,0:T(8,128)(2,1)}) custom-call(s32[1]{0:T(128)} %bitcast.co_ref, bf16[8,192,256]{2,1,0:T(8,128)(2,1)S(1)} %copy-done, bf16[8,192,256]{2,1,0:T(8,128)(2,1)} %collective-permute-done.5.xb_ref, bf16[256,256]{1,0:T(8,128)(2,1)S(1)} %shard_map.104.ga_ref.g_ref, ...), custom_call_target="tpu_custom_call" | custom-call | tf_op jit(solution)/shard_map/dw/pallas_call | solution.py:265
  85.4 3.6 %all-to-all-start.2 = ((bf16[8,192,256]{2,1,0:T(8,128)(2,1)}), bf16[8,192,256]{2,1,0:T(8,128)(2,1)S(1)}, u32[]{:S(2)}, u32[]{:S(2)}) async-start(bf16[8,192,256]{2,1,0:T(8,128)(2,1)} %get-tuple-element.18), calls=%async_computation.2 | async-start | bytes 1572864 | tf_op jit(solution)/shard_map/all_to_all | solution.py:350
  89.1 1.0 broadcast_select_fusion.refs_8_
  90.1 3.0 %collective-permute-start.19 = (bf16[384,256]{1,0:T(8,128)(2,1)S(1)}, bf16[384,256]{1,0:T(8,128)(2,1)S(1)}, u32[]{:S(2)}, u32[]{:S(2)}) collective-permute-start(bf16[384,256]{1,0:T(8,128)(2,1)S(1)} %broadcast_select_fusion.refs_8_), channel_id=1, source_target_pairs={{0,8},{8,0},{1,9},{9,1},{2,10},{10,2},{3,11},{11,3},{4,12},{12,4},... | collective-permute-start | bytes 589832 | tf_op jit(solution)/shard_map/ppermute | solution.py:336
  95.0 1.0 collective-permute-start.8
  96.0 0.7 copy-done.9
  97.4 2.7 %collective-permute-start.10 = (bf16[2,256,256]{2,1,0:T(8,128)(2,1)}, bf16[2,256,256]{2,1,0:T(8,128)(2,1)S(1)}, u32[]{:S(2)}, u32[]{:S(2)}) collective-permute-start(bf16[2,256,256]{2,1,0:T(8,128)(2,1)} %get-tuple-element.17), channel_id=1, source_target_pairs={{0,3},{8,15},{1,0},{9,12},{2,1},{10,13},{3,2},{11,14},{4,7},{12,11... | collective-permute-start | bytes 786440 | tf_op jit(solution)/shard_map/ppermute | solution.py:346
  100.0 5.4 %collective-permute-start.11 = (bf16[2,256,256]{2,1,0:T(8,128)(2,1)S(1)}, bf16[2,256,256]{2,1,0:T(8,128)(2,1)S(1)}, u32[]{:S(2)}, u32[]{:S(2)}) collective-permute-start(bf16[2,256,256]{2,1,0:T(8,128)(2,1)S(1)} %collective-permute-done.7.refs_0_), channel_id=1, source_target_pairs={{0,8},{8,0},{1,9},{9,1},{2,10},{10,2},{3,11},{11,3},{4,12},{12,4},... | collective-permute-start | bytes 786440 | tf_op jit(solution)/shard_map/ppermute | solution.py:336
  105.4 5.8 %collective-permute-done.8.refs_1_ = bf16[2,256,256]{2,1,0:T(8,128)(2,1)S(1)} collective-permute-done((bf16[2,256,256]{2,1,0:T(8,128)(2,1)}, bf16[2,256,256]{2,1,0:T(8,128)(2,1)S(1)}, u32[]{:S(2)}, u32[]{:S(2)}) %collective-permute-start.8) | collective-permute-done | bytes 262176 | tf_op jit(solution)/shard_map/ppermute | solution.py:346
  111.7 2.6 %collective-permute-start.14 = (bf16[2,256,256]{2,1,0:T(8,128)(2,1)S(1)}, bf16[2,256,256]{2,1,0:T(8,128)(2,1)}, u32[]{:S(2)}, u32[]{:S(2)}) collective-permute-start(bf16[2,256,256]{2,1,0:T(8,128)(2,1)S(1)} %collective-permute-done.10.refs_3_), channel_id=1, source_target_pairs={{0,8},{8,0},{1,9},{9,1},{2,10},{10,2},{3,11},{11,3},{4,12},{12,4},... | collective-permute-start | bytes 786440 | tf_op jit(solution)/shard_map/ppermute | solution.py:336
  114.4 0.9 shard_map.106
  115.3 8.0 %all-to-all-start.3 = ((f32[128,1,128]{2,1,0:T(1,128)}), f32[128,1,128]{2,1,0:T(1,128)S(1)}, u32[]{:S(2)}, u32[]{:S(2)}) async-start(f32[128,1,128]{2,1,0:T(1,128)} %bitcast.11), calls=%async_computation.3 | async-start | bytes 131072 | tf_op jit(solution)/shard_map/all_to_all | solution.py:350
  123.3 2.8 %shard_map.103 = bf16[3,384,384]{2,1,0:T(8,128)(2,1)} custom-call(f32[3,128,1152]{2,1,0:T(8,128)} %get-tuple-element.12.a_ref, bf16[3,128,1152]{2,1,0:T(8,128)(2,1)S(1)} %collective-permute-done.4.b_ref), custom_call_target="tpu_custom_call" | custom-call | tf_op jit(solution)/shard_map/pallas_call | solution.py:387
  126.1 0.7 copy-done.5
  126.8 0.9 copy-done.2
  127.8 0.9 copy-done.4
  128.7 0.9 copy-done.6
  129.7 0.9 copy-done.12
  130.6 2.9 %shard_map.105 = bf16[256,384]{1,0:T(8,128)(2,1)} custom-call(s32[1]{0:T(128)} %bitcast.co_ref, bf16[256,256]{1,0:T(8,128)(2,1)S(1)} %shard_map.104.ga_ref.g_ref, bf16[2,256,256]{2,1,0:T(8,128)(2,1)S(1)} %collective-permute-done.7.refs_0_, bf16[2,256,256]{2,1,0:T(8,128)(2,1)S(1)} %collective-permute-done.8.refs_1_, bf16[2,256,256]{2,1,0:T(8,128)(2,1)S(1)} %copy-done.2, ...), custom_call_target="tpu_custom_call" | custom-call | tf_op jit(solution)/shard_map/pallas_call | solution.py:384
  133.5 0.8 shard_map.107
  (90 shorter events, 6.0 us)
Async XLA Ops:
  4.0 20.5 %all-to-all-start = ((bf16[8,256,256]{2,1,0:T(8,128)(2,1)}), bf16[8,256,256]{2,1,0:T(8,128)(2,1)S(1)}, u32[]{:S(2)}, u32[]{:S(2)}) async-start(bf16[8,256,256]{2,1,0:T(8,128)(2,1)} %kv.1), calls=%async_computation | async-start | bytes 2097152 | tf_op jit(solution)/shard_map/all_to_all | solution.py:350
  9.7 3.9 %collective-permute-start.2 = (bf16[3,384,384]{2,1,0:T(8,128)(2,1)S(1)}, bf16[3,384,384]{2,1,0:T(8,128)(2,1)}, u32[]{:S(2)}, u32[]{:S(2)}) collective-permute-start(bf16[3,384,384]{2,1,0:T(8,128)(2,1)S(1)} %copy-done.16), channel_id=1, source_target_pairs={{0,8},{8,0},{1,9},{9,1},{2,10},{10,2},{3,11},{11,3},{4,12},{12,4},... | collective-permute-start | bytes 2654216 | tf_op jit(solution)/shard_map/ppermute | solution.py:336
  9.7 3.8 %collective-permute-start.3 = (bf16[3,384,384]{2,1,0:T(8,128)(2,1)}, bf16[3,384,384]{2,1,0:T(8,128)(2,1)}, u32[]{:S(2)}, u32[]{:S(2)}) collective-permute-start(bf16[3,384,384]{2,1,0:T(8,128)(2,1)} %oo.1), channel_id=1, source_target_pairs={{0,8},{8,0},{1,9},{9,1},{2,10},{10,2},{3,11},{11,3},{4,12},{12,4},... | collective-permute-start | bytes 2654216 | tf_op jit(solution)/shard_map/ppermute | solution.py:336
  10.3 3.2 %collective-permute-start.1 = (f32[3,18,128]{2,1,0:T(8,128)S(1)}, f32[3,18,128]{2,1,0:T(8,128)S(1)}, u32[]{:S(2)}, u32[]{:S(2)}) collective-permute-start(f32[3,18,128]{2,1,0:T(8,128)S(1)} %copy.17.small_o), channel_id=1, source_target_pairs={{0,8},{8,0},{1,9},{9,1},{2,10},{10,2},{3,11},{11,3},{4,12},{12,4},... | collective-permute-start | bytes 82952 | tf_op jit(solution)/shard_map/ppermute | solution.py:336
  11.3 13.1 %copy-start.23 = (s32[128]{0:T(128)}, s32[128]{0:T(128)S(1)}, u32[]{:S(2)}) copy-start(s32[128]{0:T(128)S(1)} %pad_add_fusion.ints_o) | copy-start | bytes 1540
  11.3 2.2 %collective-permute-start = (s32[128]{0:T(128)S(1)}, s32[128]{0:T(128)S(1)}, u32[]{:S(2)}, u32[]{:S(2)}) collective-permute-start(s32[128]{0:T(128)S(1)} %pad_add_fusion.ints_o), channel_id=1, source_target_pairs={{0,8},{8,0},{1,9},{9,1},{2,10},{10,2},{3,11},{11,3},{4,12},{12,4},... | collective-permute-start | bytes 1544 | tf_op jit(solution)/shard_map/ppermute | solution.py:336
  54.8 20.2 %all-to-all-start.1 = ((bf16[8,256,256]{2,1,0:T(8,128)(2,1)}), bf16[8,256,256]{2,1,0:T(8,128)(2,1)S(1)}, u32[]{:S(2)}, u32[]{:S(2)}) async-start(bf16[8,256,256]{2,1,0:T(8,128)(2,1)} %bitcast.23), calls=%async_computation.1 | async-start | bytes 2097152 | tf_op jit(solution)/shard_map/all_to_all | solution.py:350
  65.9 16.3 %copy-start = (bf16[8,192,256]{2,1,0:T(8,128)(2,1)S(1)}, bf16[8,192,256]{2,1,0:T(8,128)(2,1)}, u32[]{:S(2)}) copy-start(bf16[8,192,256]{2,1,0:T(8,128)(2,1)} %get-tuple-element.15.xa_ref) | copy-start | bytes 2359300
  65.9 11.7 %collective-permute-start.5 = (bf16[8,192,256]{2,1,0:T(8,128)(2,1)}, bf16[8,192,256]{2,1,0:T(8,128)(2,1)}, u32[]{:S(2)}, u32[]{:S(2)}) collective-permute-start(bf16[8,192,256]{2,1,0:T(8,128)(2,1)} %get-tuple-element.16), channel_id=1, source_target_pairs={{0,8},{8,0},{1,9},{9,1},{2,10},{10,2},{3,11},{11,3},{4,12},{12,4},... | collective-permute-start | bytes 2359304 | tf_op jit(solution)/shard_map/ppermute | solution.py:336
  66.8 22.3 %collective-permute-start.15 = (bf16[384,256]{1,0:T(8,128)(2,1)}, bf16[384,256]{1,0:T(8,128)(2,1)S(1)}, u32[]{:S(2)}, u32[]{:S(2)}) collective-permute-start(bf16[384,256]{1,0:T(8,128)(2,1)} %get-tuple-element.24), channel_id=1, source_target_pairs={{8,12},{9,13},{10,14},{11,15},{12,8},{13,9},{14,10},{15,11},{24,28... | collective-permute-start | bytes 589832 | tf_op jit(solution)/shard_map/ppermute | solution.py:346
  75.1 6.1 %collective-permute-start.6 = (bf16[256,256]{1,0:T(8,128)(2,1)S(1)}, bf16[256,256]{1,0:T(8,128)(2,1)S(1)}, u32[]{:S(2)}, u32[]{:S(2)}) collective-permute-start(bf16[256,256]{1,0:T(8,128)(2,1)S(1)} %shard_map.104.ga_ref.g_ref), channel_id=1, source_target_pairs={{0,8},{8,0},{1,9},{9,1},{2,10},{10,2},{3,11},{11,3},{4,12},{12,4},... | collective-permute-start | bytes 393224 | tf_op jit(solution)/shard_map/ppermute | solution.py:336
  75.2 39.1 %collective-permute-start.4 = (bf16[3,128,1152]{2,1,0:T(8,128)(2,1)}, bf16[3,128,1152]{2,1,0:T(8,128)(2,1)S(1)}, u32[]{:S(2)}, u32[]{:S(2)}) collective-permute-start(bf16[3,128,1152]{2,1,0:T(8,128)(2,1)} %get-tuple-element.13), channel_id=1, source_target_pairs={{0,8},{8,0},{1,9},{9,1},{2,10},{10,2},{3,11},{11,3},{4,12},{12,4},... | collective-permute-start | bytes 2654216 | tf_op jit(solution)/shard_map/ppermute | solution.py:336
  75.7 17.4 %collective-permute-start.16 = (bf16[384,256]{1,0:T(8,128)(2,1)}, bf16[384,256]{1,0:T(8,128)(2,1)S(1)}, u32[]{:S(2)}, u32[]{:S(2)}) collective-permute-start(bf16[384,256]{1,0:T(8,128)(2,1)} %get-tuple-element.23), channel_id=1, source_target_pairs={{0,1},{8,13},{1,2},{9,14},{2,3},{10,15},{3,0},{11,12},{4,5},{12,9}... | collective-permute-start | bytes 589832 | tf_op jit(solution)/shard_map/ppermute | solution.py:346
  77.6 15.6 %collective-permute-start.17 = (bf16[384,256]{1,0:T(8,128)(2,1)}, bf16[384,256]{1,0:T(8,128)(2,1)S(1)}, u32[]{:S(2)}, u32[]{:S(2)}) collective-permute-start(bf16[384,256]{1,0:T(8,128)(2,1)} %get-tuple-element.22), channel_id=1, source_target_pairs={{0,2},{8,14},{1,3},{9,15},{2,0},{10,12},{3,1},{11,13},{4,6},{12,10... | collective-permute-start | bytes 589832 | tf_op jit(solution)/shard_map/ppermute | solution.py:346
  81.2 12.4 %collective-permute-start.18 = (bf16[384,256]{1,0:T(8,128)(2,1)}, bf16[384,256]{1,0:T(8,128)(2,1)}, u32[]{:S(2)}, u32[]{:S(2)}) collective-permute-start(bf16[384,256]{1,0:T(8,128)(2,1)} %get-tuple-element.21), channel_id=1, source_target_pairs={{0,3},{8,15},{1,0},{9,12},{2,1},{10,13},{3,2},{11,14},{4,7},{12,11... | collective-permute-start | bytes 589832 | tf_op jit(solution)/shard_map/ppermute | solution.py:346
  85.4 29.0 %all-to-all-start.2 = ((bf16[8,192,256]{2,1,0:T(8,128)(2,1)}), bf16[8,192,256]{2,1,0:T(8,128)(2,1)S(1)}, u32[]{:S(2)}, u32[]{:S(2)}) async-start(bf16[8,192,256]{2,1,0:T(8,128)(2,1)} %get-tuple-element.18), calls=%async_computation.2 | async-start | bytes 1572864 | tf_op jit(solution)/shard_map/all_to_all | solution.py:350
  90.0 24.3 %copy-start.17 = (bf16[384,256]{1,0:T(8,128)(2,1)}, bf16[384,256]{1,0:T(8,128)(2,1)S(1)}, u32[]{:S(2)}) copy-start(bf16[384,256]{1,0:T(8,128)(2,1)S(1)} %broadcast_select_fusion.refs_8_) | copy-start | bytes 589828
  90.1 4.2 %collective-permute-start.19 = (bf16[384,256]{1,0:T(8,128)(2,1)S(1)}, bf16[384,256]{1,0:T(8,128)(2,1)S(1)}, u32[]{:S(2)}, u32[]{:S(2)}) collective-permute-start(bf16[384,256]{1,0:T(8,128)(2,1)S(1)} %broadcast_select_fusion.refs_8_), channel_id=1, source_target_pairs={{0,8},{8,0},{1,9},{9,1},{2,10},{10,2},{3,11},{11,3},{4,12},{12,4},... | collective-permute-start | bytes 589832 | tf_op jit(solution)/shard_map/ppermute | solution.py:336
  93.1 2.9 %collective-permute-start.20 = (bf16[384,256]{1,0:T(8,128)(2,1)S(1)}, bf16[384,256]{1,0:T(8,128)(2,1)S(1)}, u32[]{:S(2)}, u32[]{:S(2)}) collective-permute-start(bf16[384,256]{1,0:T(8,128)(2,1)S(1)} %collective-permute-done.16.refs_9_), channel_id=1, source_target_pairs={{0,8},{8,0},{1,9},{9,1},{2,10},{10,2},{3,11},{11,3},{4,12},{12,4},... | collective-permute-start | bytes 589832 | tf_op jit(solution)/shard_map/ppermute | solution.py:336
  93.2 3.5 %collective-permute-start.21 = (bf16[384,256]{1,0:T(8,128)(2,1)S(1)}, bf16[384,256]{1,0:T(8,128)(2,1)S(1)}, u32[]{:S(2)}, u32[]{:S(2)}) collective-permute-start(bf16[384,256]{1,0:T(8,128)(2,1)S(1)} %collective-permute-done.17.refs_10_), channel_id=1, source_target_pairs={{0,8},{8,0},{1,9},{9,1},{2,10},{10,2},{3,11},{11,3},{4,12},{12,4},... | collective-permute-start | bytes 589832 | tf_op jit(solution)/shard_map/ppermute | solution.py:336
  93.6 6.4 %collective-permute-start.7 = (bf16[2,256,256]{2,1,0:T(8,128)(2,1)}, bf16[2,256,256]{2,1,0:T(8,128)(2,1)S(1)}, u32[]{:S(2)}, u32[]{:S(2)}) collective-permute-start(bf16[2,256,256]{2,1,0:T(8,128)(2,1)} %get-tuple-element.17), channel_id=1, source_target_pairs={{8,12},{9,13},{10,14},{11,15},{12,8},{13,9},{14,10},{15,11},{24,28... | collective-permute-start | bytes 786440 | tf_op jit(solution)/shard_map/ppermute | solution.py:346
  95.0 16.2 %collective-permute-start.8 = (bf16[2,256,256]{2,1,0:T(8,128)(2,1)}, bf16[2,256,256]{2,1,0:T(8,128)(2,1)S(1)}, u32[]{:S(2)}, u32[]{:S(2)}) collective-permute-start(bf16[2,256,256]{2,1,0:T(8,128)(2,1)} %get-tuple-element.17), channel_id=1, source_target_pairs={{0,1},{8,13},{1,2},{9,14},{2,3},{10,15},{3,0},{11,12},{4,5},{12,9}... | collective-permute-start | bytes 786440 | tf_op jit(solution)/shard_map/ppermute | solution.py:346
  96.7 14.5 %collective-permute-start.9 = (bf16[2,256,256]{2,1,0:T(8,128)(2,1)}, bf16[2,256,256]{2,1,0:T(8,128)(2,1)S(1)}, u32[]{:S(2)}, u32[]{:S(2)}) collective-permute-start(bf16[2,256,256]{2,1,0:T(8,128)(2,1)} %get-tuple-element.17), channel_id=1, source_target_pairs={{0,2},{8,14},{1,3},{9,15},{2,0},{10,12},{3,1},{11,13},{4,6},{12,10... | collective-permute-start | bytes 786440 | tf_op jit(solution)/shard_map/ppermute | solution.py:346
  97.4 14.4 %collective-permute-start.10 = (bf16[2,256,256]{2,1,0:T(8,128)(2,1)}, bf16[2,256,256]{2,1,0:T(8,128)(2,1)S(1)}, u32[]{:S(2)}, u32[]{:S(2)}) collective-permute-start(bf16[2,256,256]{2,1,0:T(8,128)(2,1)} %get-tuple-element.17), channel_id=1, source_target_pairs={{0,3},{8,15},{1,0},{9,12},{2,1},{10,13},{3,2},{11,14},{4,7},{12,11... | collective-permute-start | bytes 786440 | tf_op jit(solution)/shard_map/ppermute | solution.py:346
  100.0 26.0 %collective-permute-start.11 = (bf16[2,256,256]{2,1,0:T(8,128)(2,1)S(1)}, bf16[2,256,256]{2,1,0:T(8,128)(2,1)S(1)}, u32[]{:S(2)}, u32[]{:S(2)}) collective-permute-start(bf16[2,256,256]{2,1,0:T(8,128)(2,1)S(1)} %collective-permute-done.7.refs_0_), channel_id=1, source_target_pairs={{0,8},{8,0},{1,9},{9,1},{2,10},{10,2},{3,11},{11,3},{4,12},{12,4},... | collective-permute-start | bytes 786440 | tf_op jit(solution)/shard_map/ppermute | solution.py:336
  111.2 15.6 %collective-permute-start.12 = (bf16[2,256,256]{2,1,0:T(8,128)(2,1)S(1)}, bf16[2,256,256]{2,1,0:T(8,128)(2,1)}, u32[]{:S(2)}, u32[]{:S(2)}) collective-permute-start(bf16[2,256,256]{2,1,0:T(8,128)(2,1)S(1)} %collective-permute-done.8.refs_1_), channel_id=1, source_target_pairs={{0,8},{8,0},{1,9},{9,1},{2,10},{10,2},{3,11},{11,3},{4,12},{12,4},... | collective-permute-start | bytes 786440 | tf_op jit(solution)/shard_map/ppermute | solution.py:336
  111.2 14.8 %copy-start.1 = (bf16[2,256,256]{2,1,0:T(8,128)(2,1)}, bf16[2,256,256]{2,1,0:T(8,128)(2,1)S(1)}, u32[]{:S(2)}) copy-start(bf16[2,256,256]{2,1,0:T(8,128)(2,1)S(1)} %collective-permute-done.9.refs_2_) | copy-start | bytes 786436
  111.2 15.6 %collective-permute-start.13 = (bf16[2,256,256]{2,1,0:T(8,128)(2,1)S(1)}, bf16[2,256,256]{2,1,0:T(8,128)(2,1)}, u32[]{:S(2)}, u32[]{:S(2)}) collective-permute-start(bf16[2,256,256]{2,1,0:T(8,128)(2,1)S(1)} %collective-permute-done.9.refs_2_), channel_id=1, source_target_pairs={{0,8},{8,0},{1,9},{9,1},{2,10},{10,2},{3,11},{11,3},{4,12},{12,4},... | collective-permute-start | bytes 786440 | tf_op jit(solution)/shard_map/ppermute | solution.py:336
  111.7 14.3 %copy-start.3 = (bf16[2,256,256]{2,1,0:T(8,128)(2,1)}, bf16[2,256,256]{2,1,0:T(8,128)(2,1)S(1)}, u32[]{:S(2)}) copy-start(bf16[2,256,256]{2,1,0:T(8,128)(2,1)S(1)} %collective-permute-done.10.refs_3_) | copy-start | bytes 786436
  111.7 15.1 %collective-permute-start.14 = (bf16[2,256,256]{2,1,0:T(8,128)(2,1)S(1)}, bf16[2,256,256]{2,1,0:T(8,128)(2,1)}, u32[]{:S(2)}, u32[]{:S(2)}) collective-permute-start(bf16[2,256,256]{2,1,0:T(8,128)(2,1)S(1)} %collective-permute-done.10.refs_3_), channel_id=1, source_target_pairs={{0,8},{8,0},{1,9},{9,1},{2,10},{10,2},{3,11},{11,3},{4,12},{12,4},... | collective-permute-start | bytes 786440 | tf_op jit(solution)/shard_map/ppermute | solution.py:336
  114.3 11.7 %collective-permute-start.22 = (bf16[384,256]{1,0:T(8,128)(2,1)}, bf16[384,256]{1,0:T(8,128)(2,1)}, u32[]{:S(2)}, u32[]{:S(2)}) collective-permute-start(bf16[384,256]{1,0:T(8,128)(2,1)} %collective-permute-done.18.refs_11_), channel_id=1, source_target_pairs={{0,8},{8,0},{1,9},{9,1},{2,10},{10,2},{3,11},{11,3},{4,12},{12,4},... | collective-permute-start | bytes 589832 | tf_op jit(solution)/shard_map/ppermute | solution.py:336
  115.3 18.2 %all-to-all-start.3 = ((f32[128,1,128]{2,1,0:T(1,128)}), f32[128,1,128]{2,1,0:T(1,128)S(1)}, u32[]{:S(2)}, u32[]{:S(2)}) async-start(f32[128,1,128]{2,1,0:T(1,128)} %bitcast.11), calls=%async_computation.3 | async-start | bytes 131072 | tf_op jit(solution)/shard_map/all_to_all | solution.py:350
  (20 other events, 81.8 us)

commit v6 on v5

--- a/solution.py
+++ b/solution.py
@@ -24,7 +24,7 @@
 
 
 def attn_kernel(groups, unroll, late, ints_o, ints_p, co_ref, small_o, small_p, kv_ref, qo, qp, oo, op, dkv_ref, dqo_ref, dqp_ref,
-                q_s, o_s, kT_s, acc_s, dq_s, sm_s, bias_s, lst, one_s, sem):
+                q_s, o_s, kT_s, acc_s, dq_s, sm_s, bias_s, dkv_s, dqp_s, lst, one_s, sem, out_sem):
     f32 = jnp.float32
     bf = jnp.bfloat16
     copies = [
@@ -140,13 +140,26 @@
 
     lax.fori_loop(0, (items + unroll - 1) // unroll, trip, 0)
     scale = f32(HD ** (-0.5))
-    dqo_ref[...] = dq_s[0:3] * scale
-    dqp_ref[...] = (dq_s[3:6] * scale).astype(bf)
-    dkv_ref[:, :, :HD] = (acc_s[:, :, :HD] * scale).astype(bf)
-    dkv_ref[:, :, HD:] = acc_s[:, :, HD:].astype(bf)
-
-
-def attn(ints_o, ints_p, co, small_o, small_p, kv, qo, qp, oo, op, groups=((0, 1), (2, 3), (4, 5), (6, 7), (8,)), unroll=2, late=False, near=False):
+
+    def send(src, dst, k):
+        copy = pltpu.make_async_copy(src, dst, out_sem.at[k])
+        copy.start()
+        return copy
+
+    sent = [send(dq_s.at[pl.ds(0, 3)], dqo_ref, 0)]
+    half = KB // 2
+    for k in range(2):
+        part = slice(k * half, (k + 1) * half)
+        dkv_s[part, :, :HD] = (acc_s[part, :, :HD] * scale).astype(bf)
+        dkv_s[part, :, HD:] = acc_s[part, :, HD:].astype(bf)
+        sent.append(send(dkv_s.at[pl.ds(k * half, half)], dkv_ref.at[pl.ds(k * half, half)], 1 + k))
+    dqp_s[...] = (dq_s[3:6] * scale).astype(bf)
+    sent.append(send(dqp_s, dqp_ref, 3))
+    for copy in sent:
+        copy.wait()
+
+
+def attn(ints_o, ints_p, co, small_o, small_p, kv, qo, qp, oo, op, groups=((0, 1), (2, 3), (4, 5), (6, 7), (8,)), unroll=4, late=False, near=False):
     f32 = jnp.float32
     bf = jnp.bfloat16
     smem = pl.BlockSpec(memory_space=pltpu.SMEM)
@@ -161,7 +174,7 @@
             kind((3, HD, NLH * HD), bf),
         ),
         in_specs=[smem] * 3 + [vmem] * 3 + [anym] * 4,
-        out_specs=(vmem, vmem, vmem),
+        out_specs=(anym, anym, anym),
         scratch_shapes=[
             pltpu.VMEM((2, NL, 384, 384), bf),
             pltpu.VMEM((2, NL, 384, 384), bf),
@@ -170,8 +183,11 @@
             pltpu.VMEM((QB, HD, NLH * HD), f32),
             pltpu.VMEM((QB, 2 * NLH, HD), f32),
             pltpu.VMEM((unroll, 2 * HD, HD), f32),
+            pltpu.VMEM((KB, HD, 2 * HD), bf),
+            pltpu.VMEM((3, HD, NLH * HD), bf),
             pltpu.SMEM((QB * KB + 2 * unroll + 2,), jnp.int32),
             pltpu.SMEM((QB * KB // 2 + unroll + 1,), jnp.int32),
+            pltpu.SemaphoreType.DMA((4,)),
             pltpu.SemaphoreType.DMA((4,)),
         ],
         name="attn",
@@ -317,7 +333,7 @@
     for b in range(3):
         for lh in range(NLH):
             cs = slice(lh * HD, (lh + 1) * HD)
-            t = a_ref[b, :, cs] + b_ref[b, :, cs].astype(jnp.float32)
+            t = a_ref[b, :, cs] * (HD ** (-0.5)) + b_ref[b, :, cs].astype(jnp.float32)
             h = lh % 3
             out_ref[lh // 3, b * HD : (b + 1) * HD, h * HD : (h + 1) * HD] = t.T.astype(jnp.bfloat16)
 

time: 135 us -> 134 us (level)
  Pallas kernels: 47.4 us -> 45.9 us
    all_to_all x4, starting transfers between devices: 25.4 us -> 27.2 us  [exchange(): return lax.all_to_all(a, axes, 0, 0)]
    pallas_call x1, Pallas kernels: 30.3 us -> 28.8 us  [attn(): pl.pallas_call(functools.partial(attn_kernel, groups, unroll, late), out_...]
    all_to_all x4, waiting for transfers between devices: 18.3 us -> 16.9 us  [exchange(): return lax.all_to_all(a, axes, 0, 0)]
where the time goes in v6:
time: 134 us; the launch traced here: 133 us
  starting transfers between devices  51.4 us (38%)
  Pallas kernels  45.9 us (34%)
  waiting for transfers between devices  25 us (19%)
  local copies, waits for them, and re-layouts  7.58 us (6%)
  between operations  1.58 us (1%)
    pallas_call x1, Pallas kernels, attn(): pl.pallas_call(functools.partial(attn_kernel, groups, unroll, late), out_...  28.8 us
    all_to_all x4, starting transfers between devices, exchange(): return lax.all_to_all(a, axes, 0, 0)  27.2 us
    all_to_all x4, waiting for transfers between devices, exchange(): return lax.all_to_all(a, axes, 0, 0)  16.9 us
    ppermute x15, starting transfers between devices, swap(): return lax.ppermute(a, 'co', [(0, 1), (1, 0)])  12.8 us
    ppermute x8, starting transfers between devices, split_shift(): return lax.ppermute(a, ('co', 'xh', 'z'), perm)  11.5 us
    unnamed x50, local copies, waits for them, and re-layouts  6.56 us
    ppermute x8, waiting for transfers between devices, split_shift(): return lax.ppermute(a, ('co', 'xh', 'z'), perm)  6.25 us
    pallas_call x1, Pallas kernels, project(): pl.pallas_call(kv_kernel, grid=(steps,), out_shape=jax.ShapeDtypeStruct((...  3.34 us
  transfers between devices with their start and end apart: 27, of which 4 were waited for; matrix products, arithmetic and copies ran while one was open for 2% of the time, Pallas kernels for 10%

profile of v6, /device:TPU:0, one launch (start us, length us, event | category | flops | bytes accessed | tf_op | source)
XLA Modules:
  0.0 132.5 jit_solution(15287337503843732238)
XLA Ops:
  0.6 3.3 %kv.1 = bf16[8,256,256]{2,1,0:T(8,128)(2,1)} custom-call(bf16[256,3072]{1,0:T(8,128)(2,1)} %x_ref.3, bf16[3072,256]{1,0:T(8,128)(2,1)} %w_ref.1), custom_call_target="tpu_custom_call" | custom-call | tf_op jit(solution)/shard_map/kv/pallas_call | solution.py:223
  4.0 5.7 %all-to-all-start = ((bf16[8,256,256]{2,1,0:T(8,128)(2,1)}), bf16[8,256,256]{2,1,0:T(8,128)(2,1)S(1)}, u32[]{:S(2)}, u32[]{:S(2)}) async-start(bf16[8,256,256]{2,1,0:T(8,128)(2,1)} %kv.1), calls=%async_computation | async-start | bytes 2097152 | tf_op jit(solution)/shard_map/all_to_all | solution.py:366
  11.8 1.8 %collective-permute-done.ints_p = s32[128]{0:T(128)S(1)} collective-permute-done((s32[128]{0:T(128)S(1)}, s32[128]{0:T(128)S(1)}, u32[]{:S(2)}, u32[]{:S(2)}) %collective-permute-start) | collective-permute-done | bytes 544 | tf_op jit(solution)/shard_map/ppermute | solution.py:352
  13.6 10.9 %all-to-all-done = bf16[8,256,256]{2,1,0:T(8,128)(2,1)S(1)} async-done(((bf16[8,256,256]{2,1,0:T(8,128)(2,1)}), bf16[8,256,256]{2,1,0:T(8,128)(2,1)S(1)}, u32[]{:S(2)}, u32[]{:S(2)}) %all-to-all-start) | async-done | bytes 1048608 | tf_op jit(solution)/shard_map/all_to_all | solution.py:366
  24.5 28.8 %attn.1 = (bf16[16,128,256]{2,1,0:T(8,128)(2,1)}, f32[3,128,1152]{2,1,0:T(8,128)}, bf16[3,128,1152]{2,1,0:T(8,128)(2,1)}) custom-call(s32[128]{0:T(128)} %copy-done.23, s32[128]{0:T(128)} %copy-done.24, s32[1]{0:T(128)} %bitcast.co_ref, f32[3,18,128]{2,1,0:T(8,128)S(1)} %copy.17.small_o, f32[3,18,128]{2,1,0:T(8,128)S(1)} %collective-permute-done.1.small_p, ...), custom_call_target="tpu_custom_call" | custom-call | tf_op jit(solution)/shard_map/attn/pallas_call | solution.py:169
  53.3 9.3 %all-to-all-start.1 = ((bf16[8,256,256]{2,1,0:T(8,128)(2,1)}), bf16[8,256,256]{2,1,0:T(8,128)(2,1)S(1)}, u32[]{:S(2)}, u32[]{:S(2)}) async-start(bf16[8,256,256]{2,1,0:T(8,128)(2,1)} %bitcast.23), calls=%async_computation.1 | async-start | bytes 2097152 | tf_op jit(solution)/shard_map/all_to_all | solution.py:366
  62.6 3.1 %xt.1 = (bf16[8,192,256]{2,1,0:T(8,128)(2,1)}, bf16[8,192,256]{2,1,0:T(8,128)(2,1)}) custom-call(s32[1]{0:T(128)} %bitcast.co_ref, bf16[256,3072]{1,0:T(8,128)(2,1)} %x_ref.3), custom_call_target="tpu_custom_call" | custom-call | tf_op jit(solution)/shard_map/xt/pallas_call | solution.py:255
  65.7 0.9 dynamic-slice_bitcast_fusion
  67.2 6.0 %all-to-all-done.1.r_ref = bf16[8,256,256]{2,1,0:T(8,128)(2,1)S(1)} async-done(((bf16[8,256,256]{2,1,0:T(8,128)(2,1)}), bf16[8,256,256]{2,1,0:T(8,128)(2,1)S(1)}, u32[]{:S(2)}, u32[]{:S(2)}) %all-to-all-start.1) | async-done | bytes 1048608 | tf_op jit(solution)/shard_map/all_to_all | solution.py:366
  74.0 1.9 %collective-permute-start.16 = (bf16[384,256]{1,0:T(8,128)(2,1)}, bf16[384,256]{1,0:T(8,128)(2,1)S(1)}, u32[]{:S(2)}, u32[]{:S(2)}) collective-permute-start(bf16[384,256]{1,0:T(8,128)(2,1)} %get-tuple-element.23), channel_id=1, source_target_pairs={{0,1},{8,13},{1,2},{9,14},{2,3},{10,15},{3,0},{11,12},{4,5},{12,9}... | collective-permute-start | bytes 589832 | tf_op jit(solution)/shard_map/ppermute | solution.py:362
  75.9 3.6 %collective-permute-start.17 = (bf16[384,256]{1,0:T(8,128)(2,1)}, bf16[384,256]{1,0:T(8,128)(2,1)S(1)}, u32[]{:S(2)}, u32[]{:S(2)}) collective-permute-start(bf16[384,256]{1,0:T(8,128)(2,1)} %get-tuple-element.22), channel_id=1, source_target_pairs={{0,2},{8,14},{1,3},{9,15},{2,0},{10,12},{3,1},{11,13},{4,6},{12,10... | collective-permute-start | bytes 589832 | tf_op jit(solution)/shard_map/ppermute | solution.py:362
  79.5 1.0 collective-permute-start.18
  80.5 3.2 %dw.1 = (bf16[8,192,256]{2,1,0:T(8,128)(2,1)}, bf16[2,256,256]{2,1,0:T(8,128)(2,1)}) custom-call(s32[1]{0:T(128)} %bitcast.co_ref, bf16[8,192,256]{2,1,0:T(8,128)(2,1)S(1)} %copy-done, bf16[8,192,256]{2,1,0:T(8,128)(2,1)} %collective-permute-done.5.xb_ref, bf16[256,256]{1,0:T(8,128)(2,1)S(1)} %shard_map.104.ga_ref.g_ref, ...), custom_call_target="tpu_custom_call" | custom-call | tf_op jit(solution)/shard_map/dw/pallas_call | solution.py:281
  83.7 3.7 %all-to-all-start.2 = ((bf16[8,192,256]{2,1,0:T(8,128)(2,1)}), bf16[8,192,256]{2,1,0:T(8,128)(2,1)S(1)}, u32[]{:S(2)}, u32[]{:S(2)}) async-start(bf16[8,192,256]{2,1,0:T(8,128)(2,1)} %get-tuple-element.18), calls=%async_computation.2 | async-start | bytes 1572864 | tf_op jit(solution)/shard_map/all_to_all | solution.py:366
  87.5 1.0 broadcast_select_fusion.refs_8_
  88.5 2.8 %collective-permute-start.19 = (bf16[384,256]{1,0:T(8,128)(2,1)S(1)}, bf16[384,256]{1,0:T(8,128)(2,1)S(1)}, u32[]{:S(2)}, u32[]{:S(2)}) collective-permute-start(bf16[384,256]{1,0:T(8,128)(2,1)S(1)} %broadcast_select_fusion.refs_8_), channel_id=1, source_target_pairs={{0,8},{8,0},{1,9},{9,1},{2,10},{10,2},{3,11},{11,3},{4,12},{12,4},... | collective-permute-start | bytes 589832 | tf_op jit(solution)/shard_map/ppermute | solution.py:352
  93.2 1.0 collective-permute-start.8
  94.2 0.7 copy-done.9
  95.6 2.7 %collective-permute-start.10 = (bf16[2,256,256]{2,1,0:T(8,128)(2,1)}, bf16[2,256,256]{2,1,0:T(8,128)(2,1)S(1)}, u32[]{:S(2)}, u32[]{:S(2)}) collective-permute-start(bf16[2,256,256]{2,1,0:T(8,128)(2,1)} %get-tuple-element.17), channel_id=1, source_target_pairs={{0,3},{8,15},{1,0},{9,12},{2,1},{10,13},{3,2},{11,14},{4,7},{12,11... | collective-permute-start | bytes 786440 | tf_op jit(solution)/shard_map/ppermute | solution.py:362
  98.2 4.9 %collective-permute-start.11 = (bf16[2,256,256]{2,1,0:T(8,128)(2,1)S(1)}, bf16[2,256,256]{2,1,0:T(8,128)(2,1)S(1)}, u32[]{:S(2)}, u32[]{:S(2)}) collective-permute-start(bf16[2,256,256]{2,1,0:T(8,128)(2,1)S(1)} %collective-permute-done.7.refs_0_), channel_id=1, source_target_pairs={{0,8},{8,0},{1,9},{9,1},{2,10},{10,2},{3,11},{11,3},{4,12},{12,4},... | collective-permute-start | bytes 786440 | tf_op jit(solution)/shard_map/ppermute | solution.py:352
  103.2 6.2 %collective-permute-done.8.refs_1_ = bf16[2,256,256]{2,1,0:T(8,128)(2,1)S(1)} collective-permute-done((bf16[2,256,256]{2,1,0:T(8,128)(2,1)}, bf16[2,256,256]{2,1,0:T(8,128)(2,1)S(1)}, u32[]{:S(2)}, u32[]{:S(2)}) %collective-permute-start.8) | collective-permute-done | bytes 262176 | tf_op jit(solution)/shard_map/ppermute | solution.py:362
  109.9 2.1 %collective-permute-start.14 = (bf16[2,256,256]{2,1,0:T(8,128)(2,1)S(1)}, bf16[2,256,256]{2,1,0:T(8,128)(2,1)}, u32[]{:S(2)}, u32[]{:S(2)}) collective-permute-start(bf16[2,256,256]{2,1,0:T(8,128)(2,1)S(1)} %collective-permute-done.10.refs_3_), channel_id=1, source_target_pairs={{0,8},{8,0},{1,9},{9,1},{2,10},{10,2},{3,11},{11,3},{4,12},{12,4},... | collective-permute-start | bytes 786440 | tf_op jit(solution)/shard_map/ppermute | solution.py:352
  112.1 0.9 shard_map.106
  113.0 8.4 %all-to-all-start.3 = ((f32[128,1,128]{2,1,0:T(1,128)}), f32[128,1,128]{2,1,0:T(1,128)S(1)}, u32[]{:S(2)}, u32[]{:S(2)}) async-start(f32[128,1,128]{2,1,0:T(1,128)} %bitcast.11), calls=%async_computation.3 | async-start | bytes 131072 | tf_op jit(solution)/shard_map/all_to_all | solution.py:366
  121.5 2.8 %shard_map.103 = bf16[3,384,384]{2,1,0:T(8,128)(2,1)} custom-call(f32[3,128,1152]{2,1,0:T(8,128)} %get-tuple-element.12.a_ref, bf16[3,128,1152]{2,1,0:T(8,128)(2,1)S(1)} %collective-permute-done.4.b_ref), custom_call_target="tpu_custom_call" | custom-call | tf_op jit(solution)/shard_map/pallas_call | solution.py:403
  124.3 0.7 copy-done.5
  125.1 0.9 copy-done.2
  126.0 0.9 copy-done.4
  126.9 0.9 copy-done.6
  127.9 0.9 copy-done.12
  128.8 2.9 %shard_map.105 = bf16[256,384]{1,0:T(8,128)(2,1)} custom-call(s32[1]{0:T(128)} %bitcast.co_ref, bf16[256,256]{1,0:T(8,128)(2,1)S(1)} %shard_map.104.ga_ref.g_ref, bf16[2,256,256]{2,1,0:T(8,128)(2,1)S(1)} %collective-permute-done.7.refs_0_, bf16[2,256,256]{2,1,0:T(8,128)(2,1)S(1)} %collective-permute-done.8.refs_1_, bf16[2,256,256]{2,1,0:T(8,128)(2,1)S(1)} %copy-done.2, ...), custom_call_target="tpu_custom_call" | custom-call | tf_op jit(solution)/shard_map/pallas_call | solution.py:400
  131.7 0.8 shard_map.107
  (90 shorter events, 6.0 us)
Async XLA Ops:
  4.0 20.5 %all-to-all-start = ((bf16[8,256,256]{2,1,0:T(8,128)(2,1)}), bf16[8,256,256]{2,1,0:T(8,128)(2,1)S(1)}, u32[]{:S(2)}, u32[]{:S(2)}) async-start(bf16[8,256,256]{2,1,0:T(8,128)(2,1)} %kv.1), calls=%async_computation | async-start | bytes 2097152 | tf_op jit(solution)/shard_map/all_to_all | solution.py:366
  9.7 3.9 %collective-permute-start.2 = (bf16[3,384,384]{2,1,0:T(8,128)(2,1)S(1)}, bf16[3,384,384]{2,1,0:T(8,128)(2,1)}, u32[]{:S(2)}, u32[]{:S(2)}) collective-permute-start(bf16[3,384,384]{2,1,0:T(8,128)(2,1)S(1)} %copy-done.16), channel_id=1, source_target_pairs={{0,8},{8,0},{1,9},{9,1},{2,10},{10,2},{3,11},{11,3},{4,12},{12,4},... | collective-permute-start | bytes 2654216 | tf_op jit(solution)/shard_map/ppermute | solution.py:352
  9.7 3.8 %collective-permute-start.3 = (bf16[3,384,384]{2,1,0:T(8,128)(2,1)}, bf16[3,384,384]{2,1,0:T(8,128)(2,1)}, u32[]{:S(2)}, u32[]{:S(2)}) collective-permute-start(bf16[3,384,384]{2,1,0:T(8,128)(2,1)} %oo.1), channel_id=1, source_target_pairs={{0,8},{8,0},{1,9},{9,1},{2,10},{10,2},{3,11},{11,3},{4,12},{12,4},... | collective-permute-start | bytes 2654216 | tf_op jit(solution)/shard_map/ppermute | solution.py:352
  10.3 3.2 %collective-permute-start.1 = (f32[3,18,128]{2,1,0:T(8,128)S(1)}, f32[3,18,128]{2,1,0:T(8,128)S(1)}, u32[]{:S(2)}, u32[]{:S(2)}) collective-permute-start(f32[3,18,128]{2,1,0:T(8,128)S(1)} %copy.17.small_o), channel_id=1, source_target_pairs={{0,8},{8,0},{1,9},{9,1},{2,10},{10,2},{3,11},{11,3},{4,12},{12,4},... | collective-permute-start | bytes 82952 | tf_op jit(solution)/shard_map/ppermute | solution.py:352
  11.3 13.1 %copy-start.23 = (s32[128]{0:T(128)}, s32[128]{0:T(128)S(1)}, u32[]{:S(2)}) copy-start(s32[128]{0:T(128)S(1)} %pad_add_fusion.ints_o) | copy-start | bytes 1540
  11.3 2.2 %collective-permute-start = (s32[128]{0:T(128)S(1)}, s32[128]{0:T(128)S(1)}, u32[]{:S(2)}, u32[]{:S(2)}) collective-permute-start(s32[128]{0:T(128)S(1)} %pad_add_fusion.ints_o), channel_id=1, source_target_pairs={{0,8},{8,0},{1,9},{9,1},{2,10},{10,2},{3,11},{11,3},{4,12},{12,4},... | collective-permute-start | bytes 1544 | tf_op jit(solution)/shard_map/ppermute | solution.py:352
  53.3 20.0 %all-to-all-start.1 = ((bf16[8,256,256]{2,1,0:T(8,128)(2,1)}), bf16[8,256,256]{2,1,0:T(8,128)(2,1)S(1)}, u32[]{:S(2)}, u32[]{:S(2)}) async-start(bf16[8,256,256]{2,1,0:T(8,128)(2,1)} %bitcast.23), calls=%async_computation.1 | async-start | bytes 2097152 | tf_op jit(solution)/shard_map/all_to_all | solution.py:366
  65.7 14.9 %copy-start = (bf16[8,192,256]{2,1,0:T(8,128)(2,1)S(1)}, bf16[8,192,256]{2,1,0:T(8,128)(2,1)}, u32[]{:S(2)}) copy-start(bf16[8,192,256]{2,1,0:T(8,128)(2,1)} %get-tuple-element.15.xa_ref) | copy-start | bytes 2359300
  65.7 10.3 %collective-permute-start.5 = (bf16[8,192,256]{2,1,0:T(8,128)(2,1)}, bf16[8,192,256]{2,1,0:T(8,128)(2,1)}, u32[]{:S(2)}, u32[]{:S(2)}) collective-permute-start(bf16[8,192,256]{2,1,0:T(8,128)(2,1)} %get-tuple-element.16), channel_id=1, source_target_pairs={{0,8},{8,0},{1,9},{9,1},{2,10},{10,2},{3,11},{11,3},{4,12},{12,4},... | collective-permute-start | bytes 2359304 | tf_op jit(solution)/shard_map/ppermute | solution.py:352
  66.6 20.9 %collective-permute-start.15 = (bf16[384,256]{1,0:T(8,128)(2,1)}, bf16[384,256]{1,0:T(8,128)(2,1)S(1)}, u32[]{:S(2)}, u32[]{:S(2)}) collective-permute-start(bf16[384,256]{1,0:T(8,128)(2,1)} %get-tuple-element.24), channel_id=1, source_target_pairs={{8,12},{9,13},{10,14},{11,15},{12,8},{13,9},{14,10},{15,11},{24,28... | collective-permute-start | bytes 589832 | tf_op jit(solution)/shard_map/ppermute | solution.py:362
  73.4 6.1 %collective-permute-start.6 = (bf16[256,256]{1,0:T(8,128)(2,1)S(1)}, bf16[256,256]{1,0:T(8,128)(2,1)S(1)}, u32[]{:S(2)}, u32[]{:S(2)}) collective-permute-start(bf16[256,256]{1,0:T(8,128)(2,1)S(1)} %shard_map.104.ga_ref.g_ref), channel_id=1, source_target_pairs={{0,8},{8,0},{1,9},{9,1},{2,10},{10,2},{3,11},{11,3},{4,12},{12,4},... | collective-permute-start | bytes 393224 | tf_op jit(solution)/shard_map/ppermute | solution.py:352
  73.5 38.5 %collective-permute-start.4 = (bf16[3,128,1152]{2,1,0:T(8,128)(2,1)}, bf16[3,128,1152]{2,1,0:T(8,128)(2,1)S(1)}, u32[]{:S(2)}, u32[]{:S(2)}) collective-permute-start(bf16[3,128,1152]{2,1,0:T(8,128)(2,1)} %get-tuple-element.13), channel_id=1, source_target_pairs={{0,8},{8,0},{1,9},{9,1},{2,10},{10,2},{3,11},{11,3},{4,12},{12,4},... | collective-permute-start | bytes 2654216 | tf_op jit(solution)/shard_map/ppermute | solution.py:352
  74.0 17.3 %collective-permute-start.16 = (bf16[384,256]{1,0:T(8,128)(2,1)}, bf16[384,256]{1,0:T(8,128)(2,1)S(1)}, u32[]{:S(2)}, u32[]{:S(2)}) collective-permute-start(bf16[384,256]{1,0:T(8,128)(2,1)} %get-tuple-element.23), channel_id=1, source_target_pairs={{0,1},{8,13},{1,2},{9,14},{2,3},{10,15},{3,0},{11,12},{4,5},{12,9}... | collective-permute-start | bytes 589832 | tf_op jit(solution)/shard_map/ppermute | solution.py:362
  75.9 15.5 %collective-permute-start.17 = (bf16[384,256]{1,0:T(8,128)(2,1)}, bf16[384,256]{1,0:T(8,128)(2,1)S(1)}, u32[]{:S(2)}, u32[]{:S(2)}) collective-permute-start(bf16[384,256]{1,0:T(8,128)(2,1)} %get-tuple-element.22), channel_id=1, source_target_pairs={{0,2},{8,14},{1,3},{9,15},{2,0},{10,12},{3,1},{11,13},{4,6},{12,10... | collective-permute-start | bytes 589832 | tf_op jit(solution)/shard_map/ppermute | solution.py:362
  79.5 12.3 %collective-permute-start.18 = (bf16[384,256]{1,0:T(8,128)(2,1)}, bf16[384,256]{1,0:T(8,128)(2,1)}, u32[]{:S(2)}, u32[]{:S(2)}) collective-permute-start(bf16[384,256]{1,0:T(8,128)(2,1)} %get-tuple-element.21), channel_id=1, source_target_pairs={{0,3},{8,15},{1,0},{9,12},{2,1},{10,13},{3,2},{11,14},{4,7},{12,11... | collective-permute-start | bytes 589832 | tf_op jit(solution)/shard_map/ppermute | solution.py:362
  83.7 28.4 %all-to-all-start.2 = ((bf16[8,192,256]{2,1,0:T(8,128)(2,1)}), bf16[8,192,256]{2,1,0:T(8,128)(2,1)S(1)}, u32[]{:S(2)}, u32[]{:S(2)}) async-start(bf16[8,192,256]{2,1,0:T(8,128)(2,1)} %get-tuple-element.18), calls=%async_computation.2 | async-start | bytes 1572864 | tf_op jit(solution)/shard_map/all_to_all | solution.py:366
  88.4 23.6 %copy-start.17 = (bf16[384,256]{1,0:T(8,128)(2,1)}, bf16[384,256]{1,0:T(8,128)(2,1)S(1)}, u32[]{:S(2)}) copy-start(bf16[384,256]{1,0:T(8,128)(2,1)S(1)} %broadcast_select_fusion.refs_8_) | copy-start | bytes 589828
  88.5 4.0 %collective-permute-start.19 = (bf16[384,256]{1,0:T(8,128)(2,1)S(1)}, bf16[384,256]{1,0:T(8,128)(2,1)S(1)}, u32[]{:S(2)}, u32[]{:S(2)}) collective-permute-start(bf16[384,256]{1,0:T(8,128)(2,1)S(1)} %broadcast_select_fusion.refs_8_), channel_id=1, source_target_pairs={{0,8},{8,0},{1,9},{9,1},{2,10},{10,2},{3,11},{11,3},{4,12},{12,4},... | collective-permute-start | bytes 589832 | tf_op jit(solution)/shard_map/ppermute | solution.py:352
  91.3 2.9 %collective-permute-start.20 = (bf16[384,256]{1,0:T(8,128)(2,1)S(1)}, bf16[384,256]{1,0:T(8,128)(2,1)S(1)}, u32[]{:S(2)}, u32[]{:S(2)}) collective-permute-start(bf16[384,256]{1,0:T(8,128)(2,1)S(1)} %collective-permute-done.16.refs_9_), channel_id=1, source_target_pairs={{0,8},{8,0},{1,9},{9,1},{2,10},{10,2},{3,11},{11,3},{4,12},{12,4},... | collective-permute-start | bytes 589832 | tf_op jit(solution)/shard_map/ppermute | solution.py:352
  91.4 3.5 %collective-permute-start.21 = (bf16[384,256]{1,0:T(8,128)(2,1)S(1)}, bf16[384,256]{1,0:T(8,128)(2,1)S(1)}, u32[]{:S(2)}, u32[]{:S(2)}) collective-permute-start(bf16[384,256]{1,0:T(8,128)(2,1)S(1)} %collective-permute-done.17.refs_10_), channel_id=1, source_target_pairs={{0,8},{8,0},{1,9},{9,1},{2,10},{10,2},{3,11},{11,3},{4,12},{12,4},... | collective-permute-start | bytes 589832 | tf_op jit(solution)/shard_map/ppermute | solution.py:352
  91.8 6.4 %collective-permute-start.7 = (bf16[2,256,256]{2,1,0:T(8,128)(2,1)}, bf16[2,256,256]{2,1,0:T(8,128)(2,1)S(1)}, u32[]{:S(2)}, u32[]{:S(2)}) collective-permute-start(bf16[2,256,256]{2,1,0:T(8,128)(2,1)} %get-tuple-element.17), channel_id=1, source_target_pairs={{8,12},{9,13},{10,14},{11,15},{12,8},{13,9},{14,10},{15,11},{24,28... | collective-permute-start | bytes 786440 | tf_op jit(solution)/shard_map/ppermute | solution.py:362
  93.2 16.2 %collective-permute-start.8 = (bf16[2,256,256]{2,1,0:T(8,128)(2,1)}, bf16[2,256,256]{2,1,0:T(8,128)(2,1)S(1)}, u32[]{:S(2)}, u32[]{:S(2)}) collective-permute-start(bf16[2,256,256]{2,1,0:T(8,128)(2,1)} %get-tuple-element.17), channel_id=1, source_target_pairs={{0,1},{8,13},{1,2},{9,14},{2,3},{10,15},{3,0},{11,12},{4,5},{12,9}... | collective-permute-start | bytes 786440 | tf_op jit(solution)/shard_map/ppermute | solution.py:362
  94.9 14.5 %collective-permute-start.9 = (bf16[2,256,256]{2,1,0:T(8,128)(2,1)}, bf16[2,256,256]{2,1,0:T(8,128)(2,1)S(1)}, u32[]{:S(2)}, u32[]{:S(2)}) collective-permute-start(bf16[2,256,256]{2,1,0:T(8,128)(2,1)} %get-tuple-element.17), channel_id=1, source_target_pairs={{0,2},{8,14},{1,3},{9,15},{2,0},{10,12},{3,1},{11,13},{4,6},{12,10... | collective-permute-start | bytes 786440 | tf_op jit(solution)/shard_map/ppermute | solution.py:362
  95.6 14.4 %collective-permute-start.10 = (bf16[2,256,256]{2,1,0:T(8,128)(2,1)}, bf16[2,256,256]{2,1,0:T(8,128)(2,1)S(1)}, u32[]{:S(2)}, u32[]{:S(2)}) collective-permute-start(bf16[2,256,256]{2,1,0:T(8,128)(2,1)} %get-tuple-element.17), channel_id=1, source_target_pairs={{0,3},{8,15},{1,0},{9,12},{2,1},{10,13},{3,2},{11,14},{4,7},{12,11... | collective-permute-start | bytes 786440 | tf_op jit(solution)/shard_map/ppermute | solution.py:362
  98.2 26.1 %collective-permute-start.11 = (bf16[2,256,256]{2,1,0:T(8,128)(2,1)S(1)}, bf16[2,256,256]{2,1,0:T(8,128)(2,1)S(1)}, u32[]{:S(2)}, u32[]{:S(2)}) collective-permute-start(bf16[2,256,256]{2,1,0:T(8,128)(2,1)S(1)} %collective-permute-done.7.refs_0_), channel_id=1, source_target_pairs={{0,8},{8,0},{1,9},{9,1},{2,10},{10,2},{3,11},{11,3},{4,12},{12,4},... | collective-permute-start | bytes 786440 | tf_op jit(solution)/shard_map/ppermute | solution.py:352
  109.4 15.6 %collective-permute-start.12 = (bf16[2,256,256]{2,1,0:T(8,128)(2,1)S(1)}, bf16[2,256,256]{2,1,0:T(8,128)(2,1)}, u32[]{:S(2)}, u32[]{:S(2)}) collective-permute-start(bf16[2,256,256]{2,1,0:T(8,128)(2,1)S(1)} %collective-permute-done.8.refs_1_), channel_id=1, source_target_pairs={{0,8},{8,0},{1,9},{9,1},{2,10},{10,2},{3,11},{11,3},{4,12},{12,4},... | collective-permute-start | bytes 786440 | tf_op jit(solution)/shard_map/ppermute | solution.py:352
  109.4 14.9 %copy-start.1 = (bf16[2,256,256]{2,1,0:T(8,128)(2,1)}, bf16[2,256,256]{2,1,0:T(8,128)(2,1)S(1)}, u32[]{:S(2)}) copy-start(bf16[2,256,256]{2,1,0:T(8,128)(2,1)S(1)} %collective-permute-done.9.refs_2_) | copy-start | bytes 786436
  109.4 15.6 %collective-permute-start.13 = (bf16[2,256,256]{2,1,0:T(8,128)(2,1)S(1)}, bf16[2,256,256]{2,1,0:T(8,128)(2,1)}, u32[]{:S(2)}, u32[]{:S(2)}) collective-permute-start(bf16[2,256,256]{2,1,0:T(8,128)(2,1)S(1)} %collective-permute-done.9.refs_2_), channel_id=1, source_target_pairs={{0,8},{8,0},{1,9},{9,1},{2,10},{10,2},{3,11},{11,3},{4,12},{12,4},... | collective-permute-start | bytes 786440 | tf_op jit(solution)/shard_map/ppermute | solution.py:352
  109.9 14.4 %copy-start.3 = (bf16[2,256,256]{2,1,0:T(8,128)(2,1)}, bf16[2,256,256]{2,1,0:T(8,128)(2,1)S(1)}, u32[]{:S(2)}) copy-start(bf16[2,256,256]{2,1,0:T(8,128)(2,1)S(1)} %collective-permute-done.10.refs_3_) | copy-start | bytes 786436
  109.9 15.1 %collective-permute-start.14 = (bf16[2,256,256]{2,1,0:T(8,128)(2,1)S(1)}, bf16[2,256,256]{2,1,0:T(8,128)(2,1)}, u32[]{:S(2)}, u32[]{:S(2)}) collective-permute-start(bf16[2,256,256]{2,1,0:T(8,128)(2,1)S(1)} %collective-permute-done.10.refs_3_), channel_id=1, source_target_pairs={{0,8},{8,0},{1,9},{9,1},{2,10},{10,2},{3,11},{11,3},{4,12},{12,4},... | collective-permute-start | bytes 786440 | tf_op jit(solution)/shard_map/ppermute | solution.py:352
  112.0 12.2 %collective-permute-start.22 = (bf16[384,256]{1,0:T(8,128)(2,1)}, bf16[384,256]{1,0:T(8,128)(2,1)}, u32[]{:S(2)}, u32[]{:S(2)}) collective-permute-start(bf16[384,256]{1,0:T(8,128)(2,1)} %collective-permute-done.18.refs_11_), channel_id=1, source_target_pairs={{0,8},{8,0},{1,9},{9,1},{2,10},{10,2},{3,11},{11,3},{4,12},{12,4},... | collective-permute-start | bytes 589832 | tf_op jit(solution)/shard_map/ppermute | solution.py:352
  113.0 18.7 %all-to-all-start.3 = ((f32[128,1,128]{2,1,0:T(1,128)}), f32[128,1,128]{2,1,0:T(1,128)S(1)}, u32[]{:S(2)}, u32[]{:S(2)}) async-start(f32[128,1,128]{2,1,0:T(1,128)} %bitcast.11), calls=%async_computation.3 | async-start | bytes 131072 | tf_op jit(solution)/shard_map/all_to_all | solution.py:366
  (20 other events, 83.6 us)

commit v7 on v6

--- a/solution.py
+++ b/solution.py
@@ -309,11 +309,11 @@
     out_ref[...] = grad_ref[...] / jnp.sqrt(total / (D * KVH * 2 * HD) + 1e-06)
 
 
-def dx_kernel(co_ref, g_ref, *refs):
+def dx_kernel(co_ref, g_ref, w_ref, *refs):
     ra, rb, wa, wb, out_ref = refs[:4], refs[4:8], refs[8:12], refs[12:16], refs[16]
 
     def total(me, near, far, w_near, w_far):
-        acc = lax.dot_general(g_ref[...], w_near[0][...], NT, preferred_element_type=jnp.float32)
+        acc = lax.dot_general(g_ref[...], w_ref[...], NT, preferred_element_type=jnp.float32)
         for k in range(4):
             if k > 0:
                 acc += lax.dot_general(near[k][me], w_near[k][...], NT, preferred_element_type=jnp.float32)
@@ -377,8 +377,8 @@
     wa = []
     for j in range(4):
         piece = lax.dynamic_index_in_dim(w_rows, 4 * ((xh + co) % 2) + (z + j) % 4, 0, False)
-        got = split_shift(piece, j)
-        wa.append(jnp.where(co == 0, piece, got) if j == 0 else got)
+        wa.append(split_shift(piece, j))
+    w_own = lax.dynamic_index_in_dim(w_rows, 4 * xh + z, 0, False)
     ints = jnp.concatenate([block_mask.reshape(96), offsets, jnp.zeros((31,), jnp.int32)])
     rows = jnp.concatenate([lse, delta], axis=2).reshape(NL, 3, HD, 2, 3)
     small = jnp.transpose(rows, (1, 3, 0, 4, 2)).reshape(3, 2 * NLH, HD)
@@ -397,8 +397,8 @@
     ra = [split_shift(pair, j) for j in range(4)]
     rb = [swap(r) for r in ra]
     wb = [swap(w) for w in wa]
-    (d_x,) = call(dx_kernel, [SM] + [VM] * 17, ((256, 384), bf), near=False)(
-        co1, *map(vm, [g] + ra + rb), *wa, *map(vm, wb)
+    (d_x,) = call(dx_kernel, [SM] + [VM] * 18, ((256, 384), bf), near=False)(
+        co1, vm(g), w_own, *map(vm, ra + rb), *wa, *map(vm, wb)
     )
     (d_queries,) = call(dq_kernel, [VM] * 2, ((NL, 384, 384), bf), near=False)(dqo, vm(swap(dqp)))
     (d_w,) = call(scale_kernel, [VM] * 2, ((192, 256), f32), near=False)(vm(grad), vm(parts.reshape(128, HD)))

time: 134 us -> 151 us (1.13)
  starting transfers between devices: 51.4 us -> 68.7 us
  waiting for transfers between devices: 25 us -> 16.7 us
  local copies, waits for them, and re-layouts: 7.58 us -> 15.7 us
  Pallas kernels: 45.9 us -> 47.6 us
    ppermute x15, starting transfers between devices: 12.8 us -> 28.1 us  [swap(): return lax.ppermute(a, 'co', [(0, 1), (1, 0)])]
    unnamed x50 -> x54, local copies, waits for them, and re-layouts: 6.56 us -> 13.5 us
    all_to_all x4, waiting for transfers between devices: 16.9 us -> 10.9 us  [exchange(): return lax.all_to_all(a, axes, 0, 0)]
    ppermute x8, waiting for transfers between devices: 6.25 us -> 3.01 us  [split_shift(): return lax.ppermute(a, ('co', 'xh', 'z'), perm)]
    all_to_all x4, starting transfers between devices: 27.2 us -> 29 us  [exchange(): return lax.all_to_all(a, axes, 0, 0)]
    pallas_call x1, Pallas kernels: 3.21 us -> 4.88 us  [weight_parts(): pl.pallas_call(dw_kernel, out_shape=(jax.ShapeDtypeStruct((8, 192, 256),...]
where the time goes in v7:
time: 151 us; the launch traced here: 150 us
  starting transfers between devices  68.7 us (45%)
  Pallas kernels  47.6 us (32%)
  waiting for transfers between devices  16.7 us (11%)
  local copies, waits for them, and re-layouts  15.7 us (10%)
  between operations  1.52 us (1%)
    all_to_all x4, starting transfers between devices, exchange(): return lax.all_to_all(a, axes, 0, 0)  29 us
    pallas_call x1, Pallas kernels, attn(): pl.pallas_call(functools.partial(attn_kernel, groups, unroll, late), out_...  28.8 us
    ppermute x15, starting transfers between devices, swap(): return lax.ppermute(a, 'co', [(0, 1), (1, 0)])  28.1 us
    unnamed x54, local copies, waits for them, and re-layouts  13.5 us
    ppermute x8, starting transfers between devices, split_shift(): return lax.ppermute(a, ('co', 'xh', 'z'), perm)  11.6 us
    all_to_all x4, waiting for transfers between devices, exchange(): return lax.all_to_all(a, axes, 0, 0)  10.9 us
    pallas_call x1, Pallas kernels, weight_parts(): pl.pallas_call(dw_kernel, out_shape=(jax.ShapeDtypeStruct((8, 192, 256),...  4.88 us
    pallas_call x1, Pallas kernels, project(): pl.pallas_call(kv_kernel, grid=(steps,), out_shape=jax.ShapeDtypeStruct((...  3.37 us
  transfers between devices with their start and end apart: 27, of which 4 were waited for; matrix products, arithmetic and copies ran while one was open for 2% of the time, Pallas kernels for 10%

profile of v7, /device:TPU:0, one launch (start us, length us, event | category | flops | bytes accessed | tf_op | source)
XLA Modules:
  0.0 150.3 jit_solution(3008415628742738885)
XLA Ops:
  0.6 3.4 %kv.1 = bf16[8,256,256]{2,1,0:T(8,128)(2,1)} custom-call(bf16[256,3072]{1,0:T(8,128)(2,1)} %x_ref.3, bf16[3072,256]{1,0:T(8,128)(2,1)} %w_ref.1), custom_call_target="tpu_custom_call" | custom-call | tf_op jit(solution)/shard_map/kv/pallas_call | solution.py:223
  4.0 5.7 %all-to-all-start = ((bf16[8,256,256]{2,1,0:T(8,128)(2,1)}), bf16[8,256,256]{2,1,0:T(8,128)(2,1)S(1)}, u32[]{:S(2)}, u32[]{:S(2)}) async-start(bf16[8,256,256]{2,1,0:T(8,128)(2,1)} %kv.1), calls=%async_computation | async-start | bytes 2097152 | tf_op jit(solution)/shard_map/all_to_all | solution.py:366
  11.8 1.8 %collective-permute-done.ints_p = s32[128]{0:T(128)S(1)} collective-permute-done((s32[128]{0:T(128)S(1)}, s32[128]{0:T(128)S(1)}, u32[]{:S(2)}, u32[]{:S(2)}) %collective-permute-start) | collective-permute-done | bytes 544 | tf_op jit(solution)/shard_map/ppermute | solution.py:352
  13.6 10.9 %all-to-all-done = bf16[8,256,256]{2,1,0:T(8,128)(2,1)S(1)} async-done(((bf16[8,256,256]{2,1,0:T(8,128)(2,1)}), bf16[8,256,256]{2,1,0:T(8,128)(2,1)S(1)}, u32[]{:S(2)}, u32[]{:S(2)}) %all-to-all-start) | async-done | bytes 1048608 | tf_op jit(solution)/shard_map/all_to_all | solution.py:366
  24.5 28.8 %attn.1 = (bf16[16,128,256]{2,1,0:T(8,128)(2,1)}, f32[3,128,1152]{2,1,0:T(8,128)}, bf16[3,128,1152]{2,1,0:T(8,128)(2,1)}) custom-call(s32[128]{0:T(128)} %copy-done.25, s32[128]{0:T(128)} %copy-done.26, s32[1]{0:T(128)} %bitcast.co_ref, f32[3,18,128]{2,1,0:T(8,128)S(1)} %copy.17.small_o, f32[3,18,128]{2,1,0:T(8,128)S(1)} %collective-permute-done.1.small_p, ...), custom_call_target="tpu_custom_call" | custom-call | tf_op jit(solution)/shard_map/attn/pallas_call | solution.py:169
  53.3 9.2 %all-to-all-start.1 = ((bf16[8,256,256]{2,1,0:T(8,128)(2,1)}), bf16[8,256,256]{2,1,0:T(8,128)(2,1)S(1)}, u32[]{:S(2)}, u32[]{:S(2)}) async-start(bf16[8,256,256]{2,1,0:T(8,128)(2,1)} %bitcast.25), calls=%async_computation.1 | async-start | bytes 2097152 | tf_op jit(solution)/shard_map/all_to_all | solution.py:366
  62.5 3.1 %xt.1 = (bf16[8,192,256]{2,1,0:T(8,128)(2,1)}, bf16[8,192,256]{2,1,0:T(8,128)(2,1)}) custom-call(s32[1]{0:T(128)} %bitcast.co_ref, bf16[256,3072]{1,0:T(8,128)(2,1)} %x_ref.3), custom_call_target="tpu_custom_call" | custom-call | tf_op jit(solution)/shard_map/xt/pallas_call | solution.py:255
  66.1 2.1 %dynamic-slice_bitcast_fusion = (bf16[384,256]{1,0:T(8,128)(2,1)S(1)}, bf16[384,256]{1,0:T(8,128)(2,1)S(1)}, bf16[384,256]{1,0:T(8,128)(2,1)}, bf16[384,256]{1,0:T(8,128)(2,1)}, bf16[384,256]{1,0:T(8,128)(2,1)}) fusion(bf16[8,384,256]{2,1,0:T(8,128)(2,1)} %bitcast.24, s32[]{:T(128)S(6)} %select_n.54, s32[]{:T(128)S(6)} %select_n.52, s32[]{:T(128)S(6)} %select_n.50, ...), kind=kLoop, calls=%fused_computation | loop fusion | bytes 1966100 | tf_op jit(solution)/shard_map/jit(dynamic_index_in_dim)/squeeze | solution.py:379
  68.9 2.0 %collective-permute-start.16 = (bf16[384,256]{1,0:T(8,128)(2,1)}, bf16[384,256]{1,0:T(8,128)(2,1)}, u32[]{:S(2)}, u32[]{:S(2)}) collective-permute-start(bf16[384,256]{1,0:T(8,128)(2,1)} %get-tuple-element.23), channel_id=1, source_target_pairs={{0,1},{8,13},{1,2},{9,14},{2,3},{10,15},{3,0},{11,12},{4,5},{12,9}... | collective-permute-start | bytes 589832 | tf_op jit(solution)/shard_map/ppermute | solution.py:362
  70.9 3.6 %collective-permute-start.17 = (bf16[384,256]{1,0:T(8,128)(2,1)S(1)}, bf16[384,256]{1,0:T(8,128)(2,1)}, u32[]{:S(2)}, u32[]{:S(2)}) collective-permute-start(bf16[384,256]{1,0:T(8,128)(2,1)S(1)} %get-tuple-element.22), channel_id=1, source_target_pairs={{0,2},{8,14},{1,3},{9,15},{2,0},{10,12},{3,1},{11,13},{4,6},{12,10... | collective-permute-start | bytes 589832 | tf_op jit(solution)/shard_map/ppermute | solution.py:362
  74.6 5.6 %collective-permute-start.6 = (bf16[256,256]{1,0:T(8,128)(2,1)S(1)}, bf16[256,256]{1,0:T(8,128)(2,1)S(1)}, u32[]{:S(2)}, u32[]{:S(2)}) collective-permute-start(bf16[256,256]{1,0:T(8,128)(2,1)S(1)} %shard_map.104.ga_ref.g_ref), channel_id=1, source_target_pairs={{0,8},{8,0},{1,9},{9,1},{2,10},{10,2},{3,11},{11,3},{4,12},{12,4},... | collective-permute-start | bytes 393224 | tf_op jit(solution)/shard_map/ppermute | solution.py:352
  80.2 1.0 collective-permute-done.6.gb_ref
  81.2 4.9 %dw.1 = (bf16[8,192,256]{2,1,0:T(8,128)(2,1)S(1)}, bf16[2,256,256]{2,1,0:T(8,128)(2,1)}) custom-call(s32[1]{0:T(128)} %bitcast.co_ref, bf16[8,192,256]{2,1,0:T(8,128)(2,1)S(1)} %copy-done.2, bf16[8,192,256]{2,1,0:T(8,128)(2,1)} %collective-permute-done.5.xb_ref, bf16[256,256]{1,0:T(8,128)(2,1)S(1)} %shard_map.104.ga_ref.g_ref, ...), custom_call_target="tpu_custom_call" | custom-call | tf_op jit(solution)/shard_map/dw/pallas_call | solution.py:281
  87.0 5.1 %all-to-all-start.2 = ((bf16[8,192,256]{2,1,0:T(8,128)(2,1)}), bf16[8,192,256]{2,1,0:T(8,128)(2,1)S(1)}, u32[]{:S(2)}, u32[]{:S(2)}) async-start(bf16[8,192,256]{2,1,0:T(8,128)(2,1)} %copy-done.3), calls=%async_computation.2 | async-start | bytes 1572864 | tf_op jit(solution)/shard_map/all_to_all | solution.py:366
  92.1 1.0 collective-permute-start.18
  93.1 1.3 collective-permute-start.19
  94.9 3.0 %collective-permute-done.18.refs_11_ = bf16[384,256]{1,0:T(8,128)(2,1)} collective-permute-done((bf16[384,256]{1,0:T(8,128)(2,1)S(1)}, bf16[384,256]{1,0:T(8,128)(2,1)}, u32[]{:S(2)}, u32[]{:S(2)}) %collective-permute-start.18) | collective-permute-done | bytes 196640 | tf_op jit(solution)/shard_map/ppermute | solution.py:362
  99.9 3.7 %collective-permute-start.9 = (bf16[2,256,256]{2,1,0:T(8,128)(2,1)}, bf16[2,256,256]{2,1,0:T(8,128)(2,1)S(1)}, u32[]{:S(2)}, u32[]{:S(2)}) collective-permute-start(bf16[2,256,256]{2,1,0:T(8,128)(2,1)} %get-tuple-element.17), channel_id=1, source_target_pairs={{0,2},{8,14},{1,3},{9,15},{2,0},{10,12},{3,1},{11,13},{4,6},{12,10... | collective-permute-start | bytes 786440 | tf_op jit(solution)/shard_map/ppermute | solution.py:362
  104.3 14.3 %collective-permute-start.11 = (bf16[2,256,256]{2,1,0:T(8,128)(2,1)S(1)}, bf16[2,256,256]{2,1,0:T(8,128)(2,1)S(1)}, u32[]{:S(2)}, u32[]{:S(2)}) collective-permute-start(bf16[2,256,256]{2,1,0:T(8,128)(2,1)S(1)} %collective-permute-done.7.refs_0_), channel_id=1, source_target_pairs={{0,8},{8,0},{1,9},{9,1},{2,10},{10,2},{3,11},{11,3},{4,12},{12,4},... | collective-permute-start | bytes 786440 | tf_op jit(solution)/shard_map/ppermute | solution.py:352
  118.6 0.9 collective-permute-start.12
  120.2 2.1 %collective-permute-start.13 = (bf16[2,256,256]{2,1,0:T(8,128)(2,1)S(1)}, bf16[2,256,256]{2,1,0:T(8,128)(2,1)}, u32[]{:S(2)}, u32[]{:S(2)}) collective-permute-start(bf16[2,256,256]{2,1,0:T(8,128)(2,1)S(1)} %collective-permute-done.9.refs_2_), channel_id=1, source_target_pairs={{0,8},{8,0},{1,9},{9,1},{2,10},{10,2},{3,11},{11,3},{4,12},{12,4},... | collective-permute-start | bytes 786440 | tf_op jit(solution)/shard_map/ppermute | solution.py:352
  123.1 1.7 %collective-permute-start.14 = (bf16[2,256,256]{2,1,0:T(8,128)(2,1)S(1)}, bf16[2,256,256]{2,1,0:T(8,128)(2,1)}, u32[]{:S(2)}, u32[]{:S(2)}) collective-permute-start(bf16[2,256,256]{2,1,0:T(8,128)(2,1)S(1)} %collective-permute-done.10.refs_3_), channel_id=1, source_target_pairs={{0,8},{8,0},{1,9},{9,1},{2,10},{10,2},{3,11},{11,3},{4,12},{12,4},... | collective-permute-start | bytes 786440 | tf_op jit(solution)/shard_map/ppermute | solution.py:352
  127.2 9.0 %all-to-all-start.3 = ((f32[128,1,128]{2,1,0:T(1,128)}), f32[128,1,128]{2,1,0:T(1,128)S(1)}, u32[]{:S(2)}, u32[]{:S(2)}) async-start(f32[128,1,128]{2,1,0:T(1,128)} %bitcast.12), calls=%async_computation.3 | async-start | bytes 131072 | tf_op jit(solution)/shard_map/all_to_all | solution.py:366
  136.3 1.2 copy-done.1
  137.4 2.8 %shard_map.103 = bf16[3,384,384]{2,1,0:T(8,128)(2,1)} custom-call(f32[3,128,1152]{2,1,0:T(8,128)} %get-tuple-element.12.a_ref, bf16[3,128,1152]{2,1,0:T(8,128)(2,1)S(1)} %copy-done.1), custom_call_target="tpu_custom_call" | custom-call | tf_op jit(solution)/shard_map/pallas_call | solution.py:403
  141.0 0.9 copy-done.5
  141.9 0.9 copy-done.7
  142.9 0.9 copy-done.11
  143.8 0.9 copy-done.13
  144.7 0.9 copy-done.15
  145.7 0.9 copy-done.17
  146.6 2.9 %shard_map.105 = bf16[256,384]{1,0:T(8,128)(2,1)} custom-call(s32[1]{0:T(128)} %bitcast.co_ref, bf16[256,256]{1,0:T(8,128)(2,1)S(1)} %shard_map.104.ga_ref.g_ref, bf16[384,256]{1,0:T(8,128)(2,1)} %get-tuple-element.25.w_ref, bf16[2,256,256]{2,1,0:T(8,128)(2,1)S(1)} %collective-permute-done.7.refs_0_, bf16[2,256,256]{2,1,0:T(8,128)(2,1)S(1)} %copy-done.5, ...), custom_call_target="tpu_custom_call" | custom-call | tf_op jit(solution)/shard_map/pallas_call | solution.py:400
  (93 shorter events, 12.3 us)
Async XLA Ops:
  4.0 20.5 %all-to-all-start = ((bf16[8,256,256]{2,1,0:T(8,128)(2,1)}), bf16[8,256,256]{2,1,0:T(8,128)(2,1)S(1)}, u32[]{:S(2)}, u32[]{:S(2)}) async-start(bf16[8,256,256]{2,1,0:T(8,128)(2,1)} %kv.1), calls=%async_computation | async-start | bytes 2097152 | tf_op jit(solution)/shard_map/all_to_all | solution.py:366
  9.7 3.9 %collective-permute-start.2 = (bf16[3,384,384]{2,1,0:T(8,128)(2,1)S(1)}, bf16[3,384,384]{2,1,0:T(8,128)(2,1)}, u32[]{:S(2)}, u32[]{:S(2)}) collective-permute-start(bf16[3,384,384]{2,1,0:T(8,128)(2,1)S(1)} %copy-done.20), channel_id=1, source_target_pairs={{0,8},{8,0},{1,9},{9,1},{2,10},{10,2},{3,11},{11,3},{4,12},{12,4},... | collective-permute-start | bytes 2654216 | tf_op jit(solution)/shard_map/ppermute | solution.py:352
  9.8 3.8 %collective-permute-start.3 = (bf16[3,384,384]{2,1,0:T(8,128)(2,1)}, bf16[3,384,384]{2,1,0:T(8,128)(2,1)}, u32[]{:S(2)}, u32[]{:S(2)}) collective-permute-start(bf16[3,384,384]{2,1,0:T(8,128)(2,1)} %oo.1), channel_id=1, source_target_pairs={{0,8},{8,0},{1,9},{9,1},{2,10},{10,2},{3,11},{11,3},{4,12},{12,4},... | collective-permute-start | bytes 2654216 | tf_op jit(solution)/shard_map/ppermute | solution.py:352
  10.3 3.2 %collective-permute-start.1 = (f32[3,18,128]{2,1,0:T(8,128)S(1)}, f32[3,18,128]{2,1,0:T(8,128)S(1)}, u32[]{:S(2)}, u32[]{:S(2)}) collective-permute-start(f32[3,18,128]{2,1,0:T(8,128)S(1)} %copy.17.small_o), channel_id=1, source_target_pairs={{0,8},{8,0},{1,9},{9,1},{2,10},{10,2},{3,11},{11,3},{4,12},{12,4},... | collective-permute-start | bytes 82952 | tf_op jit(solution)/shard_map/ppermute | solution.py:352
  11.3 13.1 %copy-start.25 = (s32[128]{0:T(128)}, s32[128]{0:T(128)S(1)}, u32[]{:S(2)}) copy-start(s32[128]{0:T(128)S(1)} %pad_add_fusion.ints_o) | copy-start | bytes 1540
  11.3 2.2 %collective-permute-start = (s32[128]{0:T(128)S(1)}, s32[128]{0:T(128)S(1)}, u32[]{:S(2)}, u32[]{:S(2)}) collective-permute-start(s32[128]{0:T(128)S(1)} %pad_add_fusion.ints_o), channel_id=1, source_target_pairs={{0,8},{8,0},{1,9},{9,1},{2,10},{10,2},{3,11},{11,3},{4,12},{12,4},... | collective-permute-start | bytes 1544 | tf_op jit(solution)/shard_map/ppermute | solution.py:352
  13.6 10.9 %copy-start.26 = (s32[128]{0:T(128)}, s32[128]{0:T(128)S(1)}, u32[]{:S(2)}) copy-start(s32[128]{0:T(128)S(1)} %collective-permute-done.ints_p) | copy-start | bytes 1540
  53.3 21.2 %all-to-all-start.1 = ((bf16[8,256,256]{2,1,0:T(8,128)(2,1)}), bf16[8,256,256]{2,1,0:T(8,128)(2,1)S(1)}, u32[]{:S(2)}, u32[]{:S(2)}) async-start(bf16[8,256,256]{2,1,0:T(8,128)(2,1)} %bitcast.25), calls=%async_computation.1 | async-start | bytes 2097152 | tf_op jit(solution)/shard_map/all_to_all | solution.py:366
  65.6 9.0 %collective-permute-start.5 = (bf16[8,192,256]{2,1,0:T(8,128)(2,1)}, bf16[8,192,256]{2,1,0:T(8,128)(2,1)}, u32[]{:S(2)}, u32[]{:S(2)}) collective-permute-start(bf16[8,192,256]{2,1,0:T(8,128)(2,1)} %get-tuple-element.16), channel_id=1, source_target_pairs={{0,8},{8,0},{1,9},{9,1},{2,10},{10,2},{3,11},{11,3},{4,12},{12,4},... | collective-permute-start | bytes 2359304 | tf_op jit(solution)/shard_map/ppermute | solution.py:352
  65.6 59.9 %collective-permute-start.4 = (bf16[3,128,1152]{2,1,0:T(8,128)(2,1)}, bf16[3,128,1152]{2,1,0:T(8,128)(2,1)S(1)}, u32[]{:S(2)}, u32[]{:S(2)}) collective-permute-start(bf16[3,128,1152]{2,1,0:T(8,128)(2,1)} %get-tuple-element.13), channel_id=1, source_target_pairs={{0,8},{8,0},{1,9},{9,1},{2,10},{10,2},{3,11},{11,3},{4,12},{12,4},... | collective-permute-start | bytes 2654216 | tf_op jit(solution)/shard_map/ppermute | solution.py:352
  66.1 15.1 %copy-start.2 = (bf16[8,192,256]{2,1,0:T(8,128)(2,1)S(1)}, bf16[8,192,256]{2,1,0:T(8,128)(2,1)}, u32[]{:S(2)}) copy-start(bf16[8,192,256]{2,1,0:T(8,128)(2,1)} %get-tuple-element.15.xa_ref) | copy-start | bytes 2359300
  68.2 24.9 %collective-permute-start.15 = (bf16[384,256]{1,0:T(8,128)(2,1)}, bf16[384,256]{1,0:T(8,128)(2,1)S(1)}, u32[]{:S(2)}, u32[]{:S(2)}) collective-permute-start(bf16[384,256]{1,0:T(8,128)(2,1)} %get-tuple-element.24), channel_id=1, source_target_pairs={{8,12},{9,13},{10,14},{11,15},{12,8},{13,9},{14,10},{15,11},{24,28... | collective-permute-start | bytes 589832 | tf_op jit(solution)/shard_map/ppermute | solution.py:362
  68.9 25.5 %collective-permute-start.16 = (bf16[384,256]{1,0:T(8,128)(2,1)}, bf16[384,256]{1,0:T(8,128)(2,1)}, u32[]{:S(2)}, u32[]{:S(2)}) collective-permute-start(bf16[384,256]{1,0:T(8,128)(2,1)} %get-tuple-element.23), channel_id=1, source_target_pairs={{0,1},{8,13},{1,2},{9,14},{2,3},{10,15},{3,0},{11,12},{4,5},{12,9}... | collective-permute-start | bytes 589832 | tf_op jit(solution)/shard_map/ppermute | solution.py:362
  70.9 23.6 %collective-permute-start.17 = (bf16[384,256]{1,0:T(8,128)(2,1)S(1)}, bf16[384,256]{1,0:T(8,128)(2,1)}, u32[]{:S(2)}, u32[]{:S(2)}) collective-permute-start(bf16[384,256]{1,0:T(8,128)(2,1)S(1)} %get-tuple-element.22), channel_id=1, source_target_pairs={{0,2},{8,14},{1,3},{9,15},{2,0},{10,12},{3,1},{11,13},{4,6},{12,10... | collective-permute-start | bytes 589832 | tf_op jit(solution)/shard_map/ppermute | solution.py:362
  74.6 6.6 %collective-permute-start.6 = (bf16[256,256]{1,0:T(8,128)(2,1)S(1)}, bf16[256,256]{1,0:T(8,128)(2,1)S(1)}, u32[]{:S(2)}, u32[]{:S(2)}) collective-permute-start(bf16[256,256]{1,0:T(8,128)(2,1)S(1)} %shard_map.104.ga_ref.g_ref), channel_id=1, source_target_pairs={{0,8},{8,0},{1,9},{9,1},{2,10},{10,2},{3,11},{11,3},{4,12},{12,4},... | collective-permute-start | bytes 393224 | tf_op jit(solution)/shard_map/ppermute | solution.py:352
  87.0 39.4 %all-to-all-start.2 = ((bf16[8,192,256]{2,1,0:T(8,128)(2,1)}), bf16[8,192,256]{2,1,0:T(8,128)(2,1)S(1)}, u32[]{:S(2)}, u32[]{:S(2)}) async-start(bf16[8,192,256]{2,1,0:T(8,128)(2,1)} %copy-done.3), calls=%async_computation.2 | async-start | bytes 1572864 | tf_op jit(solution)/shard_map/all_to_all | solution.py:366
  92.1 5.8 %collective-permute-start.18 = (bf16[384,256]{1,0:T(8,128)(2,1)S(1)}, bf16[384,256]{1,0:T(8,128)(2,1)}, u32[]{:S(2)}, u32[]{:S(2)}) collective-permute-start(bf16[384,256]{1,0:T(8,128)(2,1)S(1)} %get-tuple-element.21), channel_id=1, source_target_pairs={{0,3},{8,15},{1,0},{9,12},{2,1},{10,13},{3,2},{11,14},{4,7},{12,11... | collective-permute-start | bytes 589832 | tf_op jit(solution)/shard_map/ppermute | solution.py:362
  93.1 11.2 %copy-start.21 = (bf16[384,256]{1,0:T(8,128)(2,1)}, bf16[384,256]{1,0:T(8,128)(2,1)S(1)}, u32[]{:S(2)}) copy-start(bf16[384,256]{1,0:T(8,128)(2,1)S(1)} %collective-permute-done.15.refs_8_) | copy-start | bytes 589828
  93.1 5.4 %collective-permute-start.19 = (bf16[384,256]{1,0:T(8,128)(2,1)S(1)}, bf16[384,256]{1,0:T(8,128)(2,1)S(1)}, u32[]{:S(2)}, u32[]{:S(2)}) collective-permute-start(bf16[384,256]{1,0:T(8,128)(2,1)S(1)} %collective-permute-done.15.refs_8_), channel_id=1, source_target_pairs={{0,8},{8,0},{1,9},{9,1},{2,10},{10,2},{3,11},{11,3},{4,12},{12,4},... | collective-permute-start | bytes 589832 | tf_op jit(solution)/shard_map/ppermute | solution.py:352
  94.4 4.9 %collective-permute-start.20 = (bf16[384,256]{1,0:T(8,128)(2,1)}, bf16[384,256]{1,0:T(8,128)(2,1)S(1)}, u32[]{:S(2)}, u32[]{:S(2)}) collective-permute-start(bf16[384,256]{1,0:T(8,128)(2,1)} %collective-permute-done.16.refs_9_), channel_id=1, source_target_pairs={{0,8},{8,0},{1,9},{9,1},{2,10},{10,2},{3,11},{11,3},{4,12},{12,4},... | collective-permute-start | bytes 589832 | tf_op jit(solution)/shard_map/ppermute | solution.py:352
  94.4 9.1 %collective-permute-start.21 = (bf16[384,256]{1,0:T(8,128)(2,1)}, bf16[384,256]{1,0:T(8,128)(2,1)S(1)}, u32[]{:S(2)}, u32[]{:S(2)}) collective-permute-start(bf16[384,256]{1,0:T(8,128)(2,1)} %collective-permute-done.17.refs_10_), channel_id=1, source_target_pairs={{0,8},{8,0},{1,9},{9,1},{2,10},{10,2},{3,11},{11,3},{4,12},{12,4},... | collective-permute-start | bytes 589832 | tf_op jit(solution)/shard_map/ppermute | solution.py:352
  97.9 6.4 %collective-permute-start.7 = (bf16[2,256,256]{2,1,0:T(8,128)(2,1)}, bf16[2,256,256]{2,1,0:T(8,128)(2,1)S(1)}, u32[]{:S(2)}, u32[]{:S(2)}) collective-permute-start(bf16[2,256,256]{2,1,0:T(8,128)(2,1)} %get-tuple-element.17), channel_id=1, source_target_pairs={{8,12},{9,13},{10,14},{11,15},{12,8},{13,9},{14,10},{15,11},{24,28... | collective-permute-start | bytes 786440 | tf_op jit(solution)/shard_map/ppermute | solution.py:362
  99.2 19.4 %collective-permute-start.8 = (bf16[2,256,256]{2,1,0:T(8,128)(2,1)}, bf16[2,256,256]{2,1,0:T(8,128)(2,1)S(1)}, u32[]{:S(2)}, u32[]{:S(2)}) collective-permute-start(bf16[2,256,256]{2,1,0:T(8,128)(2,1)} %get-tuple-element.17), channel_id=1, source_target_pairs={{0,1},{8,13},{1,2},{9,14},{2,3},{10,15},{3,0},{11,12},{4,5},{12,9}... | collective-permute-start | bytes 786440 | tf_op jit(solution)/shard_map/ppermute | solution.py:362
  99.9 20.3 %collective-permute-start.9 = (bf16[2,256,256]{2,1,0:T(8,128)(2,1)}, bf16[2,256,256]{2,1,0:T(8,128)(2,1)S(1)}, u32[]{:S(2)}, u32[]{:S(2)}) collective-permute-start(bf16[2,256,256]{2,1,0:T(8,128)(2,1)} %get-tuple-element.17), channel_id=1, source_target_pairs={{0,2},{8,14},{1,3},{9,15},{2,0},{10,12},{3,1},{11,13},{4,6},{12,10... | collective-permute-start | bytes 786440 | tf_op jit(solution)/shard_map/ppermute | solution.py:362
  104.3 18.8 %collective-permute-start.10 = (bf16[2,256,256]{2,1,0:T(8,128)(2,1)}, bf16[2,256,256]{2,1,0:T(8,128)(2,1)S(1)}, u32[]{:S(2)}, u32[]{:S(2)}) collective-permute-start(bf16[2,256,256]{2,1,0:T(8,128)(2,1)} %get-tuple-element.17), channel_id=1, source_target_pairs={{0,3},{8,15},{1,0},{9,12},{2,1},{10,13},{3,2},{11,14},{4,7},{12,11... | collective-permute-start | bytes 786440 | tf_op jit(solution)/shard_map/ppermute | solution.py:362
  104.3 35.9 %collective-permute-start.11 = (bf16[2,256,256]{2,1,0:T(8,128)(2,1)S(1)}, bf16[2,256,256]{2,1,0:T(8,128)(2,1)S(1)}, u32[]{:S(2)}, u32[]{:S(2)}) collective-permute-start(bf16[2,256,256]{2,1,0:T(8,128)(2,1)S(1)} %collective-permute-done.7.refs_0_), channel_id=1, source_target_pairs={{0,8},{8,0},{1,9},{9,1},{2,10},{10,2},{3,11},{11,3},{4,12},{12,4},... | collective-permute-start | bytes 786440 | tf_op jit(solution)/shard_map/ppermute | solution.py:352
  118.6 22.3 %collective-permute-start.12 = (bf16[2,256,256]{2,1,0:T(8,128)(2,1)S(1)}, bf16[2,256,256]{2,1,0:T(8,128)(2,1)}, u32[]{:S(2)}, u32[]{:S(2)}) collective-permute-start(bf16[2,256,256]{2,1,0:T(8,128)(2,1)S(1)} %collective-permute-done.8.refs_1_), channel_id=1, source_target_pairs={{0,8},{8,0},{1,9},{9,1},{2,10},{10,2},{3,11},{11,3},{4,12},{12,4},... | collective-permute-start | bytes 786440 | tf_op jit(solution)/shard_map/ppermute | solution.py:352
  120.2 20.7 %collective-permute-start.13 = (bf16[2,256,256]{2,1,0:T(8,128)(2,1)S(1)}, bf16[2,256,256]{2,1,0:T(8,128)(2,1)}, u32[]{:S(2)}, u32[]{:S(2)}) collective-permute-start(bf16[2,256,256]{2,1,0:T(8,128)(2,1)S(1)} %collective-permute-done.9.refs_2_), channel_id=1, source_target_pairs={{0,8},{8,0},{1,9},{9,1},{2,10},{10,2},{3,11},{11,3},{4,12},{12,4},... | collective-permute-start | bytes 786440 | tf_op jit(solution)/shard_map/ppermute | solution.py:352
  123.1 17.9 %collective-permute-start.14 = (bf16[2,256,256]{2,1,0:T(8,128)(2,1)S(1)}, bf16[2,256,256]{2,1,0:T(8,128)(2,1)}, u32[]{:S(2)}, u32[]{:S(2)}) collective-permute-start(bf16[2,256,256]{2,1,0:T(8,128)(2,1)S(1)} %collective-permute-done.10.refs_3_), channel_id=1, source_target_pairs={{0,8},{8,0},{1,9},{9,1},{2,10},{10,2},{3,11},{11,3},{4,12},{12,4},... | collective-permute-start | bytes 786440 | tf_op jit(solution)/shard_map/ppermute | solution.py:352
  126.4 13.8 %collective-permute-start.22 = (bf16[384,256]{1,0:T(8,128)(2,1)}, bf16[384,256]{1,0:T(8,128)(2,1)}, u32[]{:S(2)}, u32[]{:S(2)}) collective-permute-start(bf16[384,256]{1,0:T(8,128)(2,1)} %collective-permute-done.18.refs_11_), channel_id=1, source_target_pairs={{0,8},{8,0},{1,9},{9,1},{2,10},{10,2},{3,11},{11,3},{4,12},{12,4},... | collective-permute-start | bytes 589832 | tf_op jit(solution)/shard_map/ppermute | solution.py:352
  127.2 13.0 %copy-start.18 = (f32[192,256]{1,0:T(8,128)}, f32[192,256]{1,0:T(8,128)S(1)}, u32[]{:S(2)}) copy-start(f32[192,256]{1,0:T(8,128)S(1)} %get-tuple-element.19.grad_ref) | copy-start | bytes 589828
  127.2 22.3 %all-to-all-start.3 = ((f32[128,1,128]{2,1,0:T(1,128)}), f32[128,1,128]{2,1,0:T(1,128)S(1)}, u32[]{:S(2)}, u32[]{:S(2)}) async-start(f32[128,1,128]{2,1,0:T(1,128)} %bitcast.12), calls=%async_computation.3 | async-start | bytes 131072 | tf_op jit(solution)/shard_map/all_to_all | solution.py:366
  (22 other events, 45.3 us)

commit v8 on v7

--- a/solution.py
+++ b/solution.py
@@ -309,24 +309,49 @@
     out_ref[...] = grad_ref[...] / jnp.sqrt(total / (D * KVH * 2 * HD) + 1e-06)
 
 
-def dx_kernel(co_ref, g_ref, w_ref, *refs):
-    ra, rb, wa, wb, out_ref = refs[:4], refs[4:8], refs[8:12], refs[12:16], refs[16]
-
-    def total(me, near, far, w_near, w_far):
-        acc = lax.dot_general(g_ref[...], w_ref[...], NT, preferred_element_type=jnp.float32)
-        for k in range(4):
-            if k > 0:
-                acc += lax.dot_general(near[k][me], w_near[k][...], NT, preferred_element_type=jnp.float32)
-            acc += lax.dot_general(far[k][me], w_far[k][...], NT, preferred_element_type=jnp.float32)
-        out_ref[...] = acc.astype(jnp.bfloat16)
-
-    @pl.when(co_ref[0] == 0)
-    def _():
-        total(0, ra, rb, wa, wb)
-
-    @pl.when(co_ref[0] == 1)
-    def _():
-        total(1, rb, ra, wb, wa)
+def dx_kernel(co_ref, g_ref, *refs):
+    ra, rb, wb, far = refs[:4], refs[4:8], refs[8:12], refs[12:17]
+    out_ref, w_s, acc_s, sem = refs[17:]
+    copies = [pltpu.make_async_copy(w, w_s.at[k], sem.at[k]) for k, w in enumerate(far)]
+    for copy in copies:
+        copy.start()
+
+    def add(acc, me, skip, grads, weights):
+        for k in range(skip, 4):
+            acc += lax.dot_general(grads[k][me], weights(k), NT, preferred_element_type=jnp.float32)
+        return acc
+
+    for me in range(2):
+        @pl.when(co_ref[0] == me)
+        def _():
+            zero = jnp.zeros((256, 384), jnp.float32)
+            acc_s[...] = add(zero, me, me, rb, lambda k: wb[k][...])
+
+    for copy in copies:
+        copy.wait()
+    for me in range(2):
+        @pl.when(co_ref[0] == me)
+        def _():
+            acc = acc_s[...] + lax.dot_general(
+                g_ref[...], w_s[4], NT, preferred_element_type=jnp.float32
+            )
+            out_ref[...] = add(acc, me, 1 - me, ra, lambda k: w_s[k]).astype(jnp.bfloat16)
+
+
+def input_grads(co, g, ra, rb, wb, wa, w_own):
+    return pl.pallas_call(
+        dx_kernel,
+        out_shape=jax.ShapeDtypeStruct((256, 384), jnp.bfloat16),
+        in_specs=[SM] + [VM] * 13 + [ANY] * 5,
+        out_specs=VM,
+        scratch_shapes=[
+            pltpu.VMEM((5, 384, 256), jnp.bfloat16),
+            pltpu.VMEM((256, 384), jnp.float32),
+            pltpu.SemaphoreType.DMA((5,)),
+        ],
+        compiler_params=pltpu.CompilerParams(vmem_limit_bytes=20 << 20),
+        name="dx",
+    )(co, *map(vm, [g] + ra + rb + wb), *wa, w_own)
 
 
 def dq_kernel(a_ref, b_ref, out_ref):
@@ -397,9 +422,7 @@
     ra = [split_shift(pair, j) for j in range(4)]
     rb = [swap(r) for r in ra]
     wb = [swap(w) for w in wa]
-    (d_x,) = call(dx_kernel, [SM] + [VM] * 18, ((256, 384), bf), near=False)(
-        co1, vm(g), w_own, *map(vm, ra + rb), *wa, *map(vm, wb)
-    )
+    d_x = input_grads(co1, g, ra, rb, wb, wa, w_own)
     (d_queries,) = call(dq_kernel, [VM] * 2, ((NL, 384, 384), bf), near=False)(dqo, vm(swap(dqp)))
     (d_w,) = call(scale_kernel, [VM] * 2, ((192, 256), f32), near=False)(vm(grad), vm(parts.reshape(128, HD)))
     return (d_queries, d_x, d_w)

time: 151 us -> 146 us (0.967)
  local copies, waits for them, and re-layouts: 15.7 us -> 6.67 us
  waiting for transfers between devices: 16.7 us -> 18.5 us
    unnamed x54 -> x38, local copies, waits for them, and re-layouts: 13.5 us -> 4.34 us
    all_to_all x4, waiting for transfers between devices: 10.9 us -> 13.3 us  [exchange(): return lax.all_to_all(a, axes, 0, 0)]
  transfers between devices with their start and end apart: 27 -> 27, of which waited for: 4 -> 5; matrix products, arithmetic and copies ran while one was open for 2% -> 2% of each run, Pallas kernels for 10% -> 11%
where the time goes in v8:
time: 146 us
  starting transfers between devices  70.1 us (48%)
  Pallas kernels  48.7 us (33%)
  waiting for transfers between devices  18.5 us (13%)
  local copies, waits for them, and re-layouts  6.67 us (5%)
  between operations  1.57 us (1%)
    ppermute x15, starting transfers between devices, swap(): return lax.ppermute(a, 'co', [(0, 1), (1, 0)])  29.5 us
    all_to_all x4, starting transfers between devices, exchange(): return lax.all_to_all(a, axes, 0, 0)  28.9 us
    pallas_call x1, Pallas kernels, attn(): pl.pallas_call(functools.partial(attn_kernel, groups, unroll, late), out_...  28.8 us
    all_to_all x4, waiting for transfers between devices, exchange(): return lax.all_to_all(a, axes, 0, 0)  13.3 us
    ppermute x8, starting transfers between devices, split_shift(): return lax.ppermute(a, ('co', 'xh', 'z'), perm)  11.7 us
    pallas_call x1, Pallas kernels, weight_parts(): pl.pallas_call(dw_kernel, out_shape=(jax.ShapeDtypeStruct((8, 192, 256),...  4.92 us
    unnamed x38, local copies, waits for them, and re-layouts  4.34 us
    pallas_call x1, Pallas kernels, input_grads(): pl.pallas_call(dx_kernel, out_shape=jax.ShapeDtypeStruct((256, 384), jnp....  3.96 us
  transfers between devices with their start and end apart: 27, of which 5 were waited for; matrix products, arithmetic and copies ran while one was open for 2% of the time, Pallas kernels for 11%

profile of v8, /device:TPU:0, one launch (start us, length us, event | category | flops | bytes accessed | tf_op | source)
XLA Modules:
  0.0 145.5 jit_solution(8699189378444417296)
XLA Ops:
  0.6 3.3 %kv.1 = bf16[8,256,256]{2,1,0:T(8,128)(2,1)} custom-call(bf16[256,3072]{1,0:T(8,128)(2,1)} %x_ref.3, bf16[3072,256]{1,0:T(8,128)(2,1)} %w_ref.1), custom_call_target="tpu_custom_call" | custom-call | tf_op jit(solution)/shard_map/kv/pallas_call | solution.py:223
  4.0 5.7 %all-to-all-start = ((bf16[8,256,256]{2,1,0:T(8,128)(2,1)}), bf16[8,256,256]{2,1,0:T(8,128)(2,1)S(1)}, u32[]{:S(2)}, u32[]{:S(2)}) async-start(bf16[8,256,256]{2,1,0:T(8,128)(2,1)} %kv.1), calls=%async_computation | async-start | bytes 2097152 | tf_op jit(solution)/shard_map/all_to_all | solution.py:391
  11.7 1.8 %collective-permute-done.ints_p = s32[128]{0:T(128)S(1)} collective-permute-done((s32[128]{0:T(128)S(1)}, s32[128]{0:T(128)S(1)}, u32[]{:S(2)}, u32[]{:S(2)}) %collective-permute-start) | collective-permute-done | bytes 544 | tf_op jit(solution)/shard_map/ppermute | solution.py:377
  13.6 10.9 %all-to-all-done = bf16[8,256,256]{2,1,0:T(8,128)(2,1)S(1)} async-done(((bf16[8,256,256]{2,1,0:T(8,128)(2,1)}), bf16[8,256,256]{2,1,0:T(8,128)(2,1)S(1)}, u32[]{:S(2)}, u32[]{:S(2)}) %all-to-all-start) | async-done | bytes 1048608 | tf_op jit(solution)/shard_map/all_to_all | solution.py:391
  24.4 28.8 %attn.1 = (bf16[16,128,256]{2,1,0:T(8,128)(2,1)}, f32[3,128,1152]{2,1,0:T(8,128)}, bf16[3,128,1152]{2,1,0:T(8,128)(2,1)}) custom-call(s32[128]{0:T(128)} %copy-done.17, s32[128]{0:T(128)} %copy-done.18, s32[1]{0:T(128)} %bitcast.co_ref, f32[3,18,128]{2,1,0:T(8,128)S(1)} %copy.17.small_o, f32[3,18,128]{2,1,0:T(8,128)S(1)} %collective-permute-done.1.small_p, ...), custom_call_target="tpu_custom_call" | custom-call | tf_op jit(solution)/shard_map/attn/pallas_call | solution.py:169
  53.2 9.2 %all-to-all-start.1 = ((bf16[8,256,256]{2,1,0:T(8,128)(2,1)}), bf16[8,256,256]{2,1,0:T(8,128)(2,1)S(1)}, u32[]{:S(2)}, u32[]{:S(2)}) async-start(bf16[8,256,256]{2,1,0:T(8,128)(2,1)} %bitcast.25), calls=%async_computation.1 | async-start | bytes 2097152 | tf_op jit(solution)/shard_map/all_to_all | solution.py:391
  62.4 3.1 %xt.1 = (bf16[8,192,256]{2,1,0:T(8,128)(2,1)}, bf16[8,192,256]{2,1,0:T(8,128)(2,1)}) custom-call(s32[1]{0:T(128)} %bitcast.co_ref, bf16[256,3072]{1,0:T(8,128)(2,1)} %x_ref.3), custom_call_target="tpu_custom_call" | custom-call | tf_op jit(solution)/shard_map/xt/pallas_call | solution.py:255
  66.0 2.2 %dynamic-slice_bitcast_fusion = (bf16[384,256]{1,0:T(8,128)(2,1)S(1)}, bf16[384,256]{1,0:T(8,128)(2,1)}, bf16[384,256]{1,0:T(8,128)(2,1)}, bf16[384,256]{1,0:T(8,128)(2,1)}, bf16[384,256]{1,0:T(8,128)(2,1)}) fusion(bf16[8,384,256]{2,1,0:T(8,128)(2,1)} %bitcast.24, s32[]{:T(128)S(6)} %select_n.54, s32[]{:T(128)S(6)} %select_n.53, s32[]{:T(128)S(6)} %select_n.51, ...), kind=kLoop, calls=%fused_computation | loop fusion | bytes 1966100 | tf_op jit(solution)/shard_map/jit(dynamic_index_in_dim)/squeeze | solution.py:406
  68.9 2.0 %collective-permute-start.17 = (bf16[384,256]{1,0:T(8,128)(2,1)}, bf16[384,256]{1,0:T(8,128)(2,1)S(1)}, u32[]{:S(2)}, u32[]{:S(2)}) collective-permute-start(bf16[384,256]{1,0:T(8,128)(2,1)} %get-tuple-element.24), channel_id=1, source_target_pairs={{0,1},{8,13},{1,2},{9,14},{2,3},{10,15},{3,0},{11,12},{4,5},{12,9}... | collective-permute-start | bytes 589832 | tf_op jit(solution)/shard_map/ppermute | solution.py:387
  70.9 3.6 %collective-permute-start.19 = (bf16[384,256]{1,0:T(8,128)(2,1)}, bf16[384,256]{1,0:T(8,128)(2,1)}, u32[]{:S(2)}, u32[]{:S(2)}) collective-permute-start(bf16[384,256]{1,0:T(8,128)(2,1)} %get-tuple-element.23), channel_id=1, source_target_pairs={{0,2},{8,14},{1,3},{9,15},{2,0},{10,12},{3,1},{11,13},{4,6},{12,10... | collective-permute-start | bytes 589832 | tf_op jit(solution)/shard_map/ppermute | solution.py:387
  74.6 5.6 %collective-permute-start.6 = (bf16[256,256]{1,0:T(8,128)(2,1)S(1)}, bf16[256,256]{1,0:T(8,128)(2,1)S(1)}, u32[]{:S(2)}, u32[]{:S(2)}) collective-permute-start(bf16[256,256]{1,0:T(8,128)(2,1)S(1)} %shard_map.104.ga_ref.g_ref), channel_id=1, source_target_pairs={{0,8},{8,0},{1,9},{9,1},{2,10},{10,2},{3,11},{11,3},{4,12},{12,4},... | collective-permute-start | bytes 393224 | tf_op jit(solution)/shard_map/ppermute | solution.py:377
  80.2 1.0 collective-permute-done.6.gb_ref
  81.2 4.9 %dw.1 = (bf16[8,192,256]{2,1,0:T(8,128)(2,1)S(1)}, bf16[2,256,256]{2,1,0:T(8,128)(2,1)}) custom-call(s32[1]{0:T(128)} %bitcast.co_ref, bf16[8,192,256]{2,1,0:T(8,128)(2,1)S(1)} %copy-done, bf16[8,192,256]{2,1,0:T(8,128)(2,1)} %collective-permute-done.5.xb_ref, bf16[256,256]{1,0:T(8,128)(2,1)S(1)} %shard_map.104.ga_ref.g_ref, ...), custom_call_target="tpu_custom_call" | custom-call | tf_op jit(solution)/shard_map/dw/pallas_call | solution.py:281
  86.2 0.9 copy-done.1
  87.0 5.1 %all-to-all-start.2 = ((bf16[8,192,256]{2,1,0:T(8,128)(2,1)}), bf16[8,192,256]{2,1,0:T(8,128)(2,1)S(1)}, u32[]{:S(2)}, u32[]{:S(2)}) async-start(bf16[8,192,256]{2,1,0:T(8,128)(2,1)} %copy-done.1), calls=%async_computation.2 | async-start | bytes 1572864 | tf_op jit(solution)/shard_map/all_to_all | solution.py:391
  92.1 1.1 collective-permute-start.21
  93.2 1.2 collective-permute-start.16
  94.6 0.7 copy-done.2
  95.7 2.3 %collective-permute-done.21.refs_15_ = bf16[384,256]{1,0:T(8,128)(2,1)} collective-permute-done((bf16[384,256]{1,0:T(8,128)(2,1)S(1)}, bf16[384,256]{1,0:T(8,128)(2,1)}, u32[]{:S(2)}, u32[]{:S(2)}) %collective-permute-start.21) | collective-permute-done | bytes 196640 | tf_op jit(solution)/shard_map/ppermute | solution.py:387
  100.0 3.7 %collective-permute-start.9 = (bf16[2,256,256]{2,1,0:T(8,128)(2,1)}, bf16[2,256,256]{2,1,0:T(8,128)(2,1)S(1)}, u32[]{:S(2)}, u32[]{:S(2)}) collective-permute-start(bf16[2,256,256]{2,1,0:T(8,128)(2,1)} %get-tuple-element.17), channel_id=1, source_target_pairs={{0,2},{8,14},{1,3},{9,15},{2,0},{10,12},{3,1},{11,13},{4,6},{12,10... | collective-permute-start | bytes 786440 | tf_op jit(solution)/shard_map/ppermute | solution.py:387
  103.7 0.7 copy-done.8
  104.4 14.2 %collective-permute-start.11 = (bf16[2,256,256]{2,1,0:T(8,128)(2,1)S(1)}, bf16[2,256,256]{2,1,0:T(8,128)(2,1)}, u32[]{:S(2)}, u32[]{:S(2)}) collective-permute-start(bf16[2,256,256]{2,1,0:T(8,128)(2,1)S(1)} %collective-permute-done.7.refs_0_), channel_id=1, source_target_pairs={{0,8},{8,0},{1,9},{9,1},{2,10},{10,2},{3,11},{11,3},{4,12},{12,4},... | collective-permute-start | bytes 786440 | tf_op jit(solution)/shard_map/ppermute | solution.py:377
  118.6 0.9 collective-permute-start.12
  119.5 2.8 %collective-permute-start.13 = (bf16[2,256,256]{2,1,0:T(8,128)(2,1)S(1)}, bf16[2,256,256]{2,1,0:T(8,128)(2,1)}, u32[]{:S(2)}, u32[]{:S(2)}) collective-permute-start(bf16[2,256,256]{2,1,0:T(8,128)(2,1)S(1)} %collective-permute-done.9.refs_2_), channel_id=1, source_target_pairs={{0,8},{8,0},{1,9},{9,1},{2,10},{10,2},{3,11},{11,3},{4,12},{12,4},... | collective-permute-start | bytes 786440 | tf_op jit(solution)/shard_map/ppermute | solution.py:377
  122.4 2.4 %collective-permute-start.14 = (bf16[2,256,256]{2,1,0:T(8,128)(2,1)S(1)}, bf16[2,256,256]{2,1,0:T(8,128)(2,1)}, u32[]{:S(2)}, u32[]{:S(2)}) collective-permute-start(bf16[2,256,256]{2,1,0:T(8,128)(2,1)S(1)} %collective-permute-done.10.refs_3_), channel_id=1, source_target_pairs={{0,8},{8,0},{1,9},{9,1},{2,10},{10,2},{3,11},{11,3},{4,12},{12,4},... | collective-permute-start | bytes 786440 | tf_op jit(solution)/shard_map/ppermute | solution.py:377
  124.8 0.9 shard_map.105
  125.7 0.7 copy-done.10
  126.4 9.0 %all-to-all-start.3 = ((f32[128,1,128]{2,1,0:T(1,128)}), f32[128,1,128]{2,1,0:T(1,128)S(1)}, u32[]{:S(2)}, u32[]{:S(2)}) async-start(f32[128,1,128]{2,1,0:T(1,128)} %bitcast.12), calls=%async_computation.3 | async-start | bytes 131072 | tf_op jit(solution)/shard_map/all_to_all | solution.py:391
  135.4 2.8 %shard_map.103 = bf16[3,384,384]{2,1,0:T(8,128)(2,1)} custom-call(f32[3,128,1152]{2,1,0:T(8,128)} %get-tuple-element.12.a_ref, bf16[3,128,1152]{2,1,0:T(8,128)(2,1)S(1)} %collective-permute-done.4.b_ref), custom_call_target="tpu_custom_call" | custom-call | tf_op jit(solution)/shard_map/pallas_call | solution.py:426
  138.3 4.0 %dx.1 = bf16[256,384]{1,0:T(8,128)(2,1)} custom-call(s32[1]{0:T(128)} %bitcast.co_ref, bf16[256,256]{1,0:T(8,128)(2,1)S(1)} %shard_map.104.ga_ref.g_ref, bf16[2,256,256]{2,1,0:T(8,128)(2,1)S(1)} %collective-permute-done.7.refs_0_, bf16[2,256,256]{2,1,0:T(8,128)(2,1)S(1)} %collective-permute-done.8.refs_1_, ...), custom_call_target="tpu_custom_call" | custom-call | tf_op jit(solution)/shard_map/dx/pallas_call | solution.py:342
  142.3 2.4 %all-to-all-done.3 = f32[128,1,128]{2,1,0:T(1,128)S(1)} async-done(((f32[128,1,128]{2,1,0:T(1,128)}), f32[128,1,128]{2,1,0:T(1,128)S(1)}, u32[]{:S(2)}, u32[]{:S(2)}) %all-to-all-start.3) | async-done | bytes 65568 | tf_op jit(solution)/shard_map/all_to_all | solution.py:391
  144.7 0.8 shard_map.106
  (77 shorter events, 5.4 us)
Async XLA Ops:
  4.0 7.2 %copy-start.16 = (s32[3,32]{1,0:T(4,128)S(1)}, s32[3,32]{1,0:T(4,128)}, u32[]{:S(2)}) copy-start(s32[3,32]{1,0:T(4,128)} %param.15) | copy-start | bytes 1156
  4.0 20.5 %all-to-all-start = ((bf16[8,256,256]{2,1,0:T(8,128)(2,1)}), bf16[8,256,256]{2,1,0:T(8,128)(2,1)S(1)}, u32[]{:S(2)}, u32[]{:S(2)}) async-start(bf16[8,256,256]{2,1,0:T(8,128)(2,1)} %kv.1), calls=%async_computation | async-start | bytes 2097152 | tf_op jit(solution)/shard_map/all_to_all | solution.py:391
  9.6 3.9 %collective-permute-start.2 = (bf16[3,384,384]{2,1,0:T(8,128)(2,1)S(1)}, bf16[3,384,384]{2,1,0:T(8,128)(2,1)}, u32[]{:S(2)}, u32[]{:S(2)}) collective-permute-start(bf16[3,384,384]{2,1,0:T(8,128)(2,1)S(1)} %copy-done.12), channel_id=1, source_target_pairs={{0,8},{8,0},{1,9},{9,1},{2,10},{10,2},{3,11},{11,3},{4,12},{12,4},... | collective-permute-start | bytes 2654216 | tf_op jit(solution)/shard_map/ppermute | solution.py:377
  9.7 3.8 %collective-permute-start.3 = (bf16[3,384,384]{2,1,0:T(8,128)(2,1)}, bf16[3,384,384]{2,1,0:T(8,128)(2,1)}, u32[]{:S(2)}, u32[]{:S(2)}) collective-permute-start(bf16[3,384,384]{2,1,0:T(8,128)(2,1)} %oo.1), channel_id=1, source_target_pairs={{0,8},{8,0},{1,9},{9,1},{2,10},{10,2},{3,11},{11,3},{4,12},{12,4},... | collective-permute-start | bytes 2654216 | tf_op jit(solution)/shard_map/ppermute | solution.py:377
  10.3 3.2 %collective-permute-start.1 = (f32[3,18,128]{2,1,0:T(8,128)S(1)}, f32[3,18,128]{2,1,0:T(8,128)S(1)}, u32[]{:S(2)}, u32[]{:S(2)}) collective-permute-start(f32[3,18,128]{2,1,0:T(8,128)S(1)} %copy.17.small_o), channel_id=1, source_target_pairs={{0,8},{8,0},{1,9},{9,1},{2,10},{10,2},{3,11},{11,3},{4,12},{12,4},... | collective-permute-start | bytes 82952 | tf_op jit(solution)/shard_map/ppermute | solution.py:377
  11.3 13.1 %copy-start.17 = (s32[128]{0:T(128)}, s32[128]{0:T(128)S(1)}, u32[]{:S(2)}) copy-start(s32[128]{0:T(128)S(1)} %pad_add_fusion.ints_o) | copy-start | bytes 1540
  11.3 2.2 %collective-permute-start = (s32[128]{0:T(128)S(1)}, s32[128]{0:T(128)S(1)}, u32[]{:S(2)}, u32[]{:S(2)}) collective-permute-start(s32[128]{0:T(128)S(1)} %pad_add_fusion.ints_o), channel_id=1, source_target_pairs={{0,8},{8,0},{1,9},{9,1},{2,10},{10,2},{3,11},{11,3},{4,12},{12,4},... | collective-permute-start | bytes 1544 | tf_op jit(solution)/shard_map/ppermute | solution.py:377
  13.5 10.9 %copy-start.18 = (s32[128]{0:T(128)}, s32[128]{0:T(128)S(1)}, u32[]{:S(2)}) copy-start(s32[128]{0:T(128)S(1)} %collective-permute-done.ints_p) | copy-start | bytes 1540
  53.2 21.2 %all-to-all-start.1 = ((bf16[8,256,256]{2,1,0:T(8,128)(2,1)}), bf16[8,256,256]{2,1,0:T(8,128)(2,1)S(1)}, u32[]{:S(2)}, u32[]{:S(2)}) async-start(bf16[8,256,256]{2,1,0:T(8,128)(2,1)} %bitcast.25), calls=%async_computation.1 | async-start | bytes 2097152 | tf_op jit(solution)/shard_map/all_to_all | solution.py:391
  65.5 9.1 %collective-permute-start.5 = (bf16[8,192,256]{2,1,0:T(8,128)(2,1)}, bf16[8,192,256]{2,1,0:T(8,128)(2,1)}, u32[]{:S(2)}, u32[]{:S(2)}) collective-permute-start(bf16[8,192,256]{2,1,0:T(8,128)(2,1)} %get-tuple-element.16), channel_id=1, source_target_pairs={{0,8},{8,0},{1,9},{9,1},{2,10},{10,2},{3,11},{11,3},{4,12},{12,4},... | collective-permute-start | bytes 2359304 | tf_op jit(solution)/shard_map/ppermute | solution.py:377
  65.5 59.3 %collective-permute-start.4 = (bf16[3,128,1152]{2,1,0:T(8,128)(2,1)}, bf16[3,128,1152]{2,1,0:T(8,128)(2,1)S(1)}, u32[]{:S(2)}, u32[]{:S(2)}) collective-permute-start(bf16[3,128,1152]{2,1,0:T(8,128)(2,1)} %get-tuple-element.13), channel_id=1, source_target_pairs={{0,8},{8,0},{1,9},{9,1},{2,10},{10,2},{3,11},{11,3},{4,12},{12,4},... | collective-permute-start | bytes 2654216 | tf_op jit(solution)/shard_map/ppermute | solution.py:377
  66.0 15.2 %copy-start = (bf16[8,192,256]{2,1,0:T(8,128)(2,1)S(1)}, bf16[8,192,256]{2,1,0:T(8,128)(2,1)}, u32[]{:S(2)}) copy-start(bf16[8,192,256]{2,1,0:T(8,128)(2,1)} %get-tuple-element.15.xa_ref) | copy-start | bytes 2359300
  68.2 25.0 %collective-permute-start.15 = (bf16[384,256]{1,0:T(8,128)(2,1)}, bf16[384,256]{1,0:T(8,128)(2,1)S(1)}, u32[]{:S(2)}, u32[]{:S(2)}) collective-permute-start(bf16[384,256]{1,0:T(8,128)(2,1)} %get-tuple-element.25), channel_id=1, source_target_pairs={{8,12},{9,13},{10,14},{11,15},{12,8},{13,9},{14,10},{15,11},{24,28... | collective-permute-start | bytes 589832 | tf_op jit(solution)/shard_map/ppermute | solution.py:387
  68.9 25.6 %collective-permute-start.17 = (bf16[384,256]{1,0:T(8,128)(2,1)}, bf16[384,256]{1,0:T(8,128)(2,1)S(1)}, u32[]{:S(2)}, u32[]{:S(2)}) collective-permute-start(bf16[384,256]{1,0:T(8,128)(2,1)} %get-tuple-element.24), channel_id=1, source_target_pairs={{0,1},{8,13},{1,2},{9,14},{2,3},{10,15},{3,0},{11,12},{4,5},{12,9}... | collective-permute-start | bytes 589832 | tf_op jit(solution)/shard_map/ppermute | solution.py:387
  70.9 24.4 %collective-permute-start.19 = (bf16[384,256]{1,0:T(8,128)(2,1)}, bf16[384,256]{1,0:T(8,128)(2,1)}, u32[]{:S(2)}, u32[]{:S(2)}) collective-permute-start(bf16[384,256]{1,0:T(8,128)(2,1)} %get-tuple-element.23), channel_id=1, source_target_pairs={{0,2},{8,14},{1,3},{9,15},{2,0},{10,12},{3,1},{11,13},{4,6},{12,10... | collective-permute-start | bytes 589832 | tf_op jit(solution)/shard_map/ppermute | solution.py:387
  74.6 6.6 %collective-permute-start.6 = (bf16[256,256]{1,0:T(8,128)(2,1)S(1)}, bf16[256,256]{1,0:T(8,128)(2,1)S(1)}, u32[]{:S(2)}, u32[]{:S(2)}) collective-permute-start(bf16[256,256]{1,0:T(8,128)(2,1)S(1)} %shard_map.104.ga_ref.g_ref), channel_id=1, source_target_pairs={{0,8},{8,0},{1,9},{9,1},{2,10},{10,2},{3,11},{11,3},{4,12},{12,4},... | collective-permute-start | bytes 393224 | tf_op jit(solution)/shard_map/ppermute | solution.py:377
  81.2 10.9 %copy-start.13 = (bf16[384,256]{1,0:T(8,128)(2,1)S(1)}, bf16[384,256]{1,0:T(8,128)(2,1)}, u32[]{:S(2)}) copy-start(bf16[384,256]{1,0:T(8,128)(2,1)} %get-tuple-element.22) | copy-start | bytes 589828
  87.0 37.8 %all-to-all-start.2 = ((bf16[8,192,256]{2,1,0:T(8,128)(2,1)}), bf16[8,192,256]{2,1,0:T(8,128)(2,1)S(1)}, u32[]{:S(2)}, u32[]{:S(2)}) async-start(bf16[8,192,256]{2,1,0:T(8,128)(2,1)} %copy-done.1), calls=%async_computation.2 | async-start | bytes 1572864 | tf_op jit(solution)/shard_map/all_to_all | solution.py:391
  92.1 5.8 %collective-permute-start.21 = (bf16[384,256]{1,0:T(8,128)(2,1)S(1)}, bf16[384,256]{1,0:T(8,128)(2,1)}, u32[]{:S(2)}, u32[]{:S(2)}) collective-permute-start(bf16[384,256]{1,0:T(8,128)(2,1)S(1)} %copy-done.13), channel_id=1, source_target_pairs={{0,3},{8,15},{1,0},{9,12},{2,1},{10,13},{3,2},{11,14},{4,7},{12,11... | collective-permute-start | bytes 589832 | tf_op jit(solution)/shard_map/ppermute | solution.py:387
  93.2 5.4 %collective-permute-start.16 = (bf16[384,256]{1,0:T(8,128)(2,1)S(1)}, bf16[384,256]{1,0:T(8,128)(2,1)S(1)}, u32[]{:S(2)}, u32[]{:S(2)}) collective-permute-start(bf16[384,256]{1,0:T(8,128)(2,1)S(1)} %collective-permute-done.15.refs_12_), channel_id=1, source_target_pairs={{0,8},{8,0},{1,9},{9,1},{2,10},{10,2},{3,11},{11,3},{4,12},{12,4},... | collective-permute-start | bytes 589832 | tf_op jit(solution)/shard_map/ppermute | solution.py:377
  94.5 4.9 %collective-permute-start.18 = (bf16[384,256]{1,0:T(8,128)(2,1)S(1)}, bf16[384,256]{1,0:T(8,128)(2,1)S(1)}, u32[]{:S(2)}, u32[]{:S(2)}) collective-permute-start(bf16[384,256]{1,0:T(8,128)(2,1)S(1)} %collective-permute-done.17.refs_13_), channel_id=1, source_target_pairs={{0,8},{8,0},{1,9},{9,1},{2,10},{10,2},{3,11},{11,3},{4,12},{12,4},... | collective-permute-start | bytes 589832 | tf_op jit(solution)/shard_map/ppermute | solution.py:377
  95.2 8.5 %collective-permute-start.20 = (bf16[384,256]{1,0:T(8,128)(2,1)}, bf16[384,256]{1,0:T(8,128)(2,1)S(1)}, u32[]{:S(2)}, u32[]{:S(2)}) collective-permute-start(bf16[384,256]{1,0:T(8,128)(2,1)} %collective-permute-done.19.refs_14_), channel_id=1, source_target_pairs={{0,8},{8,0},{1,9},{9,1},{2,10},{10,2},{3,11},{11,3},{4,12},{12,4},... | collective-permute-start | bytes 589832 | tf_op jit(solution)/shard_map/ppermute | solution.py:377
  98.0 6.4 %collective-permute-start.7 = (bf16[2,256,256]{2,1,0:T(8,128)(2,1)}, bf16[2,256,256]{2,1,0:T(8,128)(2,1)S(1)}, u32[]{:S(2)}, u32[]{:S(2)}) collective-permute-start(bf16[2,256,256]{2,1,0:T(8,128)(2,1)} %get-tuple-element.17), channel_id=1, source_target_pairs={{8,12},{9,13},{10,14},{11,15},{12,8},{13,9},{14,10},{15,11},{24,28... | collective-permute-start | bytes 786440 | tf_op jit(solution)/shard_map/ppermute | solution.py:387
  99.3 19.3 %collective-permute-start.8 = (bf16[2,256,256]{2,1,0:T(8,128)(2,1)}, bf16[2,256,256]{2,1,0:T(8,128)(2,1)S(1)}, u32[]{:S(2)}, u32[]{:S(2)}) collective-permute-start(bf16[2,256,256]{2,1,0:T(8,128)(2,1)} %get-tuple-element.17), channel_id=1, source_target_pairs={{0,1},{8,13},{1,2},{9,14},{2,3},{10,15},{3,0},{11,12},{4,5},{12,9}... | collective-permute-start | bytes 786440 | tf_op jit(solution)/shard_map/ppermute | solution.py:387
  100.0 19.5 %collective-permute-start.9 = (bf16[2,256,256]{2,1,0:T(8,128)(2,1)}, bf16[2,256,256]{2,1,0:T(8,128)(2,1)S(1)}, u32[]{:S(2)}, u32[]{:S(2)}) collective-permute-start(bf16[2,256,256]{2,1,0:T(8,128)(2,1)} %get-tuple-element.17), channel_id=1, source_target_pairs={{0,2},{8,14},{1,3},{9,15},{2,0},{10,12},{3,1},{11,13},{4,6},{12,10... | collective-permute-start | bytes 786440 | tf_op jit(solution)/shard_map/ppermute | solution.py:387
  104.4 18.0 %collective-permute-start.10 = (bf16[2,256,256]{2,1,0:T(8,128)(2,1)}, bf16[2,256,256]{2,1,0:T(8,128)(2,1)S(1)}, u32[]{:S(2)}, u32[]{:S(2)}) collective-permute-start(bf16[2,256,256]{2,1,0:T(8,128)(2,1)} %get-tuple-element.17), channel_id=1, source_target_pairs={{0,3},{8,15},{1,0},{9,12},{2,1},{10,13},{3,2},{11,14},{4,7},{12,11... | collective-permute-start | bytes 786440 | tf_op jit(solution)/shard_map/ppermute | solution.py:387
  104.4 33.8 %collective-permute-start.11 = (bf16[2,256,256]{2,1,0:T(8,128)(2,1)S(1)}, bf16[2,256,256]{2,1,0:T(8,128)(2,1)}, u32[]{:S(2)}, u32[]{:S(2)}) collective-permute-start(bf16[2,256,256]{2,1,0:T(8,128)(2,1)S(1)} %collective-permute-done.7.refs_0_), channel_id=1, source_target_pairs={{0,8},{8,0},{1,9},{9,1},{2,10},{10,2},{3,11},{11,3},{4,12},{12,4},... | collective-permute-start | bytes 786440 | tf_op jit(solution)/shard_map/ppermute | solution.py:377
  118.6 19.6 %collective-permute-start.12 = (bf16[2,256,256]{2,1,0:T(8,128)(2,1)S(1)}, bf16[2,256,256]{2,1,0:T(8,128)(2,1)}, u32[]{:S(2)}, u32[]{:S(2)}) collective-permute-start(bf16[2,256,256]{2,1,0:T(8,128)(2,1)S(1)} %collective-permute-done.8.refs_1_), channel_id=1, source_target_pairs={{0,8},{8,0},{1,9},{9,1},{2,10},{10,2},{3,11},{11,3},{4,12},{12,4},... | collective-permute-start | bytes 786440 | tf_op jit(solution)/shard_map/ppermute | solution.py:377
  119.5 18.7 %collective-permute-start.13 = (bf16[2,256,256]{2,1,0:T(8,128)(2,1)S(1)}, bf16[2,256,256]{2,1,0:T(8,128)(2,1)}, u32[]{:S(2)}, u32[]{:S(2)}) collective-permute-start(bf16[2,256,256]{2,1,0:T(8,128)(2,1)S(1)} %collective-permute-done.9.refs_2_), channel_id=1, source_target_pairs={{0,8},{8,0},{1,9},{9,1},{2,10},{10,2},{3,11},{11,3},{4,12},{12,4},... | collective-permute-start | bytes 786440 | tf_op jit(solution)/shard_map/ppermute | solution.py:377
  122.4 15.9 %collective-permute-start.14 = (bf16[2,256,256]{2,1,0:T(8,128)(2,1)S(1)}, bf16[2,256,256]{2,1,0:T(8,128)(2,1)}, u32[]{:S(2)}, u32[]{:S(2)}) collective-permute-start(bf16[2,256,256]{2,1,0:T(8,128)(2,1)S(1)} %collective-permute-done.10.refs_3_), channel_id=1, source_target_pairs={{0,8},{8,0},{1,9},{9,1},{2,10},{10,2},{3,11},{11,3},{4,12},{12,4},... | collective-permute-start | bytes 786440 | tf_op jit(solution)/shard_map/ppermute | solution.py:377
  124.8 13.4 %collective-permute-start.22 = (bf16[384,256]{1,0:T(8,128)(2,1)}, bf16[384,256]{1,0:T(8,128)(2,1)}, u32[]{:S(2)}, u32[]{:S(2)}) collective-permute-start(bf16[384,256]{1,0:T(8,128)(2,1)} %collective-permute-done.21.refs_15_), channel_id=1, source_target_pairs={{0,8},{8,0},{1,9},{9,1},{2,10},{10,2},{3,11},{11,3},{4,12},{12,4},... | collective-permute-start | bytes 589832 | tf_op jit(solution)/shard_map/ppermute | solution.py:377
  126.4 18.3 %all-to-all-start.3 = ((f32[128,1,128]{2,1,0:T(1,128)}), f32[128,1,128]{2,1,0:T(1,128)S(1)}, u32[]{:S(2)}, u32[]{:S(2)}) async-start(f32[128,1,128]{2,1,0:T(1,128)} %bitcast.12), calls=%async_computation.3 | async-start | bytes 131072 | tf_op jit(solution)/shard_map/all_to_all | solution.py:391
  (14 other events, 40.5 us)
